TPU v7x, 32 devices: a whole 2x2x4 slice. The times are simulated.
32 devices in a mesh: freq: 2 (over x), sec: 16 (over z, y, core).
Axes of the slice: x: 2, y: 2, z: 4, core: 2. Of those that a mesh axis runs over, the one named last changes fastest.
Arguments:
- layer_trans: bfloat16 [16, 1024, 1024], P('sec'), may hold values from -0.1875 to 0.1875
- layer_refl: bfloat16 [16, 1024, 1024], P('sec'), may hold values from -0.046875 to 0.046875
- source_modes: int32 [256], P('freq'), parts along dimension 0, may hold values from 0 to 1023
Outputs:
- upgoing: bfloat16 [32, 64, 1024], P(('freq', 'sec')), parts along dimension 0
There are 2 independent parts, one for each index of `freq`. A program takes and returns all parts, laid end to end along the dimension named above; an argument that names none is the same for every part. Nothing has to cross between parts.
All inputs are finite; a program needn't handle non-finite values.
Results may differ from a plain program's by a relative error of at most 0.035.
Values may be sent and summed in bfloat16 or wider, within the bound.
No kernel may reach another device: no remote copies, remote signals or barrier semaphores. Data moves between devices by JAX's collectives and lax.ppermute only.
A program may use at most 64 MiB of HBM per device.

v0:
```python
import jax
import jax.numpy as jnp
from jax import lax
from jax.sharding import PartitionSpec as P

NB = 4


def from_partner(array, axis, stride):
    return lax.ppermute(array, axis, [(i, i ^ 1 << stride) for i in range(lax.axis_size(axis))])


def from_behind(value, axis, steps):
    count = lax.axis_size(axis)
    first, last = (max(0, -steps), min(count, count - steps))
    return lax.ppermute(value, axis, [(source, source + steps) for source in range(first, last)])


def matmul_nt(left, right):
    return lax.dot_general(
        left, right, (((1,), (1,)), ((), ())), preferred_element_type=jnp.float32
    )


def shards(layer_trans, layer_refl, source_modes):
    position = lax.axis_index("sec")
    section = position // 2
    parity = position % 2
    is_upper = parity == 0
    sections = lax.axis_size("sec") // 2
    trans = layer_trans[0]
    refl = layer_refl[0]
    modes_all = trans.shape[0]
    other_t, other_r = from_partner((trans, refl), "sec", 0)
    upper_t = jnp.where(is_upper, trans, other_t)
    lower_t = jnp.where(is_upper, other_t, trans)
    upper_r = jnp.where(is_upper, refl, other_r)
    lower_r = jnp.where(is_upper, other_r, refl)
    merged_t = jnp.dot(upper_t, lower_t, preferred_element_type=jnp.float32).astype(jnp.bfloat16)
    inner = matmul_nt(lower_r, upper_t).astype(jnp.bfloat16)
    merged_r = (
        upper_r.astype(jnp.float32) + jnp.dot(upper_t, inner, preferred_element_type=jnp.float32)
    ).astype(jnp.bfloat16)
    half_rows = source_modes.shape[0] // 2
    batch_rows = half_rows // NB
    my_modes = lax.dynamic_slice_in_dim(source_modes, parity * half_rows, half_rows, 0)
    columns = jnp.arange(modes_all, dtype=jnp.int32)
    steps = sections + NB - 1

    def down_step(step, carry):
        incoming, echoes = carry
        batch = step - section
        valid = (batch >= 0) & (batch < NB)
        batch_c = jnp.clip(batch, 0, NB - 1)
        batch_modes = lax.dynamic_slice_in_dim(my_modes, batch_c * batch_rows, batch_rows, 0)
        unit_rows = (batch_modes[:, None] == columns[None, :]).astype(jnp.bfloat16)
        current = jnp.where(section == 0, unit_rows, incoming)
        echo = jnp.dot(current, merged_r, preferred_element_type=jnp.float32)
        after = jnp.dot(current, merged_t, preferred_element_type=jnp.float32).astype(jnp.bfloat16)
        previous = lax.dynamic_slice_in_dim(echoes, batch_c * batch_rows, batch_rows, 0)
        echoes = lax.dynamic_update_slice_in_dim(
            echoes, jnp.where(valid, echo, previous), batch_c * batch_rows, 0
        )
        incoming = from_behind(after, "sec", 2)
        return (incoming, echoes)

    start_in = jnp.zeros((batch_rows, modes_all), jnp.bfloat16)
    start_echo = jnp.zeros((half_rows, modes_all), jnp.float32)
    unused_in, echoes = lax.fori_loop(0, steps, down_step, (start_in, start_echo))

    def up_step(step, carry):
        incoming, upgoing = carry
        batch = step - (sections - 1 - section)
        valid = (batch >= 0) & (batch < NB)
        batch_c = jnp.clip(batch, 0, NB - 1)
        echo = lax.dynamic_slice_in_dim(echoes, batch_c * batch_rows, batch_rows, 0)
        value = (echo + matmul_nt(incoming, merged_t)).astype(jnp.bfloat16)
        previous = lax.dynamic_slice_in_dim(upgoing, batch_c * batch_rows, batch_rows, 0)
        upgoing = lax.dynamic_update_slice_in_dim(
            upgoing, jnp.where(valid, value, previous), batch_c * batch_rows, 0
        )
        incoming = from_behind(value, "sec", -2)
        return (incoming, upgoing)

    start_up = jnp.zeros((half_rows, modes_all), jnp.bfloat16)
    unused_up, upgoing = lax.fori_loop(0, steps, up_step, (start_in, start_up))
    return upgoing[None]


def solution(mesh):
    return jax.shard_map(
        shards,
        mesh=mesh,
        in_specs=(P("sec", None, None), P("sec", None, None), P("freq")),
        out_specs=P(("freq", "sec"), None, None),
        check_vma=False,
    )
```

profile of v0, /device:TPU:0, one launch (start us, length us, event | category | flops | bytes accessed | tf_op | source)
XLA Modules:
  0.0 180.7 jit_solution(18380081105397127486)
XLA Ops:
  4.6 5.2 %fusion.16 = bf16[1024,1024]{1,0:T(8,128)(2,1)S(1)} fusion(bf16[1024,1024]{1,0:T(8,128)(2,1)} %collective-permute-done.2, pred[]{:T(512)S(6)} %eq.51, bf16[1,1024,1024]{2,1,0:T(8,128)(2,1)} %param.7), kind=kOutput, calls=%fused_computation.20 | convolution fusion | flops 2150629376 | bytes 6291457 | tf_op jit(solution)/shard_map/dot_general | solution.py:39
  9.8 10.7 %add_convert_fusion = bf16[1024,1024]{1,0:T(8,128)(2,1)} fusion(bf16[1024,1024]{1,0:T(8,128)(2,1)} %collective-permute-done.3, pred[]{:T(512)S(6)} %eq.51, bf16[1024,1024]{1,0:T(8,128)(2,1)} %collective-permute-done.2, bf16[1,1024,1024]{2,1,0:T(8,128)(2,1)} %param.8, bf16[1,1024,1024]{2,1,0:T(8,128)(2,1)} %param.7), kind=kOutput, calls=%fused_computation.10 | convolution fusion | flops 4303355904 | bytes 10485761 | tf_op jit(solution)/shard_map/dot_general | solution.py:42
  20.6 78.4 %while.35 = (s32[]{:T(128)}, bf16[16,1024]{1,0:T(8,128)(2,1)S(1)}, f32[64,1024]{1,0:T(8,128)S(1)}, pred[]{:T(512)}, s32[]{:T(128)}, /*index=5*/s32[64]{0:T(128)S...) while((s32[]{:T(128)}, bf16[16,1024]{1,0:T(8,128)(2,1)S(1)}, ...), condition=%wide.region_1.2_spmd.clone, body=%wide.region_0.1_spmd.clone.sunk | while | flops 67239944 | bytes 4621279 | solution.py:69
  21.1 4.8 %collective-permute-start.1 = (bf16[16,1024]{1,0:T(8,128)(2,1)S(1)}, bf16[16,1024]{1,0:T(8,128)(2,1)S(1)}, u32[]{:S(2)}, u32[]{:S(2)}) collective-permute-start(bf16[16,1024]{1,0:T(8,128)(2,1)S(1)} %convolution_convert_fusion.2), channel_id=1, source_target_pairs={{0,2},{1,3},{2,4},{3,5},{4,6},{5,7},{6,8},{7,9},{8,10},{9,11},{10,... | collective-permute-start | bytes 98312 | tf_op jit(solution)/shard_map/while/body/eval_jaxpr/ppermute | solution.py:16
  41.8 4.6 %collective-permute-start.1 = (bf16[16,1024]{1,0:T(8,128)(2,1)S(1)}, bf16[16,1024]{1,0:T(8,128)(2,1)S(1)}, u32[]{:S(2)}, u32[]{:S(2)}) collective-permute-start(bf16[16,1024]{1,0:T(8,128)(2,1)S(1)} %convolution_convert_fusion.2), channel_id=1, source_target_pairs={{0,2},{1,3},{2,4},{3,5},{4,6},{5,7},{6,8},{7,9},{8,10},{9,11},{10,... | collective-permute-start | bytes 98312 | tf_op jit(solution)/shard_map/while/body/eval_jaxpr/ppermute | solution.py:16
  49.0 4.6 %collective-permute-start.1 = (bf16[16,1024]{1,0:T(8,128)(2,1)S(1)}, bf16[16,1024]{1,0:T(8,128)(2,1)S(1)}, u32[]{:S(2)}, u32[]{:S(2)}) collective-permute-start(bf16[16,1024]{1,0:T(8,128)(2,1)S(1)} %convolution_convert_fusion.2), channel_id=1, source_target_pairs={{0,2},{1,3},{2,4},{3,5},{4,6},{5,7},{6,8},{7,9},{8,10},{9,11},{10,... | collective-permute-start | bytes 98312 | tf_op jit(solution)/shard_map/while/body/eval_jaxpr/ppermute | solution.py:16
  56.2 4.6 %collective-permute-start.1 = (bf16[16,1024]{1,0:T(8,128)(2,1)S(1)}, bf16[16,1024]{1,0:T(8,128)(2,1)S(1)}, u32[]{:S(2)}, u32[]{:S(2)}) collective-permute-start(bf16[16,1024]{1,0:T(8,128)(2,1)S(1)} %convolution_convert_fusion.2), channel_id=1, source_target_pairs={{0,2},{1,3},{2,4},{3,5},{4,6},{5,7},{6,8},{7,9},{8,10},{9,11},{10,... | collective-permute-start | bytes 98312 | tf_op jit(solution)/shard_map/while/body/eval_jaxpr/ppermute | solution.py:16
  63.4 4.6 %collective-permute-start.1 = (bf16[16,1024]{1,0:T(8,128)(2,1)S(1)}, bf16[16,1024]{1,0:T(8,128)(2,1)S(1)}, u32[]{:S(2)}, u32[]{:S(2)}) collective-permute-start(bf16[16,1024]{1,0:T(8,128)(2,1)S(1)} %convolution_convert_fusion.2), channel_id=1, source_target_pairs={{0,2},{1,3},{2,4},{3,5},{4,6},{5,7},{6,8},{7,9},{8,10},{9,11},{10,... | collective-permute-start | bytes 98312 | tf_op jit(solution)/shard_map/while/body/eval_jaxpr/ppermute | solution.py:16
  70.6 4.6 %collective-permute-start.1 = (bf16[16,1024]{1,0:T(8,128)(2,1)S(1)}, bf16[16,1024]{1,0:T(8,128)(2,1)S(1)}, u32[]{:S(2)}, u32[]{:S(2)}) collective-permute-start(bf16[16,1024]{1,0:T(8,128)(2,1)S(1)} %convolution_convert_fusion.2), channel_id=1, source_target_pairs={{0,2},{1,3},{2,4},{3,5},{4,6},{5,7},{6,8},{7,9},{8,10},{9,11},{10,... | collective-permute-start | bytes 98312 | tf_op jit(solution)/shard_map/while/body/eval_jaxpr/ppermute | solution.py:16
  77.8 4.6 %collective-permute-start.1 = (bf16[16,1024]{1,0:T(8,128)(2,1)S(1)}, bf16[16,1024]{1,0:T(8,128)(2,1)S(1)}, u32[]{:S(2)}, u32[]{:S(2)}) collective-permute-start(bf16[16,1024]{1,0:T(8,128)(2,1)S(1)} %convolution_convert_fusion.2), channel_id=1, source_target_pairs={{0,2},{1,3},{2,4},{3,5},{4,6},{5,7},{6,8},{7,9},{8,10},{9,11},{10,... | collective-permute-start | bytes 98312 | tf_op jit(solution)/shard_map/while/body/eval_jaxpr/ppermute | solution.py:16
  85.0 4.6 %collective-permute-start.1 = (bf16[16,1024]{1,0:T(8,128)(2,1)S(1)}, bf16[16,1024]{1,0:T(8,128)(2,1)S(1)}, u32[]{:S(2)}, u32[]{:S(2)}) collective-permute-start(bf16[16,1024]{1,0:T(8,128)(2,1)S(1)} %convolution_convert_fusion.2), channel_id=1, source_target_pairs={{0,2},{1,3},{2,4},{3,5},{4,6},{5,7},{6,8},{7,9},{8,10},{9,11},{10,... | collective-permute-start | bytes 98312 | tf_op jit(solution)/shard_map/while/body/eval_jaxpr/ppermute | solution.py:16
  92.2 4.6 %collective-permute-start.1 = (bf16[16,1024]{1,0:T(8,128)(2,1)S(1)}, bf16[16,1024]{1,0:T(8,128)(2,1)S(1)}, u32[]{:S(2)}, u32[]{:S(2)}) collective-permute-start(bf16[16,1024]{1,0:T(8,128)(2,1)S(1)} %convolution_convert_fusion.2), channel_id=1, source_target_pairs={{0,2},{1,3},{2,4},{3,5},{4,6},{5,7},{6,8},{7,9},{8,10},{9,11},{10,... | collective-permute-start | bytes 98312 | tf_op jit(solution)/shard_map/while/body/eval_jaxpr/ppermute | solution.py:16
  99.0 81.1 %while.34 = (s32[]{:T(128)}, bf16[16,1024]{1,0:T(8,128)(2,1)S(1)}, bf16[64,1024]{1,0:T(8,128)(2,1)S(1)}, s32[]{:T(128)}, f32[64,1024]{1,0:T(8,128)S(1)}, /*index...) while((s32[]{:T(128)}, bf16[16,1024]{1,0:T(8,128)(2,1)S(1)}, ...), condition=%wide.region_3.4_spmd, body=%wide.region_2.3_spmd.sunk | while | flops 33603596 | bytes 2425097 | solution.py:86
  101.0 5.2 %collective-permute-done = bf16[16,1024]{1,0:T(8,128)(2,1)S(1)} collective-permute-done((bf16[16,1024]{1,0:T(8,128)(2,1)S(1)}, bf16[16,1024]{1,0:T(8,128)(2,1)S(1)}, u32[]{:S(2)}, u32[]{:S(2)}) %collective-permute-start) | collective-permute-done | bytes 32800 | tf_op jit(solution)/shard_map/while/body/eval_jaxpr/ppermute | solution.py:16
  108.1 5.6 %collective-permute-done = bf16[16,1024]{1,0:T(8,128)(2,1)S(1)} collective-permute-done((bf16[16,1024]{1,0:T(8,128)(2,1)S(1)}, bf16[16,1024]{1,0:T(8,128)(2,1)S(1)}, u32[]{:S(2)}, u32[]{:S(2)}) %collective-permute-start) | collective-permute-done | bytes 32800 | tf_op jit(solution)/shard_map/while/body/eval_jaxpr/ppermute | solution.py:16
  115.7 5.2 %collective-permute-done = bf16[16,1024]{1,0:T(8,128)(2,1)S(1)} collective-permute-done((bf16[16,1024]{1,0:T(8,128)(2,1)S(1)}, bf16[16,1024]{1,0:T(8,128)(2,1)S(1)}, u32[]{:S(2)}, u32[]{:S(2)}) %collective-permute-start) | collective-permute-done | bytes 32800 | tf_op jit(solution)/shard_map/while/body/eval_jaxpr/ppermute | solution.py:16
  122.8 5.4 %collective-permute-done = bf16[16,1024]{1,0:T(8,128)(2,1)S(1)} collective-permute-done((bf16[16,1024]{1,0:T(8,128)(2,1)S(1)}, bf16[16,1024]{1,0:T(8,128)(2,1)S(1)}, u32[]{:S(2)}, u32[]{:S(2)}) %collective-permute-start) | collective-permute-done | bytes 32800 | tf_op jit(solution)/shard_map/while/body/eval_jaxpr/ppermute | solution.py:16
  130.2 5.4 %collective-permute-done = bf16[16,1024]{1,0:T(8,128)(2,1)S(1)} collective-permute-done((bf16[16,1024]{1,0:T(8,128)(2,1)S(1)}, bf16[16,1024]{1,0:T(8,128)(2,1)S(1)}, u32[]{:S(2)}, u32[]{:S(2)}) %collective-permute-start) | collective-permute-done | bytes 32800 | tf_op jit(solution)/shard_map/while/body/eval_jaxpr/ppermute | solution.py:16
  137.6 5.4 %collective-permute-done = bf16[16,1024]{1,0:T(8,128)(2,1)S(1)} collective-permute-done((bf16[16,1024]{1,0:T(8,128)(2,1)S(1)}, bf16[16,1024]{1,0:T(8,128)(2,1)S(1)}, u32[]{:S(2)}, u32[]{:S(2)}) %collective-permute-start) | collective-permute-done | bytes 32800 | tf_op jit(solution)/shard_map/while/body/eval_jaxpr/ppermute | solution.py:16
  144.9 5.4 %collective-permute-done = bf16[16,1024]{1,0:T(8,128)(2,1)S(1)} collective-permute-done((bf16[16,1024]{1,0:T(8,128)(2,1)S(1)}, bf16[16,1024]{1,0:T(8,128)(2,1)S(1)}, u32[]{:S(2)}, u32[]{:S(2)}) %collective-permute-start) | collective-permute-done | bytes 32800 | tf_op jit(solution)/shard_map/while/body/eval_jaxpr/ppermute | solution.py:16
  152.3 5.7 %collective-permute-done = bf16[16,1024]{1,0:T(8,128)(2,1)S(1)} collective-permute-done((bf16[16,1024]{1,0:T(8,128)(2,1)S(1)}, bf16[16,1024]{1,0:T(8,128)(2,1)S(1)}, u32[]{:S(2)}, u32[]{:S(2)}) %collective-permute-start) | collective-permute-done | bytes 32800 | tf_op jit(solution)/shard_map/while/body/eval_jaxpr/ppermute | solution.py:16
  160.0 5.4 %collective-permute-done = bf16[16,1024]{1,0:T(8,128)(2,1)S(1)} collective-permute-done((bf16[16,1024]{1,0:T(8,128)(2,1)S(1)}, bf16[16,1024]{1,0:T(8,128)(2,1)S(1)}, u32[]{:S(2)}, u32[]{:S(2)}) %collective-permute-start) | collective-permute-done | bytes 32800 | tf_op jit(solution)/shard_map/while/body/eval_jaxpr/ppermute | solution.py:16
  167.3 5.4 %collective-permute-done = bf16[16,1024]{1,0:T(8,128)(2,1)S(1)} collective-permute-done((bf16[16,1024]{1,0:T(8,128)(2,1)S(1)}, bf16[16,1024]{1,0:T(8,128)(2,1)S(1)}, u32[]{:S(2)}, u32[]{:S(2)}) %collective-permute-start) | collective-permute-done | bytes 32800 | tf_op jit(solution)/shard_map/while/body/eval_jaxpr/ppermute | solution.py:16
  174.7 5.4 %collective-permute-done = bf16[16,1024]{1,0:T(8,128)(2,1)S(1)} collective-permute-done((bf16[16,1024]{1,0:T(8,128)(2,1)S(1)}, bf16[16,1024]{1,0:T(8,128)(2,1)S(1)}, u32[]{:S(2)}, u32[]{:S(2)}) %collective-permute-start) | collective-permute-done | bytes 32800 | tf_op jit(solution)/shard_map/while/body/eval_jaxpr/ppermute | solution.py:16
  (90 shorter events, 62.6 us)
Async XLA Ops:
  0.0 4.6 %collective-permute-start.2 = (bf16[1024,1024]{1,0:T(8,128)(2,1)}, bf16[1024,1024]{1,0:T(8,128)(2,1)}, u32[]{:S(2)}, u32[]{:S(2)}) collective-permute-start(bf16[1024,1024]{1,0:T(8,128)(2,1)} %bitcast.33), channel_id=1, source_target_pairs={{0,1},{1,0},{2,3},{3,2},{4,5},{5,4},{6,7},{7,6},{8,9},{9,8},{10,11... | collective-permute-start | bytes 6291464 | tf_op jit(solution)/shard_map/ppermute | solution.py:10
  0.5 9.3 %collective-permute-start.3 = (bf16[1024,1024]{1,0:T(8,128)(2,1)}, bf16[1024,1024]{1,0:T(8,128)(2,1)}, u32[]{:S(2)}, u32[]{:S(2)}) collective-permute-start(bf16[1024,1024]{1,0:T(8,128)(2,1)} %bitcast.34), channel_id=1, source_target_pairs={{0,1},{1,0},{2,3},{3,2},{4,5},{5,4},{6,7},{7,6},{8,9},{9,8},{10,11... | collective-permute-start | bytes 6291464 | tf_op jit(solution)/shard_map/ppermute | solution.py:10
  21.1 6.8 %collective-permute-start.1 = (bf16[16,1024]{1,0:T(8,128)(2,1)S(1)}, bf16[16,1024]{1,0:T(8,128)(2,1)S(1)}, u32[]{:S(2)}, u32[]{:S(2)}) collective-permute-start(bf16[16,1024]{1,0:T(8,128)(2,1)S(1)} %convolution_convert_fusion.2), channel_id=1, source_target_pairs={{0,2},{1,3},{2,4},{3,5},{4,6},{5,7},{6,8},{7,9},{8,10},{9,11},{10,... | collective-permute-start | bytes 98312 | tf_op jit(solution)/shard_map/while/body/eval_jaxpr/ppermute | solution.py:16
  28.4 5.9 %collective-permute-start.1 = (bf16[16,1024]{1,0:T(8,128)(2,1)S(1)}, bf16[16,1024]{1,0:T(8,128)(2,1)S(1)}, u32[]{:S(2)}, u32[]{:S(2)}) collective-permute-start(bf16[16,1024]{1,0:T(8,128)(2,1)S(1)} %convolution_convert_fusion.2), channel_id=1, source_target_pairs={{0,2},{1,3},{2,4},{3,5},{4,6},{5,7},{6,8},{7,9},{8,10},{9,11},{10,... | collective-permute-start | bytes 98312 | tf_op jit(solution)/shard_map/while/body/eval_jaxpr/ppermute | solution.py:16
  34.9 6.4 %collective-permute-start.1 = (bf16[16,1024]{1,0:T(8,128)(2,1)S(1)}, bf16[16,1024]{1,0:T(8,128)(2,1)S(1)}, u32[]{:S(2)}, u32[]{:S(2)}) collective-permute-start(bf16[16,1024]{1,0:T(8,128)(2,1)S(1)} %convolution_convert_fusion.2), channel_id=1, source_target_pairs={{0,2},{1,3},{2,4},{3,5},{4,6},{5,7},{6,8},{7,9},{8,10},{9,11},{10,... | collective-permute-start | bytes 98312 | tf_op jit(solution)/shard_map/while/body/eval_jaxpr/ppermute | solution.py:16
  41.8 6.7 %collective-permute-start.1 = (bf16[16,1024]{1,0:T(8,128)(2,1)S(1)}, bf16[16,1024]{1,0:T(8,128)(2,1)S(1)}, u32[]{:S(2)}, u32[]{:S(2)}) collective-permute-start(bf16[16,1024]{1,0:T(8,128)(2,1)S(1)} %convolution_convert_fusion.2), channel_id=1, source_target_pairs={{0,2},{1,3},{2,4},{3,5},{4,6},{5,7},{6,8},{7,9},{8,10},{9,11},{10,... | collective-permute-start | bytes 98312 | tf_op jit(solution)/shard_map/while/body/eval_jaxpr/ppermute | solution.py:16
  49.0 6.7 %collective-permute-start.1 = (bf16[16,1024]{1,0:T(8,128)(2,1)S(1)}, bf16[16,1024]{1,0:T(8,128)(2,1)S(1)}, u32[]{:S(2)}, u32[]{:S(2)}) collective-permute-start(bf16[16,1024]{1,0:T(8,128)(2,1)S(1)} %convolution_convert_fusion.2), channel_id=1, source_target_pairs={{0,2},{1,3},{2,4},{3,5},{4,6},{5,7},{6,8},{7,9},{8,10},{9,11},{10,... | collective-permute-start | bytes 98312 | tf_op jit(solution)/shard_map/while/body/eval_jaxpr/ppermute | solution.py:16
  56.2 6.7 %collective-permute-start.1 = (bf16[16,1024]{1,0:T(8,128)(2,1)S(1)}, bf16[16,1024]{1,0:T(8,128)(2,1)S(1)}, u32[]{:S(2)}, u32[]{:S(2)}) collective-permute-start(bf16[16,1024]{1,0:T(8,128)(2,1)S(1)} %convolution_convert_fusion.2), channel_id=1, source_target_pairs={{0,2},{1,3},{2,4},{3,5},{4,6},{5,7},{6,8},{7,9},{8,10},{9,11},{10,... | collective-permute-start | bytes 98312 | tf_op jit(solution)/shard_map/while/body/eval_jaxpr/ppermute | solution.py:16
  63.4 6.7 %collective-permute-start.1 = (bf16[16,1024]{1,0:T(8,128)(2,1)S(1)}, bf16[16,1024]{1,0:T(8,128)(2,1)S(1)}, u32[]{:S(2)}, u32[]{:S(2)}) collective-permute-start(bf16[16,1024]{1,0:T(8,128)(2,1)S(1)} %convolution_convert_fusion.2), channel_id=1, source_target_pairs={{0,2},{1,3},{2,4},{3,5},{4,6},{5,7},{6,8},{7,9},{8,10},{9,11},{10,... | collective-permute-start | bytes 98312 | tf_op jit(solution)/shard_map/while/body/eval_jaxpr/ppermute | solution.py:16
  70.6 6.7 %collective-permute-start.1 = (bf16[16,1024]{1,0:T(8,128)(2,1)S(1)}, bf16[16,1024]{1,0:T(8,128)(2,1)S(1)}, u32[]{:S(2)}, u32[]{:S(2)}) collective-permute-start(bf16[16,1024]{1,0:T(8,128)(2,1)S(1)} %convolution_convert_fusion.2), channel_id=1, source_target_pairs={{0,2},{1,3},{2,4},{3,5},{4,6},{5,7},{6,8},{7,9},{8,10},{9,11},{10,... | collective-permute-start | bytes 98312 | tf_op jit(solution)/shard_map/while/body/eval_jaxpr/ppermute | solution.py:16
  77.8 6.7 %collective-permute-start.1 = (bf16[16,1024]{1,0:T(8,128)(2,1)S(1)}, bf16[16,1024]{1,0:T(8,128)(2,1)S(1)}, u32[]{:S(2)}, u32[]{:S(2)}) collective-permute-start(bf16[16,1024]{1,0:T(8,128)(2,1)S(1)} %convolution_convert_fusion.2), channel_id=1, source_target_pairs={{0,2},{1,3},{2,4},{3,5},{4,6},{5,7},{6,8},{7,9},{8,10},{9,11},{10,... | collective-permute-start | bytes 98312 | tf_op jit(solution)/shard_map/while/body/eval_jaxpr/ppermute | solution.py:16
  85.0 6.7 %collective-permute-start.1 = (bf16[16,1024]{1,0:T(8,128)(2,1)S(1)}, bf16[16,1024]{1,0:T(8,128)(2,1)S(1)}, u32[]{:S(2)}, u32[]{:S(2)}) collective-permute-start(bf16[16,1024]{1,0:T(8,128)(2,1)S(1)} %convolution_convert_fusion.2), channel_id=1, source_target_pairs={{0,2},{1,3},{2,4},{3,5},{4,6},{5,7},{6,8},{7,9},{8,10},{9,11},{10,... | collective-permute-start | bytes 98312 | tf_op jit(solution)/shard_map/while/body/eval_jaxpr/ppermute | solution.py:16
  92.2 6.7 %collective-permute-start.1 = (bf16[16,1024]{1,0:T(8,128)(2,1)S(1)}, bf16[16,1024]{1,0:T(8,128)(2,1)S(1)}, u32[]{:S(2)}, u32[]{:S(2)}) collective-permute-start(bf16[16,1024]{1,0:T(8,128)(2,1)S(1)} %convolution_convert_fusion.2), channel_id=1, source_target_pairs={{0,2},{1,3},{2,4},{3,5},{4,6},{5,7},{6,8},{7,9},{8,10},{9,11},{10,... | collective-permute-start | bytes 98312 | tf_op jit(solution)/shard_map/while/body/eval_jaxpr/ppermute | solution.py:16
  99.6 6.5 %collective-permute-start = (bf16[16,1024]{1,0:T(8,128)(2,1)S(1)}, bf16[16,1024]{1,0:T(8,128)(2,1)S(1)}, u32[]{:S(2)}, u32[]{:S(2)}) collective-permute-start(bf16[16,1024]{1,0:T(8,128)(2,1)S(1)} %get-tuple-element.460), channel_id=1, source_target_pairs={{2,0},{3,1},{4,2},{5,3},{6,4},{7,5},{8,6},{9,7},{10,8},{11,9},{12,... | collective-permute-start | bytes 98312 | tf_op jit(solution)/shard_map/while/body/eval_jaxpr/ppermute | solution.py:16
  106.8 6.9 %collective-permute-start = (bf16[16,1024]{1,0:T(8,128)(2,1)S(1)}, bf16[16,1024]{1,0:T(8,128)(2,1)S(1)}, u32[]{:S(2)}, u32[]{:S(2)}) collective-permute-start(bf16[16,1024]{1,0:T(8,128)(2,1)S(1)} %get-tuple-element.460), channel_id=1, source_target_pairs={{2,0},{3,1},{4,2},{5,3},{6,4},{7,5},{8,6},{9,7},{10,8},{11,9},{12,... | collective-permute-start | bytes 98312 | tf_op jit(solution)/shard_map/while/body/eval_jaxpr/ppermute | solution.py:16
  114.4 6.5 %collective-permute-start = (bf16[16,1024]{1,0:T(8,128)(2,1)S(1)}, bf16[16,1024]{1,0:T(8,128)(2,1)S(1)}, u32[]{:S(2)}, u32[]{:S(2)}) collective-permute-start(bf16[16,1024]{1,0:T(8,128)(2,1)S(1)} %get-tuple-element.460), channel_id=1, source_target_pairs={{2,0},{3,1},{4,2},{5,3},{6,4},{7,5},{8,6},{9,7},{10,8},{11,9},{12,... | collective-permute-start | bytes 98312 | tf_op jit(solution)/shard_map/while/body/eval_jaxpr/ppermute | solution.py:16
  121.5 6.7 %collective-permute-start = (bf16[16,1024]{1,0:T(8,128)(2,1)S(1)}, bf16[16,1024]{1,0:T(8,128)(2,1)S(1)}, u32[]{:S(2)}, u32[]{:S(2)}) collective-permute-start(bf16[16,1024]{1,0:T(8,128)(2,1)S(1)} %get-tuple-element.460), channel_id=1, source_target_pairs={{2,0},{3,1},{4,2},{5,3},{6,4},{7,5},{8,6},{9,7},{10,8},{11,9},{12,... | collective-permute-start | bytes 98312 | tf_op jit(solution)/shard_map/while/body/eval_jaxpr/ppermute | solution.py:16
  128.9 6.7 %collective-permute-start = (bf16[16,1024]{1,0:T(8,128)(2,1)S(1)}, bf16[16,1024]{1,0:T(8,128)(2,1)S(1)}, u32[]{:S(2)}, u32[]{:S(2)}) collective-permute-start(bf16[16,1024]{1,0:T(8,128)(2,1)S(1)} %get-tuple-element.460), channel_id=1, source_target_pairs={{2,0},{3,1},{4,2},{5,3},{6,4},{7,5},{8,6},{9,7},{10,8},{11,9},{12,... | collective-permute-start | bytes 98312 | tf_op jit(solution)/shard_map/while/body/eval_jaxpr/ppermute | solution.py:16
  136.2 6.7 %collective-permute-start = (bf16[16,1024]{1,0:T(8,128)(2,1)S(1)}, bf16[16,1024]{1,0:T(8,128)(2,1)S(1)}, u32[]{:S(2)}, u32[]{:S(2)}) collective-permute-start(bf16[16,1024]{1,0:T(8,128)(2,1)S(1)} %get-tuple-element.460), channel_id=1, source_target_pairs={{2,0},{3,1},{4,2},{5,3},{6,4},{7,5},{8,6},{9,7},{10,8},{11,9},{12,... | collective-permute-start | bytes 98312 | tf_op jit(solution)/shard_map/while/body/eval_jaxpr/ppermute | solution.py:16
  143.6 6.8 %collective-permute-start = (bf16[16,1024]{1,0:T(8,128)(2,1)S(1)}, bf16[16,1024]{1,0:T(8,128)(2,1)S(1)}, u32[]{:S(2)}, u32[]{:S(2)}) collective-permute-start(bf16[16,1024]{1,0:T(8,128)(2,1)S(1)} %get-tuple-element.460), channel_id=1, source_target_pairs={{2,0},{3,1},{4,2},{5,3},{6,4},{7,5},{8,6},{9,7},{10,8},{11,9},{12,... | collective-permute-start | bytes 98312 | tf_op jit(solution)/shard_map/while/body/eval_jaxpr/ppermute | solution.py:16
  151.0 7.0 %collective-permute-start = (bf16[16,1024]{1,0:T(8,128)(2,1)S(1)}, bf16[16,1024]{1,0:T(8,128)(2,1)S(1)}, u32[]{:S(2)}, u32[]{:S(2)}) collective-permute-start(bf16[16,1024]{1,0:T(8,128)(2,1)S(1)} %get-tuple-element.460), channel_id=1, source_target_pairs={{2,0},{3,1},{4,2},{5,3},{6,4},{7,5},{8,6},{9,7},{10,8},{11,9},{12,... | collective-permute-start | bytes 98312 | tf_op jit(solution)/shard_map/while/body/eval_jaxpr/ppermute | solution.py:16
  158.6 6.7 %collective-permute-start = (bf16[16,1024]{1,0:T(8,128)(2,1)S(1)}, bf16[16,1024]{1,0:T(8,128)(2,1)S(1)}, u32[]{:S(2)}, u32[]{:S(2)}) collective-permute-start(bf16[16,1024]{1,0:T(8,128)(2,1)S(1)} %get-tuple-element.460), channel_id=1, source_target_pairs={{2,0},{3,1},{4,2},{5,3},{6,4},{7,5},{8,6},{9,7},{10,8},{11,9},{12,... | collective-permute-start | bytes 98312 | tf_op jit(solution)/shard_map/while/body/eval_jaxpr/ppermute | solution.py:16
  166.0 6.7 %collective-permute-start = (bf16[16,1024]{1,0:T(8,128)(2,1)S(1)}, bf16[16,1024]{1,0:T(8,128)(2,1)S(1)}, u32[]{:S(2)}, u32[]{:S(2)}) collective-permute-start(bf16[16,1024]{1,0:T(8,128)(2,1)S(1)} %get-tuple-element.460), channel_id=1, source_target_pairs={{2,0},{3,1},{4,2},{5,3},{6,4},{7,5},{8,6},{9,7},{10,8},{11,9},{12,... | collective-permute-start | bytes 98312 | tf_op jit(solution)/shard_map/while/body/eval_jaxpr/ppermute | solution.py:16
  173.4 6.7 %collective-permute-start = (bf16[16,1024]{1,0:T(8,128)(2,1)S(1)}, bf16[16,1024]{1,0:T(8,128)(2,1)S(1)}, u32[]{:S(2)}, u32[]{:S(2)}) collective-permute-start(bf16[16,1024]{1,0:T(8,128)(2,1)S(1)} %get-tuple-element.460), channel_id=1, source_target_pairs={{2,0},{3,1},{4,2},{5,3},{6,4},{7,5},{8,6},{9,7},{10,8},{11,9},{12,... | collective-permute-start | bytes 98312 | tf_op jit(solution)/shard_map/while/body/eval_jaxpr/ppermute | solution.py:16
  (1 other events, 0.7 us)
where the time goes:
time: 182 us; the launch traced here: 181 us
  starting transfers between devices  64.8 us (36%)
  waiting for transfers between devices  62.9 us (35%)
  matrix products  49.9 us (27%)
  local copies, waits for them, and re-layouts  2.33 us (1%)
    ppermute x22, starting transfers between devices, from_behind(): lax.ppermute(value, axis, [(source, source + steps) for source in range(f...  64.2 us
    ppermute x22, waiting for transfers between devices, from_behind(): lax.ppermute(value, axis, [(source, source + steps) for source in range(f...  59.6 us
    dot_general x11, matrix products, down_step(): echo = jnp.dot(current, merged_r, preferred_element_type=jnp.float32)  22.2 us
    dot_general x1, matrix products, shards(): jnp.dot(upper_t, inner, preferred_element_type=jnp.float32)  10.7 us
    dot_general x11, matrix products, matmul_nt(): lax.dot_general(left, right, (((1,), (1,)), ((), ())), preferred_element_...  7.11 us
    dot_general x1, matrix products, shards(): jnp.dot(upper_t, lower_t, preferred_element_type=jnp.float32)  5.2 us
    dot_general x11, matrix products, down_step(): jnp.dot(current, merged_t, preferred_element_type=jnp.float32)  4.65 us
  transfers between devices with their start and end apart: 24, of which 12 were waited for; matrix products, arithmetic and copies ran while one was open for 16% of the time, Pallas kernels for 0%

commit v1 on v0

v1 whole, which is shorter than its diff:
```python
import jax
import jax.numpy as jnp
from jax import lax
from jax.sharding import PartitionSpec as P


def swap_cores(array):
    return lax.ppermute(array, "sec", [(i, i ^ 1) for i in range(lax.axis_size("sec"))])


def swap_sections(value, one, two):
    pairs = []
    for device in range(lax.axis_size("sec")):
        section, core = divmod(device, 2)
        if section == one:
            target = 2 * two + core
        elif section == two:
            target = 2 * one + core
        else:
            target = device ^ 1
        pairs.append((device, target))
    return lax.ppermute(value, "sec", pairs)


def matmul(left, right):
    return jnp.dot(left, right, preferred_element_type=jnp.float32)


def matmul_nt(left, right):
    return lax.dot_general(
        left, right, (((1,), (1,)), ((), ())), preferred_element_type=jnp.float32
    )


def rounded(value):
    return value.astype(jnp.bfloat16)


def merge_trans(upper_t, lower_t):
    return rounded(matmul(upper_t, lower_t))


def echo_of(down, upper_t, upper_r, lower_r):
    through = rounded(matmul(down, upper_t))
    back = rounded(matmul(through, lower_r))
    return matmul(down, upper_r) + matmul_nt(back, upper_t)


def shards(layer_trans, layer_refl, source_modes):
    position = lax.axis_index("sec")
    section = position // 2
    parity = position % 2
    is_upper = parity == 0
    sections = lax.axis_size("sec") // 2
    trans = layer_trans[0]
    refl = layer_refl[0]
    half = source_modes.shape[0] // 2

    columns = jnp.arange(trans.shape[0], dtype=jnp.int32)
    units = rounded(source_modes[:, None] == columns[None, :])
    picked = rounded(matmul(units, trans))
    picked = swap_cores(picked)
    first = rounded(matmul(picked, trans))
    first = jnp.where(is_upper, swap_cores(first[:half]), first[half:])

    other_t = swap_cores(trans)
    other_r = swap_cores(refl)
    incoming = swap_sections(first, 0, 1)
    merged_t = lax.cond(
        is_upper,
        lambda: merge_trans(trans, other_t),
        lambda: merge_trans(other_t, trans),
    )
    mine = jnp.where(is_upper, units[:half], units[half:])
    mine = jnp.where(section == 1, incoming, mine)
    for step in range(1, sections - 1):
        incoming = swap_sections(rounded(matmul(incoming, merged_t)), step, step + 1)
        mine = jnp.where(section == step + 1, incoming, mine)

    echo = lax.cond(
        is_upper,
        lambda: echo_of(mine, trans, refl, other_r),
        lambda: echo_of(mine, other_t, other_r, refl),
    )

    value = rounded(echo)
    upgoing = value
    for step in range(sections - 2, -1, -1):
        incoming = swap_sections(value, step + 1, step)
        value = rounded(echo + matmul_nt(incoming, merged_t))
        upgoing = jnp.where(section == step, value, upgoing)
    return upgoing[None]


def solution(mesh):
    return jax.shard_map(
        shards,
        mesh=mesh,
        in_specs=(P("sec", None, None), P("sec", None, None), P("freq")),
        out_specs=P(("freq", "sec"), None, None),
        check_vma=False,
    )
```

time: 182 us -> 92.8 us (0.51)
  waiting for transfers between devices: 62.9 us -> 19.7 us
  matrix products: 49.9 us -> 25 us
  starting transfers between devices: 64.8 us -> 47.3 us
  local copies, waits for them, and re-layouts: 2.33 us -> 0.02 us
    ppermute x24 -> x18, waiting for transfers between devices: 62.9 us -> 19.7 us  [the longest x14 16.7 us: swap_sections(): return lax.ppermute(value, 'sec', pairs)]
    dot_general x24 -> x11, matrix products: 42.8 us -> 15.7 us  [matmul(): return jnp.dot(left, right, preferred_element_type=jnp.float32)]
    ppermute x24 -> x18, starting transfers between devices: 64.8 us -> 47.3 us  [the longest x14 45.9 us: swap_sections(): return lax.ppermute(value, 'sec', pairs)]
    dot_general x11 -> x8, matrix products: 7.11 us -> 9.33 us  [matmul_nt(): lax.dot_general(left, right, (((1,), (1,)), ((), ())), preferred_element_...]
  transfers between devices with their start and end apart: 24 -> 18, of which waited for: 12 -> 15; matrix products, arithmetic and copies ran while one was open for 16% -> 12% of each run, Pallas kernels for 0% -> 0%
where the time goes in v1:
time: 92.8 us; the launch traced here: 92.6 us
  starting transfers between devices  47.3 us (51%)
  matrix products  25 us (27%)
  waiting for transfers between devices  19.7 us (21%)
    ppermute x14, starting transfers between devices, swap_sections(): return lax.ppermute(value, 'sec', pairs)  45.9 us
    ppermute x14, waiting for transfers between devices, swap_sections(): return lax.ppermute(value, 'sec', pairs)  16.7 us
    dot_general x11, matrix products, matmul(): return jnp.dot(left, right, preferred_element_type=jnp.float32)  15.7 us
    dot_general x8, matrix products, matmul_nt(): lax.dot_general(left, right, (((1,), (1,)), ((), ())), preferred_element_...  9.33 us
    ppermute x4, waiting for transfers between devices, swap_cores(): lax.ppermute(array, 'sec', [(i, i ^ 1) for i in range(lax.axis_size('sec'...  2.93 us
  transfers between devices with their start and end apart: 18, of which 15 were waited for; matrix products, arithmetic and copies ran while one was open for 12% of the time, Pallas kernels for 0%

profile of v1, /device:TPU:0, one launch (start us, length us, event | category | flops | bytes accessed | tf_op | source)
XLA Modules:
  0.0 92.6 jit_solution(13183301210934174355)
XLA Ops:
  0.5 2.1 %convolution_convert_fusion.5 = bf16[128,1024]{1,0:T(8,128)(2,1)S(1)} fusion(s32[128]{0:T(128)} %param.9, bf16[1,1024,1024]{2,1,0:T(8,128)(2,1)} %param.7), kind=kOutput, calls=%fused_computation.7 | convolution fusion | flops 268697600 | bytes 2359808 | tf_op jit(solution)/shard_map/dot_general | solution.py:26
  2.7 1.9 %collective-permute-done = bf16[128,1024]{1,0:T(8,128)(2,1)S(1)} collective-permute-done((bf16[128,1024]{1,0:T(8,128)(2,1)S(1)}, bf16[128,1024]{1,0:T(8,128)(2,1)S(1)}, u32[]{:S(2)}, u32[]{:S(2)}) %collective-permute-start) | collective-permute-done | bytes 262176 | tf_op jit(solution)/shard_map/ppermute | solution.py:8
  4.6 2.0 %convolution_convert_fusion.4 = bf16[128,1024]{1,0:T(8,128)(2,1)S(1)} fusion(bf16[128,1024]{1,0:T(8,128)(2,1)S(1)} %collective-permute-done, bf16[1,1024,1024]{2,1,0:T(8,128)(2,1)} %param.7), kind=kOutput, calls=%fused_computation.6 | convolution fusion | flops 268566528 | bytes 2621440 | tf_op jit(solution)/shard_map/dot_general | solution.py:26
  7.1 1.0 %collective-permute-done.1 = bf16[64,1024]{1,0:T(8,128)(2,1)S(1)} collective-permute-done((bf16[64,1024]{1,0:T(8,128)(2,1)S(1)}, bf16[64,1024]{1,0:T(8,128)(2,1)S(1)}, u32[]{:S(2)}, u32[]{:S(2)}) %collective-permute-start.1) | collective-permute-done | bytes 131104 | tf_op jit(solution)/shard_map/ppermute | solution.py:8
  8.1 2.9 %collective-permute-start.2 = (bf16[64,1024]{1,0:T(8,128)(2,1)S(1)}, bf16[64,1024]{1,0:T(8,128)(2,1)S(1)}, u32[]{:S(2)}, u32[]{:S(2)}) collective-permute-start(bf16[64,1024]{1,0:T(8,128)(2,1)S(1)} %slice_select_fusion.1), channel_id=1, source_target_pairs={{0,2},{1,3},{2,0},{3,1},{4,5},{5,4},{6,7},{7,6},{8,9},{9,8},{10,11... | collective-permute-start | bytes 393224 | tf_op jit(solution)/shard_map/ppermute | solution.py:22
  11.1 4.5 %conditional.5 = (bf16[1024,1024]{1,0:T(8,128)(2,1)S(1)}) conditional(s32[]{:T(128)} %convert_element_type.86, (bf16[1024,1024]{1,0:T(8,128)(2,1)}, bf16[1024,1024]{1,0:T(8,128)(2,1)}) %tuple.46, (bf16[1024,1024]{1,0:T(8,128)(2,1)}, bf16[1024,1024]{1,0:T(8,128)(2,1)}) %tuple.47), branch_computations={%region_0.1_spmd, %region_1.2_spmd} | conditional | flops 2147483648 | bytes 6291464
  11.1 4.5 %fusion.21 = bf16[1024,1024]{1,0:T(8,128)(2,1)S(1)} fusion(bf16[1024,1024]{1,0:T(8,128)(2,1)} %get-tuple-element.67, bf16[1024,1024]{1,0:T(8,128)(2,1)} %get-tuple-element.68), kind=kOutput, calls=%fused_computation.45 | convolution fusion | flops 2147483648 | bytes 6291456 | tf_op jit(solution)/shard_map/cond/branch_1_fun/dot_general | solution.py:26
  16.2 1.3 %collective-permute-done.4 = bf16[64,1024]{1,0:T(8,128)(2,1)S(1)} collective-permute-done((bf16[64,1024]{1,0:T(8,128)(2,1)S(1)}, bf16[64,1024]{1,0:T(8,128)(2,1)S(1)}, u32[]{:S(2)}, u32[]{:S(2)}) %collective-permute-start.4) | collective-permute-done | bytes 131104 | tf_op jit(solution)/shard_map/ppermute | solution.py:22
  20.1 2.5 %collective-permute-done.6 = bf16[64,1024]{1,0:T(8,128)(2,1)S(1)} collective-permute-done((bf16[64,1024]{1,0:T(8,128)(2,1)S(1)}, bf16[64,1024]{1,0:T(8,128)(2,1)S(1)}, u32[]{:S(2)}, u32[]{:S(2)}) %collective-permute-start.6) | collective-permute-done | bytes 131104 | tf_op jit(solution)/shard_map/ppermute | solution.py:22
  23.5 1.0 %collective-permute-done.7 = bf16[64,1024]{1,0:T(8,128)(2,1)S(1)} collective-permute-done((bf16[64,1024]{1,0:T(8,128)(2,1)S(1)}, bf16[64,1024]{1,0:T(8,128)(2,1)S(1)}, u32[]{:S(2)}, u32[]{:S(2)}) %collective-permute-start.7) | collective-permute-done | bytes 131104 | tf_op jit(solution)/shard_map/ppermute | solution.py:22
  25.4 1.0 %collective-permute-done.8 = bf16[64,1024]{1,0:T(8,128)(2,1)S(1)} collective-permute-done((bf16[64,1024]{1,0:T(8,128)(2,1)S(1)}, bf16[64,1024]{1,0:T(8,128)(2,1)S(1)}, u32[]{:S(2)}, u32[]{:S(2)}) %collective-permute-start.8) | collective-permute-done | bytes 131104 | tf_op jit(solution)/shard_map/ppermute | solution.py:22
  28.4 7.7 %conditional.12 = (f32[64,1024]{1,0:T(8,128)S(1)}) conditional(s32[]{:T(128)} %convert_element_type.86, (bf16[64,1024]{1,0:T(8,128)(2,1)S(1)}, bf16[1024,1024]{1,0:T(8,128)(2,1)}, bf16[1024,1024]{1,0:T(8,128)(2,1)}, bf16[1024,1024]{1,0:T(8,128)(2,1)}) %tuple.40, (bf16[64,1024]{1,0:T(8,128)(2,1)S(1)}, bf16[1024,1024]{1,0:T(8,128)(2,1)}, ...), branch_computations={%region_2.3_spmd, %region_3.4_spmd} | conditional | flops 537067520 | bytes 9699336
  28.4 2.1 %convolution_convert_fusion.3 = bf16[64,1024]{1,0:T(8,128)(2,1)S(1)} fusion(bf16[64,1024]{1,0:T(8,128)(2,1)S(1)} %get-tuple-element.73, bf16[1024,1024]{1,0:T(8,128)(2,1)} %get-tuple-element.75), kind=kOutput, calls=%fused_computation.5 | convolution fusion | flops 134283264 | bytes 2359296 | tf_op jit(solution)/shard_map/cond/branch_1_fun/dot_general | solution.py:26
  30.5 2.1 %fusion.23 = f32[64,1024]{1,0:T(8,128)S(1)} fusion(bf16[64,1024]{1,0:T(8,128)(2,1)S(1)} %get-tuple-element.73, bf16[1024,1024]{1,0:T(8,128)(2,1)} %get-tuple-element.74), kind=kOutput, calls=%fused_computation.47 | convolution fusion | flops 134217728 | bytes 2490368 | tf_op jit(solution)/shard_map/cond/branch_1_fun/dot_general | solution.py:26
  32.6 3.3 %convolution_add_fusion.1 = f32[64,1024]{1,0:T(8,128)S(1)} fusion(f32[64,1024]{1,0:T(8,128)S(1)} %fusion.23, bf16[1024,1024]{1,0:T(8,128)(2,1)} %get-tuple-element.75, bf16[64,1024]{1,0:T(8,128)(2,1)S(1)} %convolution_convert_fusion.3, bf16[1024,1024]{1,0:T(8,128)(2,1)} %get-tuple-element.76), kind=kOutput, calls=%fused_computation.3 | convolution fusion | flops 268566528 | bytes 4849664 | tf_op jit(solution)/shard_map/cond/branch_1_fun/dot_general | solution.py:30
  36.5 1.0 %collective-permute-done.11 = bf16[64,1024]{1,0:T(8,128)(2,1)S(1)} collective-permute-done((bf16[64,1024]{1,0:T(8,128)(2,1)S(1)}, bf16[64,1024]{1,0:T(8,128)(2,1)S(1)}, u32[]{:S(2)}, u32[]{:S(2)}) %collective-permute-start.11) | collective-permute-done | bytes 131104 | tf_op jit(solution)/shard_map/ppermute | solution.py:22
  38.7 1.0 %collective-permute-done.12 = bf16[64,1024]{1,0:T(8,128)(2,1)S(1)} collective-permute-done((bf16[64,1024]{1,0:T(8,128)(2,1)S(1)}, bf16[64,1024]{1,0:T(8,128)(2,1)S(1)}, u32[]{:S(2)}, u32[]{:S(2)}) %collective-permute-start.12) | collective-permute-done | bytes 131104 | tf_op jit(solution)/shard_map/ppermute | solution.py:22
  40.9 1.0 %collective-permute-done.13 = bf16[64,1024]{1,0:T(8,128)(2,1)S(1)} collective-permute-done((bf16[64,1024]{1,0:T(8,128)(2,1)S(1)}, bf16[64,1024]{1,0:T(8,128)(2,1)S(1)}, u32[]{:S(2)}, u32[]{:S(2)}) %collective-permute-start.13) | collective-permute-done | bytes 131104 | tf_op jit(solution)/shard_map/ppermute | solution.py:22
  43.1 1.0 %collective-permute-done.14 = bf16[64,1024]{1,0:T(8,128)(2,1)S(1)} collective-permute-done((bf16[64,1024]{1,0:T(8,128)(2,1)S(1)}, bf16[64,1024]{1,0:T(8,128)(2,1)S(1)}, u32[]{:S(2)}, u32[]{:S(2)}) %collective-permute-start.14) | collective-permute-done | bytes 131104 | tf_op jit(solution)/shard_map/ppermute | solution.py:22
  45.2 1.0 %collective-permute-done.15 = bf16[64,1024]{1,0:T(8,128)(2,1)S(1)} collective-permute-done((bf16[64,1024]{1,0:T(8,128)(2,1)S(1)}, bf16[64,1024]{1,0:T(8,128)(2,1)S(1)}, u32[]{:S(2)}, u32[]{:S(2)}) %collective-permute-start.15) | collective-permute-done | bytes 131104 | tf_op jit(solution)/shard_map/ppermute | solution.py:22
  47.4 1.0 %collective-permute-done.16 = bf16[64,1024]{1,0:T(8,128)(2,1)S(1)} collective-permute-done((bf16[64,1024]{1,0:T(8,128)(2,1)S(1)}, bf16[64,1024]{1,0:T(8,128)(2,1)S(1)}, u32[]{:S(2)}, u32[]{:S(2)}) %collective-permute-start.16) | collective-permute-done | bytes 131104 | tf_op jit(solution)/shard_map/ppermute | solution.py:22
  49.2 39.0 %collective-permute-start.17 = (bf16[64,1024]{1,0:T(8,128)(2,1)S(1)}, bf16[64,1024]{1,0:T(8,128)(2,1)S(1)}, u32[]{:S(2)}, u32[]{:S(2)}) collective-permute-start(bf16[64,1024]{1,0:T(8,128)(2,1)S(1)} %fusion.5), channel_id=1, source_target_pairs={{0,2},{1,3},{2,0},{3,1},{4,5},{5,4},{6,7},{7,6},{8,9},{9,8},{10,11... | collective-permute-start | bytes 393224 | tf_op jit(solution)/shard_map/ppermute | solution.py:22
  88.2 2.9 %collective-permute-done.17 = bf16[64,1024]{1,0:T(8,128)(2,1)S(1)} collective-permute-done((bf16[64,1024]{1,0:T(8,128)(2,1)S(1)}, bf16[64,1024]{1,0:T(8,128)(2,1)S(1)}, u32[]{:S(2)}, u32[]{:S(2)}) %collective-permute-start.17) | collective-permute-done | bytes 131104 | tf_op jit(solution)/shard_map/ppermute | solution.py:22
  91.1 1.4 %fusion.8 = bf16[1,64,1024]{2,1,0:T(8,128)(2,1)} fusion(f32[64,1024]{1,0:T(8,128)S(1)} %get-tuple-element.78, bf16[64,1024]{1,0:T(8,128)(2,1)S(1)} %collective-permute-done.17, bf16[1024,1024]{1,0:T(8,128)(2,1)S(1)} %get-tuple-element.77, bf16[64,1024]{1,0:T(8,128)(2,1)S(1)} %fusion.5, bf16[64,1024]{1,0:T(8,128)(2,1)S(1)} %fusion.4, ...), kind=kOutput, calls=%fused_computation.29 | convolution fusion | flops 134873088 | bytes 3407879 | tf_op jit(solution)/shard_map/dot_general | solution.py:30
  (40 shorter events, 14.8 us)
Async XLA Ops:
  0.0 11.1 %collective-permute-start.3 = (bf16[1024,1024]{1,0:T(8,128)(2,1)}, bf16[1024,1024]{1,0:T(8,128)(2,1)}, u32[]{:S(2)}, u32[]{:S(2)}) collective-permute-start(bf16[1024,1024]{1,0:T(8,128)(2,1)} %bitcast.53), channel_id=1, source_target_pairs={{0,1},{1,0},{2,3},{3,2},{4,5},{5,4},{6,7},{7,6},{8,9},{9,8},{10,11... | collective-permute-start | bytes 6291464 | tf_op jit(solution)/shard_map/ppermute | solution.py:8
  2.5 2.1 %collective-permute-start = (bf16[128,1024]{1,0:T(8,128)(2,1)S(1)}, bf16[128,1024]{1,0:T(8,128)(2,1)S(1)}, u32[]{:S(2)}, u32[]{:S(2)}) collective-permute-start(bf16[128,1024]{1,0:T(8,128)(2,1)S(1)} %convolution_convert_fusion.5), channel_id=1, source_target_pairs={{0,1},{1,0},{2,3},{3,2},{4,5},{5,4},{6,7},{7,6},{8,9},{9,8},{10,11... | collective-permute-start | bytes 786440 | tf_op jit(solution)/shard_map/ppermute | solution.py:8
  6.7 1.4 %collective-permute-start.1 = (bf16[64,1024]{1,0:T(8,128)(2,1)S(1)}, bf16[64,1024]{1,0:T(8,128)(2,1)S(1)}, u32[]{:S(2)}, u32[]{:S(2)}) collective-permute-start(bf16[64,1024]{1,0:T(8,128)(2,1)S(1)} %slice.16), channel_id=1, source_target_pairs={{0,1},{1,0},{2,3},{3,2},{4,5},{5,4},{6,7},{7,6},{8,9},{9,8},{10,11... | collective-permute-start | bytes 393224 | tf_op jit(solution)/shard_map/ppermute | solution.py:8
  8.1 7.5 %collective-permute-start.2 = (bf16[64,1024]{1,0:T(8,128)(2,1)S(1)}, bf16[64,1024]{1,0:T(8,128)(2,1)S(1)}, u32[]{:S(2)}, u32[]{:S(2)}) collective-permute-start(bf16[64,1024]{1,0:T(8,128)(2,1)S(1)} %slice_select_fusion.1), channel_id=1, source_target_pairs={{0,2},{1,3},{2,0},{3,1},{4,5},{5,4},{6,7},{7,6},{8,9},{9,8},{10,11... | collective-permute-start | bytes 393224 | tf_op jit(solution)/shard_map/ppermute | solution.py:22
  16.1 1.4 %collective-permute-start.4 = (bf16[64,1024]{1,0:T(8,128)(2,1)S(1)}, bf16[64,1024]{1,0:T(8,128)(2,1)S(1)}, u32[]{:S(2)}, u32[]{:S(2)}) collective-permute-start(bf16[64,1024]{1,0:T(8,128)(2,1)S(1)} %convolution_convert_fusion.11), channel_id=1, source_target_pairs={{0,1},{1,0},{2,4},{3,5},{4,2},{5,3},{6,7},{7,6},{8,9},{9,8},{10,11... | collective-permute-start | bytes 393224 | tf_op jit(solution)/shard_map/ppermute | solution.py:22
  18.0 1.4 %collective-permute-start.5 = (bf16[64,1024]{1,0:T(8,128)(2,1)S(1)}, bf16[64,1024]{1,0:T(8,128)(2,1)S(1)}, u32[]{:S(2)}, u32[]{:S(2)}) collective-permute-start(bf16[64,1024]{1,0:T(8,128)(2,1)S(1)} %convolution_convert_fusion.10), channel_id=1, source_target_pairs={{0,1},{1,0},{2,3},{3,2},{4,6},{5,7},{6,4},{7,5},{8,9},{9,8},{10,11... | collective-permute-start | bytes 393224 | tf_op jit(solution)/shard_map/ppermute | solution.py:22
  18.2 10.2 %collective-permute-start.10 = (bf16[1024,1024]{1,0:T(8,128)(2,1)}, bf16[1024,1024]{1,0:T(8,128)(2,1)}, u32[]{:S(2)}, u32[]{:S(2)}) collective-permute-start(bf16[1024,1024]{1,0:T(8,128)(2,1)} %bitcast.1), channel_id=1, source_target_pairs={{0,1},{1,0},{2,3},{3,2},{4,5},{5,4},{6,7},{7,6},{8,9},{9,8},{10,11... | collective-permute-start | bytes 6291464 | tf_op jit(solution)/shard_map/ppermute | solution.py:8
  19.9 2.7 %collective-permute-start.6 = (bf16[64,1024]{1,0:T(8,128)(2,1)S(1)}, bf16[64,1024]{1,0:T(8,128)(2,1)S(1)}, u32[]{:S(2)}, u32[]{:S(2)}) collective-permute-start(bf16[64,1024]{1,0:T(8,128)(2,1)S(1)} %convolution_convert_fusion.9), channel_id=1, source_target_pairs={{0,1},{1,0},{2,3},{3,2},{4,5},{5,4},{6,8},{7,9},{8,6},{9,7},{10,11... | collective-permute-start | bytes 393224 | tf_op jit(solution)/shard_map/ppermute | solution.py:22
  23.1 4.2 %copy-start = (s32[128]{0:T(128)S(1)}, s32[128]{0:T(128)}, u32[]{:S(2)}) copy-start(s32[128]{0:T(128)} %param.9) | copy-start | bytes 1540
  23.1 1.4 %collective-permute-start.7 = (bf16[64,1024]{1,0:T(8,128)(2,1)S(1)}, bf16[64,1024]{1,0:T(8,128)(2,1)S(1)}, u32[]{:S(2)}, u32[]{:S(2)}) collective-permute-start(bf16[64,1024]{1,0:T(8,128)(2,1)S(1)} %convolution_convert_fusion.8), channel_id=1, source_target_pairs={{0,1},{1,0},{2,3},{3,2},{4,5},{5,4},{6,7},{7,6},{8,10},{9,11},{10,... | collective-permute-start | bytes 393224 | tf_op jit(solution)/shard_map/ppermute | solution.py:22
  25.0 1.4 %collective-permute-start.8 = (bf16[64,1024]{1,0:T(8,128)(2,1)S(1)}, bf16[64,1024]{1,0:T(8,128)(2,1)S(1)}, u32[]{:S(2)}, u32[]{:S(2)}) collective-permute-start(bf16[64,1024]{1,0:T(8,128)(2,1)S(1)} %convolution_convert_fusion.7), channel_id=1, source_target_pairs={{0,1},{1,0},{2,3},{3,2},{4,5},{5,4},{6,7},{7,6},{8,9},{9,8},{10,12... | collective-permute-start | bytes 393224 | tf_op jit(solution)/shard_map/ppermute | solution.py:22
  26.9 1.4 %collective-permute-start.9 = (bf16[64,1024]{1,0:T(8,128)(2,1)S(1)}, bf16[64,1024]{1,0:T(8,128)(2,1)S(1)}, u32[]{:S(2)}, u32[]{:S(2)}) collective-permute-start(bf16[64,1024]{1,0:T(8,128)(2,1)S(1)} %convolution_convert_fusion.6), channel_id=1, source_target_pairs={{0,1},{1,0},{2,3},{3,2},{4,5},{5,4},{6,7},{7,6},{8,9},{9,8},{10,11... | collective-permute-start | bytes 393224 | tf_op jit(solution)/shard_map/ppermute | solution.py:22
  36.2 1.4 %collective-permute-start.11 = (bf16[64,1024]{1,0:T(8,128)(2,1)S(1)}, bf16[64,1024]{1,0:T(8,128)(2,1)S(1)}, u32[]{:S(2)}, u32[]{:S(2)}) collective-permute-start(bf16[64,1024]{1,0:T(8,128)(2,1)S(1)} %convert_element_type.97), channel_id=1, source_target_pairs={{0,1},{1,0},{2,3},{3,2},{4,5},{5,4},{6,7},{7,6},{8,9},{9,8},{10,11... | collective-permute-start | bytes 393224 | tf_op jit(solution)/shard_map/ppermute | solution.py:22
  38.3 1.4 %collective-permute-start.12 = (bf16[64,1024]{1,0:T(8,128)(2,1)S(1)}, bf16[64,1024]{1,0:T(8,128)(2,1)S(1)}, u32[]{:S(2)}, u32[]{:S(2)}) collective-permute-start(bf16[64,1024]{1,0:T(8,128)(2,1)S(1)} %fusion), channel_id=1, source_target_pairs={{0,1},{1,0},{2,3},{3,2},{4,5},{5,4},{6,7},{7,6},{8,9},{9,8},{10,12... | collective-permute-start | bytes 393224 | tf_op jit(solution)/shard_map/ppermute | solution.py:22
  40.5 1.4 %collective-permute-start.13 = (bf16[64,1024]{1,0:T(8,128)(2,1)S(1)}, bf16[64,1024]{1,0:T(8,128)(2,1)S(1)}, u32[]{:S(2)}, u32[]{:S(2)}) collective-permute-start(bf16[64,1024]{1,0:T(8,128)(2,1)S(1)} %fusion.1), channel_id=1, source_target_pairs={{0,1},{1,0},{2,3},{3,2},{4,5},{5,4},{6,7},{7,6},{8,10},{9,11},{10,... | collective-permute-start | bytes 393224 | tf_op jit(solution)/shard_map/ppermute | solution.py:22
  42.7 1.4 %collective-permute-start.14 = (bf16[64,1024]{1,0:T(8,128)(2,1)S(1)}, bf16[64,1024]{1,0:T(8,128)(2,1)S(1)}, u32[]{:S(2)}, u32[]{:S(2)}) collective-permute-start(bf16[64,1024]{1,0:T(8,128)(2,1)S(1)} %fusion.2), channel_id=1, source_target_pairs={{0,1},{1,0},{2,3},{3,2},{4,5},{5,4},{6,8},{7,9},{8,6},{9,7},{10,11... | collective-permute-start | bytes 393224 | tf_op jit(solution)/shard_map/ppermute | solution.py:22
  44.8 1.4 %collective-permute-start.15 = (bf16[64,1024]{1,0:T(8,128)(2,1)S(1)}, bf16[64,1024]{1,0:T(8,128)(2,1)S(1)}, u32[]{:S(2)}, u32[]{:S(2)}) collective-permute-start(bf16[64,1024]{1,0:T(8,128)(2,1)S(1)} %fusion.3), channel_id=1, source_target_pairs={{0,1},{1,0},{2,3},{3,2},{4,6},{5,7},{6,4},{7,5},{8,9},{9,8},{10,11... | collective-permute-start | bytes 393224 | tf_op jit(solution)/shard_map/ppermute | solution.py:22
  47.0 1.4 %collective-permute-start.16 = (bf16[64,1024]{1,0:T(8,128)(2,1)S(1)}, bf16[64,1024]{1,0:T(8,128)(2,1)S(1)}, u32[]{:S(2)}, u32[]{:S(2)}) collective-permute-start(bf16[64,1024]{1,0:T(8,128)(2,1)S(1)} %fusion.4), channel_id=1, source_target_pairs={{0,1},{1,0},{2,4},{3,5},{4,2},{5,3},{6,7},{7,6},{8,9},{9,8},{10,11... | collective-permute-start | bytes 393224 | tf_op jit(solution)/shard_map/ppermute | solution.py:22
  49.2 42.0 %collective-permute-start.17 = (bf16[64,1024]{1,0:T(8,128)(2,1)S(1)}, bf16[64,1024]{1,0:T(8,128)(2,1)S(1)}, u32[]{:S(2)}, u32[]{:S(2)}) collective-permute-start(bf16[64,1024]{1,0:T(8,128)(2,1)S(1)} %fusion.5), channel_id=1, source_target_pairs={{0,2},{1,3},{2,0},{3,1},{4,5},{5,4},{6,7},{7,6},{8,9},{9,8},{10,11... | collective-permute-start | bytes 393224 | tf_op jit(solution)/shard_map/ppermute | solution.py:22

commit v2 on v1

--- a/solution.py
+++ b/solution.py
@@ -1,7 +1,11 @@
 import jax
 import jax.numpy as jnp
 from jax import lax
+from jax.experimental import pallas as pl
+from jax.experimental.pallas import tpu as pltpu
 from jax.sharding import PartitionSpec as P
+
+BLOCKS = 4
 
 
 def swap_cores(array):
@@ -40,10 +44,62 @@
     return rounded(matmul(upper_t, lower_t))
 
 
-def echo_of(down, upper_t, upper_r, lower_r):
-    through = rounded(matmul(down, upper_t))
-    back = rounded(matmul(through, lower_r))
-    return matmul(down, upper_r) + matmul_nt(back, upper_t)
+def fetch(even_ref, odd_ref, target, sems, odd):
+    rows = target.shape[0] // BLOCKS
+
+    def start(ref):
+        for j in range(BLOCKS):
+            at = pl.ds(j * rows, rows)
+            pltpu.make_async_copy(ref.at[at, :], target.at[at, :], sems.at[j]).start()
+
+    pl.when(jnp.logical_not(odd))(lambda: start(even_ref))
+    pl.when(odd)(lambda: start(odd_ref))
+
+
+def arrived(ref, target, sems, j):
+    rows = target.shape[0] // BLOCKS
+    at = pl.ds(j * rows, rows)
+    pltpu.make_async_copy(ref.at[at, :], target.at[at, :], sems.at[j]).wait()
+
+
+def streamed(left, ref, target, sems):
+    rows = target.shape[0] // BLOCKS
+    total = None
+    for j in range(BLOCKS):
+        arrived(ref, target, sems, j)
+        part = matmul(left[:, j * rows : (j + 1) * rows], target[pl.ds(j * rows, rows), :])
+        total = part if total is None else total + part
+    return total
+
+
+def echo_kernel(down, trans, other_t, refl, other_r, out, upper_t, upper_r, lower_r, sems):
+    odd = lax.rem(lax.axis_index("sec"), 2) == 1
+    fetch(trans, other_t, upper_t, sems.at[0], odd)
+    fetch(other_r, refl, lower_r, sems.at[1], odd)
+    fetch(refl, other_r, upper_r, sems.at[2], odd)
+    field = down[...]
+    through = rounded(streamed(field, trans, upper_t, sems.at[0]))
+    back = rounded(streamed(through, refl, lower_r, sems.at[1]))
+    direct = streamed(field, refl, upper_r, sems.at[2])
+    out[...] = direct + matmul_nt(back, upper_t[...])
+
+
+def echo_of(down, trans, other_t, refl, other_r):
+    size = trans.shape[0]
+    matrix = pltpu.VMEM((size, size), jnp.bfloat16)
+    hbm = pl.BlockSpec(memory_space=pltpu.HBM)
+    vmem = pl.BlockSpec(memory_space=pltpu.VMEM)
+    return pl.pallas_call(
+        echo_kernel,
+        out_shape=jax.ShapeDtypeStruct(down.shape, jnp.float32),
+        in_specs=[vmem, hbm, hbm, hbm, hbm],
+        out_specs=vmem,
+        scratch_shapes=[matrix, matrix, matrix, pltpu.SemaphoreType.DMA((3, BLOCKS))],
+        compiler_params=pltpu.CompilerParams(vmem_limit_bytes=52 * 2**20),
+        cost_estimate=pl.CostEstimate(
+            flops=8 * down.shape[0] * size * size, bytes_accessed=6 * size * size, transcendentals=0
+        ),
+    )(down, trans, other_t, refl, other_r)
 
 
 def shards(layer_trans, layer_refl, source_modes):
@@ -77,11 +133,7 @@
         incoming = swap_sections(rounded(matmul(incoming, merged_t)), step, step + 1)
         mine = jnp.where(section == step + 1, incoming, mine)
 
-    echo = lax.cond(
-        is_upper,
-        lambda: echo_of(mine, trans, refl, other_r),
-        lambda: echo_of(mine, other_t, other_r, refl),
-    )
+    echo = echo_of(mine, trans, other_t, refl, other_r)
 
     value = rounded(echo)
     upgoing = value

time: 92.8 us -> 88.5 us (0.954)
  matrix products: 25 us -> 17.5 us
  Pallas kernels: 0 us -> 3.45 us
    dot_general x11 -> x9, matrix products: 15.7 us -> 11.5 us  [matmul(): return jnp.dot(left, right, preferred_element_type=jnp.float32)]
    pallas_call x0 -> x1, Pallas kernels: none -> 3.45 us  [echo_of(): pl.pallas_call(echo_kernel, out_shape=jax.ShapeDtypeStruct(down.shape, jn...]
    dot_general x8 -> x7, matrix products: 9.33 us -> 5.98 us  [matmul_nt(): lax.dot_general(left, right, (((1,), (1,)), ((), ())), preferred_element_...]
where the time goes in v2:
time: 88.5 us; the launch traced here: 88.3 us
  starting transfers between devices  47.5 us (54%)
  waiting for transfers between devices  19.4 us (22%)
  matrix products  17.5 us (20%)
  Pallas kernels  3.45 us (4%)
    ppermute x14, starting transfers between devices, swap_sections(): return lax.ppermute(value, 'sec', pairs)  46.2 us
    ppermute x14, waiting for transfers between devices, swap_sections(): return lax.ppermute(value, 'sec', pairs)  16.5 us
    dot_general x9, matrix products, matmul(): return jnp.dot(left, right, preferred_element_type=jnp.float32)  11.5 us
    dot_general x7, matrix products, matmul_nt(): lax.dot_general(left, right, (((1,), (1,)), ((), ())), preferred_element_...  5.98 us
    pallas_call x1, Pallas kernels, echo_of(): pl.pallas_call(echo_kernel, out_shape=jax.ShapeDtypeStruct(down.shape, jn...  3.45 us
    ppermute x4, waiting for transfers between devices, swap_cores(): lax.ppermute(array, 'sec', [(i, i ^ 1) for i in range(lax.axis_size('sec'...  2.93 us
  transfers between devices with their start and end apart: 18, of which 15 were waited for; matrix products, arithmetic and copies ran while one was open for 12% of the time, Pallas kernels for 0%

profile of v2, /device:TPU:0, one launch (start us, length us, event | category | flops | bytes accessed | tf_op | source)
XLA Modules:
  0.0 88.3 jit_solution(18035269599856551721)
XLA Ops:
  0.5 2.1 %convolution_convert_fusion.1 = bf16[128,1024]{1,0:T(8,128)(2,1)S(1)} fusion(s32[128]{0:T(128)} %param.7, bf16[1,1024,1024]{2,1,0:T(8,128)(2,1)} %param.5), kind=kOutput, calls=%fused_computation.1 | convolution fusion | flops 268697600 | bytes 2359808 | tf_op jit(solution)/shard_map/dot_general | solution.py:30
  2.7 1.9 %collective-permute-done = bf16[128,1024]{1,0:T(8,128)(2,1)S(1)} collective-permute-done((bf16[128,1024]{1,0:T(8,128)(2,1)S(1)}, bf16[128,1024]{1,0:T(8,128)(2,1)S(1)}, u32[]{:S(2)}, u32[]{:S(2)}) %collective-permute-start) | collective-permute-done | bytes 262176 | tf_op jit(solution)/shard_map/ppermute | solution.py:12
  4.6 2.0 %convolution_convert_fusion = bf16[128,1024]{1,0:T(8,128)(2,1)S(1)} fusion(bf16[128,1024]{1,0:T(8,128)(2,1)S(1)} %collective-permute-done, bf16[1,1024,1024]{2,1,0:T(8,128)(2,1)} %param.5), kind=kOutput, calls=%fused_computation | convolution fusion | flops 268566528 | bytes 2621440 | tf_op jit(solution)/shard_map/dot_general | solution.py:30
  7.1 1.0 %collective-permute-done.1 = bf16[64,1024]{1,0:T(8,128)(2,1)S(1)} collective-permute-done((bf16[64,1024]{1,0:T(8,128)(2,1)S(1)}, bf16[64,1024]{1,0:T(8,128)(2,1)S(1)}, u32[]{:S(2)}, u32[]{:S(2)}) %collective-permute-start.1) | collective-permute-done | bytes 131104 | tf_op jit(solution)/shard_map/ppermute | solution.py:12
  8.1 2.9 %collective-permute-start.2 = (bf16[64,1024]{1,0:T(8,128)(2,1)S(1)}, bf16[64,1024]{1,0:T(8,128)(2,1)S(1)}, u32[]{:S(2)}, u32[]{:S(2)}) collective-permute-start(bf16[64,1024]{1,0:T(8,128)(2,1)S(1)} %slice_select_fusion.1), channel_id=1, source_target_pairs={{0,2},{1,3},{2,0},{3,1},{4,5},{5,4},{6,7},{7,6},{8,9},{9,8},{10,11... | collective-permute-start | bytes 393224 | tf_op jit(solution)/shard_map/ppermute | solution.py:26
  11.1 4.5 %conditional.2 = (bf16[1024,1024]{1,0:T(8,128)(2,1)S(1)}) conditional(s32[]{:T(128)} %convert_element_type.61, (bf16[1024,1024]{1,0:T(8,128)(2,1)}, bf16[1024,1024]{1,0:T(8,128)(2,1)}) %tuple.18, (bf16[1024,1024]{1,0:T(8,128)(2,1)}, bf16[1024,1024]{1,0:T(8,128)(2,1)}) %tuple.19), branch_computations={%region_0.1_spmd, %region_1.2_spmd} | conditional | flops 2147483648 | bytes 6291464
  11.1 4.5 %fusion.21 = bf16[1024,1024]{1,0:T(8,128)(2,1)S(1)} fusion(bf16[1024,1024]{1,0:T(8,128)(2,1)} %get-tuple-element.20, bf16[1024,1024]{1,0:T(8,128)(2,1)} %get-tuple-element.21), kind=kOutput, calls=%fused_computation.39 | convolution fusion | flops 2147483648 | bytes 6291456 | tf_op jit(solution)/shard_map/cond/branch_1_fun/dot_general | solution.py:30
  16.2 1.3 %collective-permute-done.4 = bf16[64,1024]{1,0:T(8,128)(2,1)S(1)} collective-permute-done((bf16[64,1024]{1,0:T(8,128)(2,1)S(1)}, bf16[64,1024]{1,0:T(8,128)(2,1)S(1)}, u32[]{:S(2)}, u32[]{:S(2)}) %collective-permute-start.4) | collective-permute-done | bytes 131104 | tf_op jit(solution)/shard_map/ppermute | solution.py:26
  18.6 0.8 collective-permute-done.5
  20.1 2.5 %collective-permute-done.6 = bf16[64,1024]{1,0:T(8,128)(2,1)S(1)} collective-permute-done((bf16[64,1024]{1,0:T(8,128)(2,1)S(1)}, bf16[64,1024]{1,0:T(8,128)(2,1)S(1)}, u32[]{:S(2)}, u32[]{:S(2)}) %collective-permute-start.6) | collective-permute-done | bytes 131104 | tf_op jit(solution)/shard_map/ppermute | solution.py:26
  23.5 1.0 %collective-permute-done.7 = bf16[64,1024]{1,0:T(8,128)(2,1)S(1)} collective-permute-done((bf16[64,1024]{1,0:T(8,128)(2,1)S(1)}, bf16[64,1024]{1,0:T(8,128)(2,1)S(1)}, u32[]{:S(2)}, u32[]{:S(2)}) %collective-permute-start.7) | collective-permute-done | bytes 131104 | tf_op jit(solution)/shard_map/ppermute | solution.py:26
  25.4 1.0 %collective-permute-done.8 = bf16[64,1024]{1,0:T(8,128)(2,1)S(1)} collective-permute-done((bf16[64,1024]{1,0:T(8,128)(2,1)S(1)}, bf16[64,1024]{1,0:T(8,128)(2,1)S(1)}, u32[]{:S(2)}, u32[]{:S(2)}) %collective-permute-start.8) | collective-permute-done | bytes 131104 | tf_op jit(solution)/shard_map/ppermute | solution.py:26
  27.4 0.9 %collective-permute-done.9 = bf16[64,1024]{1,0:T(8,128)(2,1)S(1)} collective-permute-done((bf16[64,1024]{1,0:T(8,128)(2,1)S(1)}, bf16[64,1024]{1,0:T(8,128)(2,1)S(1)}, u32[]{:S(2)}, u32[]{:S(2)}) %collective-permute-start.9) | collective-permute-done | bytes 131104 | tf_op jit(solution)/shard_map/ppermute | solution.py:26
  28.4 3.5 %shard_map.37 = f32[64,1024]{1,0:T(8,128)S(1)} custom-call(bf16[64,1024]{1,0:T(8,128)(2,1)S(1)} %fusion.17.down, bf16[1024,1024]{1,0:T(8,128)(2,1)S(1)} %bitcast.42, bf16[1024,1024]{1,0:T(8,128)(2,1)} %collective-permute-done.3.other_t, bf16[1024,1024]{1,0:T(8,128)(2,1)} %bitcast.1.refl, bf16[1024,1024]{1,0:T(8,128)(2,1)} %collective-permute-done.10.other_r), custom_call_target="tpu_custom_call" | custom-call | flops 536870912 | bytes 6291456 | tf_op jit(solution)/shard_map/pallas_call | solution.py:92
  31.9 0.9 collective-permute-start.11
  32.8 1.0 %collective-permute-done.11 = bf16[64,1024]{1,0:T(8,128)(2,1)S(1)} collective-permute-done((bf16[64,1024]{1,0:T(8,128)(2,1)S(1)}, bf16[64,1024]{1,0:T(8,128)(2,1)S(1)}, u32[]{:S(2)}, u32[]{:S(2)}) %collective-permute-start.11) | collective-permute-done | bytes 131104 | tf_op jit(solution)/shard_map/ppermute | solution.py:26
  34.9 1.0 %collective-permute-done.12 = bf16[64,1024]{1,0:T(8,128)(2,1)S(1)} collective-permute-done((bf16[64,1024]{1,0:T(8,128)(2,1)S(1)}, bf16[64,1024]{1,0:T(8,128)(2,1)S(1)}, u32[]{:S(2)}, u32[]{:S(2)}) %collective-permute-start.12) | collective-permute-done | bytes 131104 | tf_op jit(solution)/shard_map/ppermute | solution.py:26
  37.1 1.0 %collective-permute-done.13 = bf16[64,1024]{1,0:T(8,128)(2,1)S(1)} collective-permute-done((bf16[64,1024]{1,0:T(8,128)(2,1)S(1)}, bf16[64,1024]{1,0:T(8,128)(2,1)S(1)}, u32[]{:S(2)}, u32[]{:S(2)}) %collective-permute-start.13) | collective-permute-done | bytes 131104 | tf_op jit(solution)/shard_map/ppermute | solution.py:26
  39.3 1.0 %collective-permute-done.14 = bf16[64,1024]{1,0:T(8,128)(2,1)S(1)} collective-permute-done((bf16[64,1024]{1,0:T(8,128)(2,1)S(1)}, bf16[64,1024]{1,0:T(8,128)(2,1)S(1)}, u32[]{:S(2)}, u32[]{:S(2)}) %collective-permute-start.14) | collective-permute-done | bytes 131104 | tf_op jit(solution)/shard_map/ppermute | solution.py:26
  41.5 1.0 %collective-permute-done.15 = bf16[64,1024]{1,0:T(8,128)(2,1)S(1)} collective-permute-done((bf16[64,1024]{1,0:T(8,128)(2,1)S(1)}, bf16[64,1024]{1,0:T(8,128)(2,1)S(1)}, u32[]{:S(2)}, u32[]{:S(2)}) %collective-permute-start.15) | collective-permute-done | bytes 131104 | tf_op jit(solution)/shard_map/ppermute | solution.py:26
  43.6 1.0 %collective-permute-done.16 = bf16[64,1024]{1,0:T(8,128)(2,1)S(1)} collective-permute-done((bf16[64,1024]{1,0:T(8,128)(2,1)S(1)}, bf16[64,1024]{1,0:T(8,128)(2,1)S(1)}, u32[]{:S(2)}, u32[]{:S(2)}) %collective-permute-start.16) | collective-permute-done | bytes 131104 | tf_op jit(solution)/shard_map/ppermute | solution.py:26
  45.4 38.6 %collective-permute-start.17 = (bf16[64,1024]{1,0:T(8,128)(2,1)S(1)}, bf16[64,1024]{1,0:T(8,128)(2,1)S(1)}, u32[]{:S(2)}, u32[]{:S(2)}) collective-permute-start(bf16[64,1024]{1,0:T(8,128)(2,1)S(1)} %fusion.5), channel_id=1, source_target_pairs={{0,2},{1,3},{2,0},{3,1},{4,5},{5,4},{6,7},{7,6},{8,9},{9,8},{10,11... | collective-permute-start | bytes 393224 | tf_op jit(solution)/shard_map/ppermute | solution.py:26
  83.9 2.9 %collective-permute-done.17 = bf16[64,1024]{1,0:T(8,128)(2,1)S(1)} collective-permute-done((bf16[64,1024]{1,0:T(8,128)(2,1)S(1)}, bf16[64,1024]{1,0:T(8,128)(2,1)S(1)}, u32[]{:S(2)}, u32[]{:S(2)}) %collective-permute-start.17) | collective-permute-done | bytes 131104 | tf_op jit(solution)/shard_map/ppermute | solution.py:26
  86.9 1.4 %fusion.8 = bf16[1,64,1024]{2,1,0:T(8,128)(2,1)} fusion(f32[64,1024]{1,0:T(8,128)S(1)} %shard_map.37, bf16[64,1024]{1,0:T(8,128)(2,1)S(1)} %collective-permute-done.17, bf16[1024,1024]{1,0:T(8,128)(2,1)S(1)} %get-tuple-element.22, bf16[64,1024]{1,0:T(8,128)(2,1)S(1)} %fusion.5, bf16[64,1024]{1,0:T(8,128)(2,1)S(1)} %fusion.4, ...), kind=kOutput, calls=%fused_computation.23 | convolution fusion | flops 134873088 | bytes 3407879 | tf_op jit(solution)/shard_map/dot_general | solution.py:34
  (39 shorter events, 12.8 us)
Async XLA Ops:
  0.0 11.1 %collective-permute-start.3 = (bf16[1024,1024]{1,0:T(8,128)(2,1)}, bf16[1024,1024]{1,0:T(8,128)(2,1)}, u32[]{:S(2)}, u32[]{:S(2)}) collective-permute-start(bf16[1024,1024]{1,0:T(8,128)(2,1)} %bitcast.39), channel_id=1, source_target_pairs={{0,1},{1,0},{2,3},{3,2},{4,5},{5,4},{6,7},{7,6},{8,9},{9,8},{10,11... | collective-permute-start | bytes 6291464 | tf_op jit(solution)/shard_map/ppermute | solution.py:12
  2.5 2.1 %collective-permute-start = (bf16[128,1024]{1,0:T(8,128)(2,1)S(1)}, bf16[128,1024]{1,0:T(8,128)(2,1)S(1)}, u32[]{:S(2)}, u32[]{:S(2)}) collective-permute-start(bf16[128,1024]{1,0:T(8,128)(2,1)S(1)} %convolution_convert_fusion.1), channel_id=1, source_target_pairs={{0,1},{1,0},{2,3},{3,2},{4,5},{5,4},{6,7},{7,6},{8,9},{9,8},{10,11... | collective-permute-start | bytes 786440 | tf_op jit(solution)/shard_map/ppermute | solution.py:12
  6.7 1.4 %collective-permute-start.1 = (bf16[64,1024]{1,0:T(8,128)(2,1)S(1)}, bf16[64,1024]{1,0:T(8,128)(2,1)S(1)}, u32[]{:S(2)}, u32[]{:S(2)}) collective-permute-start(bf16[64,1024]{1,0:T(8,128)(2,1)S(1)} %slice.16), channel_id=1, source_target_pairs={{0,1},{1,0},{2,3},{3,2},{4,5},{5,4},{6,7},{7,6},{8,9},{9,8},{10,11... | collective-permute-start | bytes 393224 | tf_op jit(solution)/shard_map/ppermute | solution.py:12
  8.1 7.5 %collective-permute-start.2 = (bf16[64,1024]{1,0:T(8,128)(2,1)S(1)}, bf16[64,1024]{1,0:T(8,128)(2,1)S(1)}, u32[]{:S(2)}, u32[]{:S(2)}) collective-permute-start(bf16[64,1024]{1,0:T(8,128)(2,1)S(1)} %slice_select_fusion.1), channel_id=1, source_target_pairs={{0,2},{1,3},{2,0},{3,1},{4,5},{5,4},{6,7},{7,6},{8,9},{9,8},{10,11... | collective-permute-start | bytes 393224 | tf_op jit(solution)/shard_map/ppermute | solution.py:26
  16.1 1.4 %collective-permute-start.4 = (bf16[64,1024]{1,0:T(8,128)(2,1)S(1)}, bf16[64,1024]{1,0:T(8,128)(2,1)S(1)}, u32[]{:S(2)}, u32[]{:S(2)}) collective-permute-start(bf16[64,1024]{1,0:T(8,128)(2,1)S(1)} %convolution_convert_fusion.7), channel_id=1, source_target_pairs={{0,1},{1,0},{2,4},{3,5},{4,2},{5,3},{6,7},{7,6},{8,9},{9,8},{10,11... | collective-permute-start | bytes 393224 | tf_op jit(solution)/shard_map/ppermute | solution.py:26
  18.0 1.4 %collective-permute-start.5 = (bf16[64,1024]{1,0:T(8,128)(2,1)S(1)}, bf16[64,1024]{1,0:T(8,128)(2,1)S(1)}, u32[]{:S(2)}, u32[]{:S(2)}) collective-permute-start(bf16[64,1024]{1,0:T(8,128)(2,1)S(1)} %convolution_convert_fusion.6), channel_id=1, source_target_pairs={{0,1},{1,0},{2,3},{3,2},{4,6},{5,7},{6,4},{7,5},{8,9},{9,8},{10,11... | collective-permute-start | bytes 393224 | tf_op jit(solution)/shard_map/ppermute | solution.py:26
  18.2 10.2 %collective-permute-start.10 = (bf16[1024,1024]{1,0:T(8,128)(2,1)}, bf16[1024,1024]{1,0:T(8,128)(2,1)}, u32[]{:S(2)}, u32[]{:S(2)}) collective-permute-start(bf16[1024,1024]{1,0:T(8,128)(2,1)} %bitcast.1.refl), channel_id=1, source_target_pairs={{0,1},{1,0},{2,3},{3,2},{4,5},{5,4},{6,7},{7,6},{8,9},{9,8},{10,11... | collective-permute-start | bytes 6291464 | tf_op jit(solution)/shard_map/ppermute | solution.py:12
  19.9 2.7 %collective-permute-start.6 = (bf16[64,1024]{1,0:T(8,128)(2,1)S(1)}, bf16[64,1024]{1,0:T(8,128)(2,1)S(1)}, u32[]{:S(2)}, u32[]{:S(2)}) collective-permute-start(bf16[64,1024]{1,0:T(8,128)(2,1)S(1)} %convolution_convert_fusion.5), channel_id=1, source_target_pairs={{0,1},{1,0},{2,3},{3,2},{4,5},{5,4},{6,8},{7,9},{8,6},{9,7},{10,11... | collective-permute-start | bytes 393224 | tf_op jit(solution)/shard_map/ppermute | solution.py:26
  23.1 4.2 %copy-start.1 = (s32[128]{0:T(128)S(1)}, s32[128]{0:T(128)}, u32[]{:S(2)}) copy-start(s32[128]{0:T(128)} %param.7) | copy-start | bytes 1540
  23.1 1.4 %collective-permute-start.7 = (bf16[64,1024]{1,0:T(8,128)(2,1)S(1)}, bf16[64,1024]{1,0:T(8,128)(2,1)S(1)}, u32[]{:S(2)}, u32[]{:S(2)}) collective-permute-start(bf16[64,1024]{1,0:T(8,128)(2,1)S(1)} %convolution_convert_fusion.4), channel_id=1, source_target_pairs={{0,1},{1,0},{2,3},{3,2},{4,5},{5,4},{6,7},{7,6},{8,10},{9,11},{10,... | collective-permute-start | bytes 393224 | tf_op jit(solution)/shard_map/ppermute | solution.py:26
  25.0 1.4 %collective-permute-start.8 = (bf16[64,1024]{1,0:T(8,128)(2,1)S(1)}, bf16[64,1024]{1,0:T(8,128)(2,1)S(1)}, u32[]{:S(2)}, u32[]{:S(2)}) collective-permute-start(bf16[64,1024]{1,0:T(8,128)(2,1)S(1)} %convolution_convert_fusion.3), channel_id=1, source_target_pairs={{0,1},{1,0},{2,3},{3,2},{4,5},{5,4},{6,7},{7,6},{8,9},{9,8},{10,12... | collective-permute-start | bytes 393224 | tf_op jit(solution)/shard_map/ppermute | solution.py:26
  25.4 3.0 %copy-start = (bf16[1,1024,1024]{2,1,0:T(8,128)(2,1)S(1)}, bf16[1,1024,1024]{2,1,0:T(8,128)(2,1)}, u32[]{:S(2)}) copy-start(bf16[1,1024,1024]{2,1,0:T(8,128)(2,1)} %param.5) | copy-start | bytes 6291460
  26.9 1.4 %collective-permute-start.9 = (bf16[64,1024]{1,0:T(8,128)(2,1)S(1)}, bf16[64,1024]{1,0:T(8,128)(2,1)S(1)}, u32[]{:S(2)}, u32[]{:S(2)}) collective-permute-start(bf16[64,1024]{1,0:T(8,128)(2,1)S(1)} %convolution_convert_fusion.2), channel_id=1, source_target_pairs={{0,1},{1,0},{2,3},{3,2},{4,5},{5,4},{6,7},{7,6},{8,9},{9,8},{10,11... | collective-permute-start | bytes 393224 | tf_op jit(solution)/shard_map/ppermute | solution.py:26
  31.9 1.8 %collective-permute-start.11 = (bf16[64,1024]{1,0:T(8,128)(2,1)S(1)}, bf16[64,1024]{1,0:T(8,128)(2,1)S(1)}, u32[]{:S(2)}, u32[]{:S(2)}) collective-permute-start(bf16[64,1024]{1,0:T(8,128)(2,1)S(1)} %convert_element_type.70), channel_id=1, source_target_pairs={{0,1},{1,0},{2,3},{3,2},{4,5},{5,4},{6,7},{7,6},{8,9},{9,8},{10,11... | collective-permute-start | bytes 393224 | tf_op jit(solution)/shard_map/ppermute | solution.py:26
  34.5 1.4 %collective-permute-start.12 = (bf16[64,1024]{1,0:T(8,128)(2,1)S(1)}, bf16[64,1024]{1,0:T(8,128)(2,1)S(1)}, u32[]{:S(2)}, u32[]{:S(2)}) collective-permute-start(bf16[64,1024]{1,0:T(8,128)(2,1)S(1)} %fusion), channel_id=1, source_target_pairs={{0,1},{1,0},{2,3},{3,2},{4,5},{5,4},{6,7},{7,6},{8,9},{9,8},{10,12... | collective-permute-start | bytes 393224 | tf_op jit(solution)/shard_map/ppermute | solution.py:26
  36.7 1.4 %collective-permute-start.13 = (bf16[64,1024]{1,0:T(8,128)(2,1)S(1)}, bf16[64,1024]{1,0:T(8,128)(2,1)S(1)}, u32[]{:S(2)}, u32[]{:S(2)}) collective-permute-start(bf16[64,1024]{1,0:T(8,128)(2,1)S(1)} %fusion.1), channel_id=1, source_target_pairs={{0,1},{1,0},{2,3},{3,2},{4,5},{5,4},{6,7},{7,6},{8,10},{9,11},{10,... | collective-permute-start | bytes 393224 | tf_op jit(solution)/shard_map/ppermute | solution.py:26
  38.9 1.4 %collective-permute-start.14 = (bf16[64,1024]{1,0:T(8,128)(2,1)S(1)}, bf16[64,1024]{1,0:T(8,128)(2,1)S(1)}, u32[]{:S(2)}, u32[]{:S(2)}) collective-permute-start(bf16[64,1024]{1,0:T(8,128)(2,1)S(1)} %fusion.2), channel_id=1, source_target_pairs={{0,1},{1,0},{2,3},{3,2},{4,5},{5,4},{6,8},{7,9},{8,6},{9,7},{10,11... | collective-permute-start | bytes 393224 | tf_op jit(solution)/shard_map/ppermute | solution.py:26
  41.0 1.4 %collective-permute-start.15 = (bf16[64,1024]{1,0:T(8,128)(2,1)S(1)}, bf16[64,1024]{1,0:T(8,128)(2,1)S(1)}, u32[]{:S(2)}, u32[]{:S(2)}) collective-permute-start(bf16[64,1024]{1,0:T(8,128)(2,1)S(1)} %fusion.3), channel_id=1, source_target_pairs={{0,1},{1,0},{2,3},{3,2},{4,6},{5,7},{6,4},{7,5},{8,9},{9,8},{10,11... | collective-permute-start | bytes 393224 | tf_op jit(solution)/shard_map/ppermute | solution.py:26
  43.2 1.4 %collective-permute-start.16 = (bf16[64,1024]{1,0:T(8,128)(2,1)S(1)}, bf16[64,1024]{1,0:T(8,128)(2,1)S(1)}, u32[]{:S(2)}, u32[]{:S(2)}) collective-permute-start(bf16[64,1024]{1,0:T(8,128)(2,1)S(1)} %fusion.4), channel_id=1, source_target_pairs={{0,1},{1,0},{2,4},{3,5},{4,2},{5,3},{6,7},{7,6},{8,9},{9,8},{10,11... | collective-permute-start | bytes 393224 | tf_op jit(solution)/shard_map/ppermute | solution.py:26
  45.4 41.5 %collective-permute-start.17 = (bf16[64,1024]{1,0:T(8,128)(2,1)S(1)}, bf16[64,1024]{1,0:T(8,128)(2,1)S(1)}, u32[]{:S(2)}, u32[]{:S(2)}) collective-permute-start(bf16[64,1024]{1,0:T(8,128)(2,1)S(1)} %fusion.5), channel_id=1, source_target_pairs={{0,2},{1,3},{2,0},{3,1},{4,5},{5,4},{6,7},{7,6},{8,9},{9,8},{10,11... | collective-permute-start | bytes 393224 | tf_op jit(solution)/shard_map/ppermute | solution.py:26

commit v3 on v2

--- a/solution.py
+++ b/solution.py
@@ -6,6 +6,8 @@
 from jax.sharding import PartitionSpec as P
 
 BLOCKS = 4
+KEEP = 1
+VMEM = 52 * 2**20
 
 
 def swap_cores(array):
@@ -95,11 +97,68 @@
         in_specs=[vmem, hbm, hbm, hbm, hbm],
         out_specs=vmem,
         scratch_shapes=[matrix, matrix, matrix, pltpu.SemaphoreType.DMA((3, BLOCKS))],
-        compiler_params=pltpu.CompilerParams(vmem_limit_bytes=52 * 2**20),
+        compiler_params=pltpu.CompilerParams(vmem_limit_bytes=VMEM),
         cost_estimate=pl.CostEstimate(
-            flops=8 * down.shape[0] * size * size, bytes_accessed=6 * size * size, transcendentals=0
+            flops=8 * down.shape[0] * size, bytes_accessed=6 * size, transcendentals=0
         ),
     )(down, trans, other_t, refl, other_r)
+
+
+def refl_kernel(trans, other_t, refl, other_r, out, upper_t, lower_r, upper_r, inner, result, sems, more):
+    odd = lax.rem(lax.axis_index("sec"), 2) == 1
+    rows, half = result.shape
+    fetch(trans, other_t, upper_t, sems.at[0], odd)
+    fetch(other_r, refl, lower_r, sems.at[1], odd)
+    pl.when(jnp.logical_not(odd))(
+        lambda: pltpu.make_async_copy(refl.at[:, pl.ds(0, half)], upper_r, more.at[0]).start()
+    )
+    pl.when(odd)(
+        lambda: pltpu.make_async_copy(other_r.at[:, pl.ds(half, half)], upper_r, more.at[0]).start()
+    )
+    for j in range(BLOCKS):
+        arrived(trans, upper_t, sems.at[0], j)
+    start = pl.multiple_of(lax.rem(lax.axis_index("sec"), 2) * half, half)
+    mine = upper_t[pl.ds(start, half), :]
+    step = rows // BLOCKS
+    for j in range(BLOCKS):
+        arrived(refl, lower_r, sems.at[1], j)
+        at = pl.ds(j * step, step)
+        inner[at, :] = rounded(matmul_nt(lower_r[at, :], mine))
+    pltpu.make_async_copy(refl.at[:, pl.ds(0, half)], upper_r, more.at[0]).wait()
+    for j in range(BLOCKS):
+        at = pl.ds(j * step, step)
+        total = matmul(upper_t[at, :], inner[...])
+        result[at, :] = rounded(upper_r[at, :].astype(jnp.float32) + total)
+        pltpu.make_async_copy(result.at[at, :], out.at[at, :], more.at[1 + j]).start()
+    for j in range(BLOCKS):
+        at = pl.ds(j * step, step)
+        pltpu.make_async_copy(result.at[at, :], out.at[at, :], more.at[1 + j]).wait()
+
+
+def merge_refl(trans, other_t, refl, other_r):
+    size = trans.shape[0]
+    matrix = pltpu.VMEM((size, size), jnp.bfloat16)
+    part = pltpu.VMEM((size, size // 2), jnp.bfloat16)
+    hbm = pl.BlockSpec(memory_space=pltpu.HBM)
+    return pl.pallas_call(
+        refl_kernel,
+        out_shape=jax.ShapeDtypeStruct((size, size // 2), jnp.bfloat16),
+        in_specs=[hbm] * 4,
+        out_specs=hbm,
+        scratch_shapes=[
+            matrix,
+            matrix,
+            part,
+            part,
+            part,
+            pltpu.SemaphoreType.DMA((2, BLOCKS)),
+            pltpu.SemaphoreType.DMA((1 + BLOCKS,)),
+        ],
+        compiler_params=pltpu.CompilerParams(vmem_limit_bytes=VMEM),
+        cost_estimate=pl.CostEstimate(
+            flops=2 * size**3, bytes_accessed=6 * size * size, transcendentals=0
+        ),
+    )(trans, other_t, refl, other_r)
 
 
 def shards(layer_trans, layer_refl, source_modes):
@@ -112,32 +171,66 @@
     refl = layer_refl[0]
     half = source_modes.shape[0] // 2
 
-    columns = jnp.arange(trans.shape[0], dtype=jnp.int32)
-    units = rounded(source_modes[:, None] == columns[None, :])
-    picked = rounded(matmul(units, trans))
-    picked = swap_cores(picked)
-    first = rounded(matmul(picked, trans))
-    first = jnp.where(is_upper, swap_cores(first[:half]), first[half:])
-
     other_t = swap_cores(trans)
     other_r = swap_cores(refl)
-    incoming = swap_sections(first, 0, 1)
-    merged_t = lax.cond(
-        is_upper,
-        lambda: merge_trans(trans, other_t),
-        lambda: merge_trans(other_t, trans),
-    )
-    mine = jnp.where(is_upper, units[:half], units[half:])
-    mine = jnp.where(section == 1, incoming, mine)
-    for step in range(1, sections - 1):
-        incoming = swap_sections(rounded(matmul(incoming, merged_t)), step, step + 1)
-        mine = jnp.where(section == step + 1, incoming, mine)
-
+    my_modes = lax.dynamic_slice_in_dim(source_modes, parity * half, half, 0)
+    columns = jnp.arange(trans.shape[0], dtype=jnp.int32)
+    incoming = rounded(my_modes[:, None] == columns[None, :])
+    mine = incoming
+    last = sections - 1
+    merged_t = lax.switch(
+        jnp.where(section == last, 2, parity),
+        [
+            lambda: merge_trans(trans, other_t),
+            lambda: merge_trans(other_t, trans),
+            lambda: trans,
+        ],
+    )
+    other_r, merged_t = lax.optimization_barrier((other_r, merged_t))
+    refl_half = lax.cond(
+        section == last,
+        lambda: merge_refl(trans, other_t, refl, other_r),
+        lambda: jnp.zeros((trans.shape[0], trans.shape[1] // 2), jnp.bfloat16),
+    )
+    merged_t, refl_half = lax.optimization_barrier((merged_t, refl_half))
+
+    def descend(first_step, stop, incoming):
+        passed = []
+        for step in range(first_step, stop):
+            incoming = swap_sections(rounded(matmul(incoming, merged_t)), step, step + 1)
+            passed.append(incoming)
+        return passed
+
+    next_half = swap_sections(refl_half, last - 1, last)
+    fields = descend(0, KEEP, incoming)
+    fields += lax.cond(
+        source_modes[0] >= 0,
+        lambda: descend(KEEP, last - 2, fields[-1]),
+        lambda: [fields[-1]] * (last - 2 - KEEP),
+    )
+    after, *fields = lax.optimization_barrier((rounded(matmul(fields[-1], merged_t)), *fields))
+    for step, field in enumerate(fields):
+        mine = jnp.where(section == step + 1, field, mine)
     echo = echo_of(mine, trans, other_t, refl, other_r)
-
-    value = rounded(echo)
-    upgoing = value
-    for step in range(sections - 2, -1, -1):
+    incoming = swap_sections(after, last - 2, last - 1)
+    incoming, echo = lax.optimization_barrier((incoming, echo))
+    mine = jnp.where(section == last - 1, incoming, mine)
+    echo = lax.cond(
+        section == last - 1,
+        lambda: echo_of(mine, trans, other_t, refl, other_r),
+        lambda: echo,
+    )
+    below = rounded(matmul(mine, merged_t))
+    below = jnp.concatenate([below, swap_cores(below)], 0)
+    echo, next_half = lax.optimization_barrier((echo, next_half))
+    part = rounded(matmul(below, next_half))
+    kept, passed = part[:half], swap_cores(part[half:])
+    up_last = jnp.concatenate(
+        [jnp.where(is_upper, kept, passed), jnp.where(is_upper, passed, kept)], 1
+    )
+    value = rounded(echo + matmul_nt(up_last, merged_t))
+    upgoing = jnp.where(section == last, swap_sections(up_last, last - 1, last), value)
+    for step in range(last - 2, -1, -1):
         incoming = swap_sections(value, step + 1, step)
         value = rounded(echo + matmul_nt(incoming, merged_t))
         upgoing = jnp.where(section == step, value, upgoing)

time: 88.5 us -> 86.1 us (0.973)
  starting transfers between devices: 47.5 us -> 40.3 us
  waiting for transfers between devices: 19.4 us -> 22.2 us
  matrix products: 17.5 us -> 18.7 us
    ppermute x14, starting transfers between devices: 46.2 us -> 38.6 us  [swap_sections(): return lax.ppermute(value, 'sec', pairs)]
    ppermute x4, waiting for transfers between devices: 2.93 us -> 5.57 us  [swap_cores(): lax.ppermute(array, 'sec', [(i, i ^ 1) for i in range(lax.axis_size('sec'...]
    dot_general x9, matrix products: 11.5 us -> 12.7 us  [matmul(): return jnp.dot(left, right, preferred_element_type=jnp.float32)]
  transfers between devices with their start and end apart: 18 -> 18, of which waited for: 15 -> 14; matrix products, arithmetic and copies ran while one was open for 12% -> 15% of each run, Pallas kernels for 0% -> 4%
where the time goes in v3:
time: 86.1 us; the launch traced here: 85.9 us
  starting transfers between devices  40.3 us (47%)
  waiting for transfers between devices  22.2 us (26%)
  matrix products  18.7 us (22%)
  Pallas kernels  3.27 us (4%)
    ppermute x14, starting transfers between devices, swap_sections(): return lax.ppermute(value, 'sec', pairs)  38.6 us
    ppermute x14, waiting for transfers between devices, swap_sections(): return lax.ppermute(value, 'sec', pairs)  16.7 us
    dot_general x9, matrix products, matmul(): return jnp.dot(left, right, preferred_element_type=jnp.float32)  12.7 us
    dot_general x7, matrix products, matmul_nt(): lax.dot_general(left, right, (((1,), (1,)), ((), ())), preferred_element_...  5.99 us
    ppermute x4, waiting for transfers between devices, swap_cores(): lax.ppermute(array, 'sec', [(i, i ^ 1) for i in range(lax.axis_size('sec'...  5.57 us
    pallas_call x1, Pallas kernels, echo_of(): pl.pallas_call(echo_kernel, out_shape=jax.ShapeDtypeStruct(down.shape, jn...  3.27 us
    ppermute x4, starting transfers between devices, swap_cores(): lax.ppermute(array, 'sec', [(i, i ^ 1) for i in range(lax.axis_size('sec'...  1.77 us
  transfers between devices with their start and end apart: 18, of which 14 were waited for; matrix products, arithmetic and copies ran while one was open for 15% of the time, Pallas kernels for 4%

profile of v3, /device:TPU:0, one launch (start us, length us, event | category | flops | bytes accessed | tf_op | source)
XLA Modules:
  0.0 85.9 jit_solution(17842263331304545505)
XLA Ops:
  1.2 3.3 %collective-permute-done.5.other_t = bf16[1024,1024]{1,0:T(8,128)(2,1)} collective-permute-done((bf16[1024,1024]{1,0:T(8,128)(2,1)}, bf16[1024,1024]{1,0:T(8,128)(2,1)}, u32[]{:S(2)}, u32[]{:S(2)}) %collective-permute-start.5) | collective-permute-done | bytes 2097184 | tf_op jit(solution)/shard_map/ppermute | solution.py:14
  4.6 4.6 %conditional.4 = (bf16[1024,1024]{1,0:T(8,128)(2,1)S(1)}) conditional(s32[]{:T(128)} %clamp.3, (bf16[1024,1024]{1,0:T(8,128)(2,1)}, bf16[1024,1024]{1,0:T(8,128)(2,1)}) %tuple.61, (bf16[1024,1024]{1,0:T(8,128)(2,1)}, bf16[1024,1024]{1,0:T(8,128)(2,1)}) %tuple.62, bf16[1024,1024]{1,0:T(8,128)(2,1)} %bitcast.38), branch_computations={%region_0.1_spmd, %region_1.2_spmd, %region_2.3_spmd} | conditional | flops 2148532224 | bytes 6291464 | solution.py:181
  4.6 4.5 %convolution_convert_fusion = bf16[1024,1024]{1,0:T(8,128)(2,1)S(1)} fusion(bf16[1024,1024]{1,0:T(8,128)(2,1)} %get-tuple-element.48, bf16[1024,1024]{1,0:T(8,128)(2,1)} %get-tuple-element.49), kind=kOutput, calls=%fused_computation | convolution fusion | flops 2148532224 | bytes 6291456 | tf_op jit(solution)/shard_map/cond/branch_0_fun/dot_general | solution.py:32
  9.8 3.0 %collective-permute-start.6 = (bf16[64,1024]{1,0:T(8,128)(2,1)S(1)}, bf16[64,1024]{1,0:T(8,128)(2,1)S(1)}, u32[]{:S(2)}, u32[]{:S(2)}) collective-permute-start(bf16[64,1024]{1,0:T(8,128)(2,1)S(1)} %convolution_convert_fusion.9), channel_id=1, source_target_pairs={{0,2},{1,3},{2,0},{3,1},{4,5},{5,4},{6,7},{7,6},{8,9},{9,8},{10,11... | collective-permute-start | bytes 393224 | tf_op jit(solution)/shard_map/ppermute | solution.py:28
  12.9 3.7 %collective-permute-done.6 = bf16[64,1024]{1,0:T(8,128)(2,1)S(1)} collective-permute-done((bf16[64,1024]{1,0:T(8,128)(2,1)S(1)}, bf16[64,1024]{1,0:T(8,128)(2,1)S(1)}, u32[]{:S(2)}, u32[]{:S(2)}) %collective-permute-start.6) | collective-permute-done | bytes 131104 | tf_op jit(solution)/shard_map/ppermute | solution.py:28
  16.6 9.8 %conditional.6 = (bf16[64,1024]{1,0:T(8,128)(2,1)S(1)}, bf16[64,1024]{1,0:T(8,128)(2,1)}, bf16[64,1024]{1,0:T(8,128)(2,1)}, bf16[64,1024]{1,0:T(8,128)(2,1)}) conditional(s32[]{:T(128)} %bitcast, bf16[64,1024]{1,0:T(8,128)(2,1)S(1)} %collective-permute-done.6, (bf16[64,1024]{1,0:T(8,128)(2,1)S(1)}, bf16[1024,1024]{1,0:T(8,128)(2,1)S(1)}) %tuple.45), branch_computations={%region_5.6_spmd, %region_6.7_spmd} | conditional | flops 537133056 | bytes 12583160 | solution.py:206
  17.1 1.3 %collective-permute-done = bf16[64,1024]{1,0:T(8,128)(2,1)S(1)} collective-permute-done((bf16[64,1024]{1,0:T(8,128)(2,1)S(1)}, bf16[64,1024]{1,0:T(8,128)(2,1)S(1)}, u32[]{:S(2)}, u32[]{:S(2)}) %collective-permute-start) | collective-permute-done | bytes 131104 | tf_op jit(solution)/shard_map/cond/branch_1_fun/ppermute | solution.py:28
  19.2 1.3 %collective-permute-done.1 = bf16[64,1024]{1,0:T(8,128)(2,1)} collective-permute-done((bf16[64,1024]{1,0:T(8,128)(2,1)S(1)}, bf16[64,1024]{1,0:T(8,128)(2,1)}, u32[]{:S(2)}, u32[]{:S(2)}) %collective-permute-start.1) | collective-permute-done | bytes 131104 | tf_op jit(solution)/shard_map/cond/branch_1_fun/ppermute | solution.py:28
  20.5 1.4 %convolution_convert_fusion.3 = bf16[64,1024]{1,0:T(8,128)(2,1)S(1)} fusion(bf16[64,1024]{1,0:T(8,128)(2,1)} %collective-permute-done.1, bf16[1024,1024]{1,0:T(8,128)(2,1)S(1)} %get-tuple-element.57), kind=kOutput, calls=%fused_computation.3 | convolution fusion | flops 134283264 | bytes 2359296 | tf_op jit(solution)/shard_map/cond/branch_1_fun/dot_general | solution.py:32
  22.1 1.3 %collective-permute-done.2 = bf16[64,1024]{1,0:T(8,128)(2,1)} collective-permute-done((bf16[64,1024]{1,0:T(8,128)(2,1)S(1)}, bf16[64,1024]{1,0:T(8,128)(2,1)}, u32[]{:S(2)}, u32[]{:S(2)}) %collective-permute-start.2) | collective-permute-done | bytes 131104 | tf_op jit(solution)/shard_map/cond/branch_1_fun/ppermute | solution.py:28
  23.4 1.4 %convolution_convert_fusion.2 = bf16[64,1024]{1,0:T(8,128)(2,1)S(1)} fusion(bf16[64,1024]{1,0:T(8,128)(2,1)} %collective-permute-done.2, bf16[1024,1024]{1,0:T(8,128)(2,1)S(1)} %get-tuple-element.57), kind=kOutput, calls=%fused_computation.2 | convolution fusion | flops 134283264 | bytes 2359296 | tf_op jit(solution)/shard_map/cond/branch_1_fun/dot_general | solution.py:32
  25.0 1.3 %collective-permute-done.3 = bf16[64,1024]{1,0:T(8,128)(2,1)} collective-permute-done((bf16[64,1024]{1,0:T(8,128)(2,1)S(1)}, bf16[64,1024]{1,0:T(8,128)(2,1)}, u32[]{:S(2)}, u32[]{:S(2)}) %collective-permute-start.3) | collective-permute-done | bytes 131104 | tf_op jit(solution)/shard_map/cond/branch_1_fun/ppermute | solution.py:28
  26.4 1.5 %convolution_convert_fusion.8 = bf16[64,1024]{1,0:T(8,128)(2,1)S(1)} fusion(bf16[64,1024]{1,0:T(8,128)(2,1)} %get-tuple-element.89, bf16[1024,1024]{1,0:T(8,128)(2,1)S(1)} %get-tuple-element.109), kind=kOutput, calls=%fused_computation.22 | convolution fusion | flops 134283264 | bytes 2359296 | tf_op jit(solution)/shard_map/dot_general | solution.py:32
  28.4 3.3 %shard_map.37 = f32[64,1024]{1,0:T(8,128)S(1)} custom-call(bf16[64,1024]{1,0:T(8,128)(2,1)S(1)} %fusion.17.down, bf16[1024,1024]{1,0:T(8,128)(2,1)S(1)} %bitcast.43, bf16[1024,1024]{1,0:T(8,128)(2,1)} %collective-permute-done.5.other_t, bf16[1024,1024]{1,0:T(8,128)(2,1)} %bitcast.46, bf16[1024,1024]{1,0:T(8,128)(2,1)} %collective-permute-done.4.other_r), custom_call_target="tpu_custom_call" | custom-call | flops 524288 | bytes 6144 | tf_op jit(solution)/shard_map/pallas_call | solution.py:94
  31.7 1.1 %convolution_convert_fusion.7 = bf16[64,1024]{1,0:T(8,128)(2,1)} fusion(bf16[64,1024]{1,0:T(8,128)(2,1)S(1)} %broadcast_select_fusion, bf16[1024,1024]{1,0:T(8,128)(2,1)S(1)} %get-tuple-element.109), kind=kOutput, calls=%fused_computation.21 | convolution fusion | flops 134283264 | bytes 2359296 | tf_op jit(solution)/shard_map/dot_general | solution.py:32
  33.7 1.3 %collective-permute-done.9 = bf16[64,1024]{1,0:T(8,128)(2,1)} collective-permute-done((bf16[64,1024]{1,0:T(8,128)(2,1)}, bf16[64,1024]{1,0:T(8,128)(2,1)}, u32[]{:S(2)}, u32[]{:S(2)}) %collective-permute-start.9) | collective-permute-done | bytes 131104 | tf_op jit(solution)/shard_map/ppermute | solution.py:14
  35.0 1.3 %convolution_convert_fusion.6 = bf16[128,512]{1,0:T(8,128)(2,1)S(1)} fusion(bf16[1024,512]{1,0:T(8,128)(2,1)S(1)} %collective-permute-done.8, bf16[64,1024]{1,0:T(8,128)(2,1)} %collective-permute-done.9, bf16[64,1024]{1,0:T(8,128)(2,1)} %convolution_convert_fusion.7), kind=kOutput, calls=%fused_computation.20 | convolution fusion | flops 134807552 | bytes 1441792 | tf_op jit(solution)/shard_map/dot_general | solution.py:32
  38.8 1.0 %collective-permute-done.11 = bf16[64,1024]{1,0:T(8,128)(2,1)S(1)} collective-permute-done((bf16[64,1024]{1,0:T(8,128)(2,1)S(1)}, bf16[64,1024]{1,0:T(8,128)(2,1)S(1)}, u32[]{:S(2)}, u32[]{:S(2)}) %collective-permute-start.11) | collective-permute-done | bytes 131104 | tf_op jit(solution)/shard_map/ppermute | solution.py:28
  41.0 1.0 %collective-permute-done.12 = bf16[64,1024]{1,0:T(8,128)(2,1)S(1)} collective-permute-done((bf16[64,1024]{1,0:T(8,128)(2,1)S(1)}, bf16[64,1024]{1,0:T(8,128)(2,1)S(1)}, u32[]{:S(2)}, u32[]{:S(2)}) %collective-permute-start.12) | collective-permute-done | bytes 131104 | tf_op jit(solution)/shard_map/ppermute | solution.py:28
  43.1 1.0 %collective-permute-done.13 = bf16[64,1024]{1,0:T(8,128)(2,1)S(1)} collective-permute-done((bf16[64,1024]{1,0:T(8,128)(2,1)S(1)}, bf16[64,1024]{1,0:T(8,128)(2,1)S(1)}, u32[]{:S(2)}, u32[]{:S(2)}) %collective-permute-start.13) | collective-permute-done | bytes 131104 | tf_op jit(solution)/shard_map/ppermute | solution.py:28
  45.3 1.0 %collective-permute-done.14 = bf16[64,1024]{1,0:T(8,128)(2,1)S(1)} collective-permute-done((bf16[64,1024]{1,0:T(8,128)(2,1)S(1)}, bf16[64,1024]{1,0:T(8,128)(2,1)S(1)}, u32[]{:S(2)}, u32[]{:S(2)}) %collective-permute-start.14) | collective-permute-done | bytes 131104 | tf_op jit(solution)/shard_map/ppermute | solution.py:28
  49.2 32.3 %collective-permute-start.16 = (bf16[64,1024]{1,0:T(8,128)(2,1)S(1)}, bf16[64,1024]{1,0:T(8,128)(2,1)S(1)}, u32[]{:S(2)}, u32[]{:S(2)}) collective-permute-start(bf16[64,1024]{1,0:T(8,128)(2,1)S(1)} %fusion.5), channel_id=1, source_target_pairs={{0,2},{1,3},{2,0},{3,1},{4,5},{5,4},{6,7},{7,6},{8,9},{9,8},{10,11... | collective-permute-start | bytes 393224 | tf_op jit(solution)/shard_map/ppermute | solution.py:28
  81.6 2.9 %collective-permute-done.16 = bf16[64,1024]{1,0:T(8,128)(2,1)S(1)} collective-permute-done((bf16[64,1024]{1,0:T(8,128)(2,1)S(1)}, bf16[64,1024]{1,0:T(8,128)(2,1)S(1)}, u32[]{:S(2)}, u32[]{:S(2)}) %collective-permute-start.16) | collective-permute-done | bytes 131104 | tf_op jit(solution)/shard_map/ppermute | solution.py:28
  84.5 1.4 %fusion.8 = bf16[1,64,1024]{2,1,0:T(8,128)(2,1)} fusion(f32[64,1024]{1,0:T(8,128)S(1)} %get-tuple-element.111, bf16[64,1024]{1,0:T(8,128)(2,1)S(1)} %collective-permute-done.16, bf16[1024,1024]{1,0:T(8,128)(2,1)S(1)} %get-tuple-element.109, bf16[64,1024]{1,0:T(8,128)(2,1)S(1)} %fusion.5, bf16[64,1024]{1,0:T(8,128)(2,1)S(1)} %fusion.4, ...), kind=kOutput, calls=%fused_computation.25 | convolution fusion | flops 134807552 | bytes 3538951 | tf_op jit(solution)/shard_map/dot_general | solution.py:36
  (50 shorter events, 13.9 us)
Async XLA Ops:
  0.0 4.6 %collective-permute-start.5 = (bf16[1024,1024]{1,0:T(8,128)(2,1)}, bf16[1024,1024]{1,0:T(8,128)(2,1)}, u32[]{:S(2)}, u32[]{:S(2)}) collective-permute-start(bf16[1024,1024]{1,0:T(8,128)(2,1)} %bitcast.37), channel_id=1, source_target_pairs={{0,1},{1,0},{2,3},{3,2},{4,5},{5,4},{6,7},{7,6},{8,9},{9,8},{10,11... | collective-permute-start | bytes 6291464 | tf_op jit(solution)/shard_map/ppermute | solution.py:14
  0.5 8.7 %collective-permute-start.4 = (bf16[1024,1024]{1,0:T(8,128)(2,1)}, bf16[1024,1024]{1,0:T(8,128)(2,1)}, u32[]{:S(2)}, u32[]{:S(2)}) collective-permute-start(bf16[1024,1024]{1,0:T(8,128)(2,1)} %bitcast.44), channel_id=1, source_target_pairs={{0,1},{1,0},{2,3},{3,2},{4,5},{5,4},{6,7},{7,6},{8,9},{9,8},{10,11... | collective-permute-start | bytes 6291464 | tf_op jit(solution)/shard_map/ppermute | solution.py:14
  9.3 3.6 %copy-start.3 = (bf16[1024,512]{1,0:T(8,128)(2,1)}, bf16[1024,512]{1,0:T(8,128)(2,1)S(1)}, u32[]{:S(2)}) copy-start(bf16[1024,512]{1,0:T(8,128)(2,1)S(1)} %get-tuple-element.110) | copy-start | bytes 3145732
  9.3 3.5 %copy-start.4 = (s32[128]{0:T(128)S(1)}, s32[128]{0:T(128)}, u32[]{:S(2)}) copy-start(s32[128]{0:T(128)} %param.14) | copy-start | bytes 1540
  9.8 6.8 %collective-permute-start.6 = (bf16[64,1024]{1,0:T(8,128)(2,1)S(1)}, bf16[64,1024]{1,0:T(8,128)(2,1)S(1)}, u32[]{:S(2)}, u32[]{:S(2)}) collective-permute-start(bf16[64,1024]{1,0:T(8,128)(2,1)S(1)} %convolution_convert_fusion.9), channel_id=1, source_target_pairs={{0,2},{1,3},{2,0},{3,1},{4,5},{5,4},{6,7},{7,6},{8,9},{9,8},{10,11... | collective-permute-start | bytes 393224 | tf_op jit(solution)/shard_map/ppermute | solution.py:28
  12.8 20.8 %collective-permute-start.8 = (bf16[1024,512]{1,0:T(8,128)(2,1)}, bf16[1024,512]{1,0:T(8,128)(2,1)S(1)}, u32[]{:S(2)}, u32[]{:S(2)}) collective-permute-start(bf16[1024,512]{1,0:T(8,128)(2,1)} %copy-done.3), channel_id=1, source_target_pairs={{0,1},{1,0},{2,3},{3,2},{4,5},{5,4},{6,7},{7,6},{8,9},{9,8},{10,11... | collective-permute-start | bytes 3145736 | tf_op jit(solution)/shard_map/ppermute | solution.py:28
  17.0 1.4 %collective-permute-start = (bf16[64,1024]{1,0:T(8,128)(2,1)S(1)}, bf16[64,1024]{1,0:T(8,128)(2,1)S(1)}, u32[]{:S(2)}, u32[]{:S(2)}) collective-permute-start(bf16[64,1024]{1,0:T(8,128)(2,1)S(1)} %convolution_convert_fusion.5), channel_id=1, source_target_pairs={{0,1},{1,0},{2,4},{3,5},{4,2},{5,3},{6,7},{7,6},{8,9},{9,8},{10,11... | collective-permute-start | bytes 393224 | tf_op jit(solution)/shard_map/cond/branch_1_fun/ppermute | solution.py:28
  18.5 3.4 %copy-start.1 = (bf16[64,1024]{1,0:T(8,128)(2,1)}, bf16[64,1024]{1,0:T(8,128)(2,1)S(1)}, u32[]{:S(2)}) copy-start(bf16[64,1024]{1,0:T(8,128)(2,1)S(1)} %collective-permute-done) | copy-start | bytes 393220 | tf_op jit(solution)/shard_map/cond
  19.0 1.5 %collective-permute-start.1 = (bf16[64,1024]{1,0:T(8,128)(2,1)S(1)}, bf16[64,1024]{1,0:T(8,128)(2,1)}, u32[]{:S(2)}, u32[]{:S(2)}) collective-permute-start(bf16[64,1024]{1,0:T(8,128)(2,1)S(1)} %convolution_convert_fusion.4), channel_id=1, source_target_pairs={{0,1},{1,0},{2,3},{3,2},{4,6},{5,7},{6,4},{7,5},{8,9},{9,8},{10,11... | collective-permute-start | bytes 393224 | tf_op jit(solution)/shard_map/cond/branch_1_fun/ppermute | solution.py:28
  21.9 1.5 %collective-permute-start.2 = (bf16[64,1024]{1,0:T(8,128)(2,1)S(1)}, bf16[64,1024]{1,0:T(8,128)(2,1)}, u32[]{:S(2)}, u32[]{:S(2)}) collective-permute-start(bf16[64,1024]{1,0:T(8,128)(2,1)S(1)} %convolution_convert_fusion.3), channel_id=1, source_target_pairs={{0,1},{1,0},{2,3},{3,2},{4,5},{5,4},{6,8},{7,9},{8,6},{9,7},{10,11... | collective-permute-start | bytes 393224 | tf_op jit(solution)/shard_map/cond/branch_1_fun/ppermute | solution.py:28
  22.1 4.3 %copy-start.2 = (bf16[64,1024]{1,0:T(8,128)(2,1)S(1)}, bf16[64,1024]{1,0:T(8,128)(2,1)}, u32[]{:S(2)}) copy-start(bf16[64,1024]{1,0:T(8,128)(2,1)} %copy-done.1) | copy-start | bytes 393220 | tf_op jit(solution)/shard_map/cond
  24.8 1.5 %collective-permute-start.3 = (bf16[64,1024]{1,0:T(8,128)(2,1)S(1)}, bf16[64,1024]{1,0:T(8,128)(2,1)}, u32[]{:S(2)}, u32[]{:S(2)}) collective-permute-start(bf16[64,1024]{1,0:T(8,128)(2,1)S(1)} %convolution_convert_fusion.2), channel_id=1, source_target_pairs={{0,1},{1,0},{2,3},{3,2},{4,5},{5,4},{6,7},{7,6},{8,10},{9,11},{10,... | collective-permute-start | bytes 393224 | tf_op jit(solution)/shard_map/cond/branch_1_fun/ppermute | solution.py:28
  26.4 2.0 %copy-start = (bf16[1,1024,1024]{2,1,0:T(8,128)(2,1)S(1)}, bf16[1,1024,1024]{2,1,0:T(8,128)(2,1)}, u32[]{:S(2)}) copy-start(bf16[1,1024,1024]{2,1,0:T(8,128)(2,1)} %param.12) | copy-start | bytes 6291460
  27.9 3.7 %collective-permute-start.7 = (bf16[64,1024]{1,0:T(8,128)(2,1)S(1)}, bf16[64,1024]{1,0:T(8,128)(2,1)S(1)}, u32[]{:S(2)}, u32[]{:S(2)}) collective-permute-start(bf16[64,1024]{1,0:T(8,128)(2,1)S(1)} %convolution_convert_fusion.8), channel_id=1, source_target_pairs={{0,1},{1,0},{2,3},{3,2},{4,5},{5,4},{6,7},{7,6},{8,9},{9,8},{10,12... | collective-permute-start | bytes 393224 | tf_op jit(solution)/shard_map/ppermute | solution.py:28
  32.8 2.2 %collective-permute-start.9 = (bf16[64,1024]{1,0:T(8,128)(2,1)}, bf16[64,1024]{1,0:T(8,128)(2,1)}, u32[]{:S(2)}, u32[]{:S(2)}) collective-permute-start(bf16[64,1024]{1,0:T(8,128)(2,1)} %convolution_convert_fusion.7), channel_id=1, source_target_pairs={{0,1},{1,0},{2,3},{3,2},{4,5},{5,4},{6,7},{7,6},{8,9},{9,8},{10,11... | collective-permute-start | bytes 393224 | tf_op jit(solution)/shard_map/ppermute | solution.py:14
  36.3 1.3 %collective-permute-start.10 = (bf16[64,512]{1,0:T(8,128)(2,1)S(1)}, bf16[64,512]{1,0:T(8,128)(2,1)S(1)}, u32[]{:S(2)}, u32[]{:S(2)}) collective-permute-start(bf16[64,512]{1,0:T(8,128)(2,1)S(1)} %slice.13), channel_id=1, source_target_pairs={{0,1},{1,0},{2,3},{3,2},{4,5},{5,4},{6,7},{7,6},{8,9},{9,8},{10,11... | collective-permute-start | bytes 196616 | tf_op jit(solution)/shard_map/ppermute | solution.py:14
  38.4 1.4 %collective-permute-start.11 = (bf16[64,1024]{1,0:T(8,128)(2,1)S(1)}, bf16[64,1024]{1,0:T(8,128)(2,1)S(1)}, u32[]{:S(2)}, u32[]{:S(2)}) collective-permute-start(bf16[64,1024]{1,0:T(8,128)(2,1)S(1)} %fusion), channel_id=1, source_target_pairs={{0,1},{1,0},{2,3},{3,2},{4,5},{5,4},{6,7},{7,6},{8,9},{9,8},{10,12... | collective-permute-start | bytes 393224 | tf_op jit(solution)/shard_map/ppermute | solution.py:28
  40.6 1.4 %collective-permute-start.12 = (bf16[64,1024]{1,0:T(8,128)(2,1)S(1)}, bf16[64,1024]{1,0:T(8,128)(2,1)S(1)}, u32[]{:S(2)}, u32[]{:S(2)}) collective-permute-start(bf16[64,1024]{1,0:T(8,128)(2,1)S(1)} %fusion.1), channel_id=1, source_target_pairs={{0,1},{1,0},{2,3},{3,2},{4,5},{5,4},{6,7},{7,6},{8,10},{9,11},{10,... | collective-permute-start | bytes 393224 | tf_op jit(solution)/shard_map/ppermute | solution.py:28
  42.7 1.4 %collective-permute-start.13 = (bf16[64,1024]{1,0:T(8,128)(2,1)S(1)}, bf16[64,1024]{1,0:T(8,128)(2,1)S(1)}, u32[]{:S(2)}, u32[]{:S(2)}) collective-permute-start(bf16[64,1024]{1,0:T(8,128)(2,1)S(1)} %fusion.2), channel_id=1, source_target_pairs={{0,1},{1,0},{2,3},{3,2},{4,5},{5,4},{6,8},{7,9},{8,6},{9,7},{10,11... | collective-permute-start | bytes 393224 | tf_op jit(solution)/shard_map/ppermute | solution.py:28
  44.9 1.4 %collective-permute-start.14 = (bf16[64,1024]{1,0:T(8,128)(2,1)S(1)}, bf16[64,1024]{1,0:T(8,128)(2,1)S(1)}, u32[]{:S(2)}, u32[]{:S(2)}) collective-permute-start(bf16[64,1024]{1,0:T(8,128)(2,1)S(1)} %fusion.3), channel_id=1, source_target_pairs={{0,1},{1,0},{2,3},{3,2},{4,6},{5,7},{6,4},{7,5},{8,9},{9,8},{10,11... | collective-permute-start | bytes 393224 | tf_op jit(solution)/shard_map/ppermute | solution.py:28
  47.1 1.4 %collective-permute-start.15 = (bf16[64,1024]{1,0:T(8,128)(2,1)S(1)}, bf16[64,1024]{1,0:T(8,128)(2,1)S(1)}, u32[]{:S(2)}, u32[]{:S(2)}) collective-permute-start(bf16[64,1024]{1,0:T(8,128)(2,1)S(1)} %fusion.4), channel_id=1, source_target_pairs={{0,1},{1,0},{2,4},{3,5},{4,2},{5,3},{6,7},{7,6},{8,9},{9,8},{10,11... | collective-permute-start | bytes 393224 | tf_op jit(solution)/shard_map/ppermute | solution.py:28
  47.5 34.1 %collective-permute-start.17 = (bf16[64,1024]{1,0:T(8,128)(2,1)S(1)}, bf16[64,1024]{1,0:T(8,128)(2,1)S(1)}, u32[]{:S(2)}, u32[]{:S(2)}) collective-permute-start(bf16[64,1024]{1,0:T(8,128)(2,1)S(1)} %pad_maximum_fusion), channel_id=1, source_target_pairs={{0,1},{1,0},{2,3},{3,2},{4,5},{5,4},{6,7},{7,6},{8,9},{9,8},{10,11... | collective-permute-start | bytes 393224 | tf_op jit(solution)/shard_map/ppermute | solution.py:28
  49.2 35.3 %collective-permute-start.16 = (bf16[64,1024]{1,0:T(8,128)(2,1)S(1)}, bf16[64,1024]{1,0:T(8,128)(2,1)S(1)}, u32[]{:S(2)}, u32[]{:S(2)}) collective-permute-start(bf16[64,1024]{1,0:T(8,128)(2,1)S(1)} %fusion.5), channel_id=1, source_target_pairs={{0,2},{1,3},{2,0},{3,1},{4,5},{5,4},{6,7},{7,6},{8,9},{9,8},{10,11... | collective-permute-start | bytes 393224 | tf_op jit(solution)/shard_map/ppermute | solution.py:28

commit v4 on v3

--- a/solution.py
+++ b/solution.py
@@ -6,7 +6,7 @@
 from jax.sharding import PartitionSpec as P
 
 BLOCKS = 4
-KEEP = 1
+KEEP = 3
 VMEM = 52 * 2**20
 
 

time: 86.1 us -> 85.1 us (0.988)
  matrix products: 18.7 us -> 17.8 us
    dot_general x9, matrix products: 12.7 us -> 11.8 us  [matmul(): return jnp.dot(left, right, preferred_element_type=jnp.float32)]
  transfers between devices with their start and end apart: 18 -> 18, of which waited for: 14 -> 14; matrix products, arithmetic and copies ran while one was open for 15% -> 13% of each run, Pallas kernels for 4% -> 4%
where the time goes in v4:
time: 85.1 us; the launch traced here: 84.9 us
  starting transfers between devices  40.8 us (48%)
  waiting for transfers between devices  21.7 us (25%)
  matrix products  17.8 us (21%)
  Pallas kernels  3.27 us (4%)
    ppermute x14, starting transfers between devices, swap_sections(): return lax.ppermute(value, 'sec', pairs)  39.1 us
    ppermute x14, waiting for transfers between devices, swap_sections(): return lax.ppermute(value, 'sec', pairs)  16.1 us
    dot_general x9, matrix products, matmul(): return jnp.dot(left, right, preferred_element_type=jnp.float32)  11.8 us
    dot_general x7, matrix products, matmul_nt(): lax.dot_general(left, right, (((1,), (1,)), ((), ())), preferred_element_...  5.99 us
    ppermute x4, waiting for transfers between devices, swap_cores(): lax.ppermute(array, 'sec', [(i, i ^ 1) for i in range(lax.axis_size('sec'...  5.57 us
    pallas_call x1, Pallas kernels, echo_of(): pl.pallas_call(echo_kernel, out_shape=jax.ShapeDtypeStruct(down.shape, jn...  3.27 us
  transfers between devices with their start and end apart: 18, of which 14 were waited for; matrix products, arithmetic and copies ran while one was open for 13% of the time, Pallas kernels for 4%

profile of v4, /device:TPU:0, one launch (start us, length us, event | category | flops | bytes accessed | tf_op | source)
XLA Modules:
  0.0 84.9 jit_solution(12980589969971215035)
XLA Ops:
  1.2 3.3 %collective-permute-done.3.other_t = bf16[1024,1024]{1,0:T(8,128)(2,1)} collective-permute-done((bf16[1024,1024]{1,0:T(8,128)(2,1)}, bf16[1024,1024]{1,0:T(8,128)(2,1)}, u32[]{:S(2)}, u32[]{:S(2)}) %collective-permute-start.3) | collective-permute-done | bytes 2097184 | tf_op jit(solution)/shard_map/ppermute | solution.py:14
  4.6 4.6 %conditional.4 = (bf16[1024,1024]{1,0:T(8,128)(2,1)S(1)}) conditional(s32[]{:T(128)} %clamp.3, (bf16[1024,1024]{1,0:T(8,128)(2,1)}, bf16[1024,1024]{1,0:T(8,128)(2,1)}) %tuple.61, (bf16[1024,1024]{1,0:T(8,128)(2,1)}, bf16[1024,1024]{1,0:T(8,128)(2,1)}) %tuple.62, bf16[1024,1024]{1,0:T(8,128)(2,1)} %bitcast.38), branch_computations={%region_0.1_spmd, %region_1.2_spmd, %region_2.3_spmd} | conditional | flops 2148532224 | bytes 6291464 | solution.py:181
  4.6 4.5 %convolution_convert_fusion = bf16[1024,1024]{1,0:T(8,128)(2,1)S(1)} fusion(bf16[1024,1024]{1,0:T(8,128)(2,1)} %get-tuple-element.48, bf16[1024,1024]{1,0:T(8,128)(2,1)} %get-tuple-element.49), kind=kOutput, calls=%fused_computation | convolution fusion | flops 2148532224 | bytes 6291456 | tf_op jit(solution)/shard_map/cond/branch_0_fun/dot_general | solution.py:32
  9.8 3.0 %collective-permute-start.4 = (bf16[64,1024]{1,0:T(8,128)(2,1)S(1)}, bf16[64,1024]{1,0:T(8,128)(2,1)S(1)}, u32[]{:S(2)}, u32[]{:S(2)}) collective-permute-start(bf16[64,1024]{1,0:T(8,128)(2,1)S(1)} %convolution_convert_fusion.9), channel_id=1, source_target_pairs={{0,2},{1,3},{2,0},{3,1},{4,5},{5,4},{6,7},{7,6},{8,9},{9,8},{10,11... | collective-permute-start | bytes 393224 | tf_op jit(solution)/shard_map/ppermute | solution.py:28
  12.8 3.8 %collective-permute-done.4 = bf16[64,1024]{1,0:T(8,128)(2,1)S(1)} collective-permute-done((bf16[64,1024]{1,0:T(8,128)(2,1)S(1)}, bf16[64,1024]{1,0:T(8,128)(2,1)S(1)}, u32[]{:S(2)}, u32[]{:S(2)}) %collective-permute-start.4) | collective-permute-done | bytes 131104 | tf_op jit(solution)/shard_map/ppermute | solution.py:28
  17.1 1.3 %collective-permute-done.5 = bf16[64,1024]{1,0:T(8,128)(2,1)S(1)} collective-permute-done((bf16[64,1024]{1,0:T(8,128)(2,1)S(1)}, bf16[64,1024]{1,0:T(8,128)(2,1)S(1)}, u32[]{:S(2)}, u32[]{:S(2)}) %collective-permute-start.5) | collective-permute-done | bytes 131104 | tf_op jit(solution)/shard_map/ppermute | solution.py:28
  20.4 5.0 %conditional.6 = (bf16[64,1024]{1,0:T(8,128)(2,1)}, bf16[64,1024]{1,0:T(8,128)(2,1)}) conditional(s32[]{:T(128)} %bitcast, bf16[64,1024]{1,0:T(8,128)(2,1)S(1)} %collective-permute-done.6, (bf16[64,1024]{1,0:T(8,128)(2,1)S(1)}, bf16[1024,1024]{1,0:T(8,128)(2,1)S(1)}) %tuple.45), branch_computations={%region_5.6_spmd, %region_6.7_spmd} | conditional | flops 268566528 | bytes 5767264 | solution.py:206
  21.1 1.3 %collective-permute-done = bf16[64,1024]{1,0:T(8,128)(2,1)} collective-permute-done((bf16[64,1024]{1,0:T(8,128)(2,1)S(1)}, bf16[64,1024]{1,0:T(8,128)(2,1)}, u32[]{:S(2)}, u32[]{:S(2)}) %collective-permute-start) | collective-permute-done | bytes 131104 | tf_op jit(solution)/shard_map/cond/branch_1_fun/ppermute | solution.py:28
  22.4 1.4 %convolution_convert_fusion.2 = bf16[64,1024]{1,0:T(8,128)(2,1)S(1)} fusion(bf16[64,1024]{1,0:T(8,128)(2,1)} %collective-permute-done, bf16[1024,1024]{1,0:T(8,128)(2,1)S(1)} %get-tuple-element.57), kind=kOutput, calls=%fused_computation.2 | convolution fusion | flops 134283264 | bytes 2359296 | tf_op jit(solution)/shard_map/cond/branch_1_fun/dot_general | solution.py:32
  24.1 1.2 %collective-permute-done.1 = bf16[64,1024]{1,0:T(8,128)(2,1)} collective-permute-done((bf16[64,1024]{1,0:T(8,128)(2,1)S(1)}, bf16[64,1024]{1,0:T(8,128)(2,1)}, u32[]{:S(2)}, u32[]{:S(2)}) %collective-permute-start.1) | collective-permute-done | bytes 131104 | tf_op jit(solution)/shard_map/cond/branch_1_fun/ppermute | solution.py:28
  25.4 1.5 %convolution_convert_fusion.6 = bf16[64,1024]{1,0:T(8,128)(2,1)S(1)} fusion(bf16[64,1024]{1,0:T(8,128)(2,1)} %get-tuple-element.85, bf16[1024,1024]{1,0:T(8,128)(2,1)S(1)} %get-tuple-element.101), kind=kOutput, calls=%fused_computation.20 | convolution fusion | flops 134283264 | bytes 2359296 | tf_op jit(solution)/shard_map/dot_general | solution.py:32
  27.4 3.3 %shard_map.37 = f32[64,1024]{1,0:T(8,128)S(1)} custom-call(bf16[64,1024]{1,0:T(8,128)(2,1)S(1)} %fusion.17.down, bf16[1024,1024]{1,0:T(8,128)(2,1)S(1)} %bitcast.43, bf16[1024,1024]{1,0:T(8,128)(2,1)} %collective-permute-done.3.other_t, bf16[1024,1024]{1,0:T(8,128)(2,1)} %bitcast.46, bf16[1024,1024]{1,0:T(8,128)(2,1)} %collective-permute-done.2.other_r), custom_call_target="tpu_custom_call" | custom-call | flops 524288 | bytes 6144 | tf_op jit(solution)/shard_map/pallas_call | solution.py:94
  30.7 1.1 %convolution_convert_fusion.5 = bf16[64,1024]{1,0:T(8,128)(2,1)} fusion(bf16[64,1024]{1,0:T(8,128)(2,1)S(1)} %broadcast_select_fusion, bf16[1024,1024]{1,0:T(8,128)(2,1)S(1)} %get-tuple-element.101), kind=kOutput, calls=%fused_computation.19 | convolution fusion | flops 134283264 | bytes 2359296 | tf_op jit(solution)/shard_map/dot_general | solution.py:32
  32.6 1.3 %collective-permute-done.9 = bf16[64,1024]{1,0:T(8,128)(2,1)} collective-permute-done((bf16[64,1024]{1,0:T(8,128)(2,1)}, bf16[64,1024]{1,0:T(8,128)(2,1)}, u32[]{:S(2)}, u32[]{:S(2)}) %collective-permute-start.9) | collective-permute-done | bytes 131104 | tf_op jit(solution)/shard_map/ppermute | solution.py:14
  34.0 1.3 %convolution_convert_fusion.4 = bf16[128,512]{1,0:T(8,128)(2,1)S(1)} fusion(bf16[1024,512]{1,0:T(8,128)(2,1)S(1)} %collective-permute-done.8, bf16[64,1024]{1,0:T(8,128)(2,1)} %collective-permute-done.9, bf16[64,1024]{1,0:T(8,128)(2,1)} %convolution_convert_fusion.5), kind=kOutput, calls=%fused_computation.18 | convolution fusion | flops 134807552 | bytes 1441792 | tf_op jit(solution)/shard_map/dot_general | solution.py:32
  35.7 0.9 %collective-permute-done.10 = bf16[64,512]{1,0:T(8,128)(2,1)S(1)} collective-permute-done((bf16[64,512]{1,0:T(8,128)(2,1)S(1)}, bf16[64,512]{1,0:T(8,128)(2,1)S(1)}, u32[]{:S(2)}, u32[]{:S(2)}) %collective-permute-start.10) | collective-permute-done | bytes 65568 | tf_op jit(solution)/shard_map/ppermute | solution.py:14
  36.6 0.8 fusion
  37.8 1.0 %collective-permute-done.11 = bf16[64,1024]{1,0:T(8,128)(2,1)S(1)} collective-permute-done((bf16[64,1024]{1,0:T(8,128)(2,1)S(1)}, bf16[64,1024]{1,0:T(8,128)(2,1)S(1)}, u32[]{:S(2)}, u32[]{:S(2)}) %collective-permute-start.11) | collective-permute-done | bytes 131104 | tf_op jit(solution)/shard_map/ppermute | solution.py:28
  40.0 1.0 %collective-permute-done.12 = bf16[64,1024]{1,0:T(8,128)(2,1)S(1)} collective-permute-done((bf16[64,1024]{1,0:T(8,128)(2,1)S(1)}, bf16[64,1024]{1,0:T(8,128)(2,1)S(1)}, u32[]{:S(2)}, u32[]{:S(2)}) %collective-permute-start.12) | collective-permute-done | bytes 131104 | tf_op jit(solution)/shard_map/ppermute | solution.py:28
  42.1 1.0 %collective-permute-done.13 = bf16[64,1024]{1,0:T(8,128)(2,1)S(1)} collective-permute-done((bf16[64,1024]{1,0:T(8,128)(2,1)S(1)}, bf16[64,1024]{1,0:T(8,128)(2,1)S(1)}, u32[]{:S(2)}, u32[]{:S(2)}) %collective-permute-start.13) | collective-permute-done | bytes 131104 | tf_op jit(solution)/shard_map/ppermute | solution.py:28
  44.3 1.0 %collective-permute-done.14 = bf16[64,1024]{1,0:T(8,128)(2,1)S(1)} collective-permute-done((bf16[64,1024]{1,0:T(8,128)(2,1)S(1)}, bf16[64,1024]{1,0:T(8,128)(2,1)S(1)}, u32[]{:S(2)}, u32[]{:S(2)}) %collective-permute-start.14) | collective-permute-done | bytes 131104 | tf_op jit(solution)/shard_map/ppermute | solution.py:28
  48.2 32.3 %collective-permute-start.16 = (bf16[64,1024]{1,0:T(8,128)(2,1)S(1)}, bf16[64,1024]{1,0:T(8,128)(2,1)S(1)}, u32[]{:S(2)}, u32[]{:S(2)}) collective-permute-start(bf16[64,1024]{1,0:T(8,128)(2,1)S(1)} %fusion.5), channel_id=1, source_target_pairs={{0,2},{1,3},{2,0},{3,1},{4,5},{5,4},{6,7},{7,6},{8,9},{9,8},{10,11... | collective-permute-start | bytes 393224 | tf_op jit(solution)/shard_map/ppermute | solution.py:28
  80.6 2.9 %collective-permute-done.16 = bf16[64,1024]{1,0:T(8,128)(2,1)S(1)} collective-permute-done((bf16[64,1024]{1,0:T(8,128)(2,1)S(1)}, bf16[64,1024]{1,0:T(8,128)(2,1)S(1)}, u32[]{:S(2)}, u32[]{:S(2)}) %collective-permute-start.16) | collective-permute-done | bytes 131104 | tf_op jit(solution)/shard_map/ppermute | solution.py:28
  83.5 1.4 %fusion.8 = bf16[1,64,1024]{2,1,0:T(8,128)(2,1)} fusion(f32[64,1024]{1,0:T(8,128)S(1)} %get-tuple-element.103, bf16[64,1024]{1,0:T(8,128)(2,1)S(1)} %collective-permute-done.16, bf16[1024,1024]{1,0:T(8,128)(2,1)S(1)} %get-tuple-element.101, bf16[64,1024]{1,0:T(8,128)(2,1)S(1)} %fusion.5, bf16[64,1024]{1,0:T(8,128)(2,1)S(1)} %fusion.4, ...), kind=kOutput, calls=%fused_computation.25 | convolution fusion | flops 134807552 | bytes 3538951 | tf_op jit(solution)/shard_map/dot_general | solution.py:36
  (50 shorter events, 13.9 us)
Async XLA Ops:
  0.0 4.6 %collective-permute-start.3 = (bf16[1024,1024]{1,0:T(8,128)(2,1)}, bf16[1024,1024]{1,0:T(8,128)(2,1)}, u32[]{:S(2)}, u32[]{:S(2)}) collective-permute-start(bf16[1024,1024]{1,0:T(8,128)(2,1)} %bitcast.37), channel_id=1, source_target_pairs={{0,1},{1,0},{2,3},{3,2},{4,5},{5,4},{6,7},{7,6},{8,9},{9,8},{10,11... | collective-permute-start | bytes 6291464 | tf_op jit(solution)/shard_map/ppermute | solution.py:14
  0.5 8.7 %collective-permute-start.2 = (bf16[1024,1024]{1,0:T(8,128)(2,1)}, bf16[1024,1024]{1,0:T(8,128)(2,1)}, u32[]{:S(2)}, u32[]{:S(2)}) collective-permute-start(bf16[1024,1024]{1,0:T(8,128)(2,1)} %bitcast.44), channel_id=1, source_target_pairs={{0,1},{1,0},{2,3},{3,2},{4,5},{5,4},{6,7},{7,6},{8,9},{9,8},{10,11... | collective-permute-start | bytes 6291464 | tf_op jit(solution)/shard_map/ppermute | solution.py:14
  9.3 7.8 %copy-start.1 = (bf16[1024,512]{1,0:T(8,128)(2,1)}, bf16[1024,512]{1,0:T(8,128)(2,1)S(1)}, u32[]{:S(2)}) copy-start(bf16[1024,512]{1,0:T(8,128)(2,1)S(1)} %get-tuple-element.102) | copy-start | bytes 3145732
  9.8 9.4 %copy-start.4 = (s32[128]{0:T(128)S(1)}, s32[128]{0:T(128)}, u32[]{:S(2)}) copy-start(s32[128]{0:T(128)} %param.14) | copy-start | bytes 1540
  9.8 6.8 %collective-permute-start.4 = (bf16[64,1024]{1,0:T(8,128)(2,1)S(1)}, bf16[64,1024]{1,0:T(8,128)(2,1)S(1)}, u32[]{:S(2)}, u32[]{:S(2)}) collective-permute-start(bf16[64,1024]{1,0:T(8,128)(2,1)S(1)} %convolution_convert_fusion.9), channel_id=1, source_target_pairs={{0,2},{1,3},{2,0},{3,1},{4,5},{5,4},{6,7},{7,6},{8,9},{9,8},{10,11... | collective-permute-start | bytes 393224 | tf_op jit(solution)/shard_map/ppermute | solution.py:28
  17.1 1.4 %collective-permute-start.5 = (bf16[64,1024]{1,0:T(8,128)(2,1)S(1)}, bf16[64,1024]{1,0:T(8,128)(2,1)S(1)}, u32[]{:S(2)}, u32[]{:S(2)}) collective-permute-start(bf16[64,1024]{1,0:T(8,128)(2,1)S(1)} %convolution_convert_fusion.8), channel_id=1, source_target_pairs={{0,1},{1,0},{2,4},{3,5},{4,2},{5,3},{6,7},{7,6},{8,9},{9,8},{10,11... | collective-permute-start | bytes 393224 | tf_op jit(solution)/shard_map/ppermute | solution.py:28
  18.5 0.8 copy-start.2
  19.0 1.4 %collective-permute-start.6 = (bf16[64,1024]{1,0:T(8,128)(2,1)S(1)}, bf16[64,1024]{1,0:T(8,128)(2,1)S(1)}, u32[]{:S(2)}, u32[]{:S(2)}) collective-permute-start(bf16[64,1024]{1,0:T(8,128)(2,1)S(1)} %convolution_convert_fusion.7), channel_id=1, source_target_pairs={{0,1},{1,0},{2,3},{3,2},{4,6},{5,7},{6,4},{7,5},{8,9},{9,8},{10,11... | collective-permute-start | bytes 393224 | tf_op jit(solution)/shard_map/ppermute | solution.py:28
  19.2 13.4 %collective-permute-start.8 = (bf16[1024,512]{1,0:T(8,128)(2,1)}, bf16[1024,512]{1,0:T(8,128)(2,1)S(1)}, u32[]{:S(2)}, u32[]{:S(2)}) collective-permute-start(bf16[1024,512]{1,0:T(8,128)(2,1)} %copy-done.1), channel_id=1, source_target_pairs={{0,1},{1,0},{2,3},{3,2},{4,5},{5,4},{6,7},{7,6},{8,9},{9,8},{10,11... | collective-permute-start | bytes 3145736 | tf_op jit(solution)/shard_map/ppermute | solution.py:28
  20.9 1.5 %collective-permute-start = (bf16[64,1024]{1,0:T(8,128)(2,1)S(1)}, bf16[64,1024]{1,0:T(8,128)(2,1)}, u32[]{:S(2)}, u32[]{:S(2)}) collective-permute-start(bf16[64,1024]{1,0:T(8,128)(2,1)S(1)} %convolution_convert_fusion.3), channel_id=1, source_target_pairs={{0,1},{1,0},{2,3},{3,2},{4,5},{5,4},{6,8},{7,9},{8,6},{9,7},{10,11... | collective-permute-start | bytes 393224 | tf_op jit(solution)/shard_map/cond/branch_1_fun/ppermute | solution.py:28
  23.8 1.5 %collective-permute-start.1 = (bf16[64,1024]{1,0:T(8,128)(2,1)S(1)}, bf16[64,1024]{1,0:T(8,128)(2,1)}, u32[]{:S(2)}, u32[]{:S(2)}) collective-permute-start(bf16[64,1024]{1,0:T(8,128)(2,1)S(1)} %convolution_convert_fusion.2), channel_id=1, source_target_pairs={{0,1},{1,0},{2,3},{3,2},{4,5},{5,4},{6,7},{7,6},{8,10},{9,11},{10,... | collective-permute-start | bytes 393224 | tf_op jit(solution)/shard_map/cond/branch_1_fun/ppermute | solution.py:28
  25.3 1.8 %copy-start.3 = (bf16[64,1024]{1,0:T(8,128)(2,1)S(1)}, bf16[64,1024]{1,0:T(8,128)(2,1)}, u32[]{:S(2)}) copy-start(bf16[64,1024]{1,0:T(8,128)(2,1)} %copy-done.2) | copy-start | bytes 393220
  25.4 2.1 %copy-start = (bf16[1,1024,1024]{2,1,0:T(8,128)(2,1)S(1)}, bf16[1,1024,1024]{2,1,0:T(8,128)(2,1)}, u32[]{:S(2)}) copy-start(bf16[1,1024,1024]{2,1,0:T(8,128)(2,1)} %param.12) | copy-start | bytes 6291460
  26.9 3.8 %collective-permute-start.7 = (bf16[64,1024]{1,0:T(8,128)(2,1)S(1)}, bf16[64,1024]{1,0:T(8,128)(2,1)S(1)}, u32[]{:S(2)}, u32[]{:S(2)}) collective-permute-start(bf16[64,1024]{1,0:T(8,128)(2,1)S(1)} %convolution_convert_fusion.6), channel_id=1, source_target_pairs={{0,1},{1,0},{2,3},{3,2},{4,5},{5,4},{6,7},{7,6},{8,9},{9,8},{10,12... | collective-permute-start | bytes 393224 | tf_op jit(solution)/shard_map/ppermute | solution.py:28
  31.9 2.1 %collective-permute-start.9 = (bf16[64,1024]{1,0:T(8,128)(2,1)}, bf16[64,1024]{1,0:T(8,128)(2,1)}, u32[]{:S(2)}, u32[]{:S(2)}) collective-permute-start(bf16[64,1024]{1,0:T(8,128)(2,1)} %convolution_convert_fusion.5), channel_id=1, source_target_pairs={{0,1},{1,0},{2,3},{3,2},{4,5},{5,4},{6,7},{7,6},{8,9},{9,8},{10,11... | collective-permute-start | bytes 393224 | tf_op jit(solution)/shard_map/ppermute | solution.py:14
  35.3 1.3 %collective-permute-start.10 = (bf16[64,512]{1,0:T(8,128)(2,1)S(1)}, bf16[64,512]{1,0:T(8,128)(2,1)S(1)}, u32[]{:S(2)}, u32[]{:S(2)}) collective-permute-start(bf16[64,512]{1,0:T(8,128)(2,1)S(1)} %slice.13), channel_id=1, source_target_pairs={{0,1},{1,0},{2,3},{3,2},{4,5},{5,4},{6,7},{7,6},{8,9},{9,8},{10,11... | collective-permute-start | bytes 196616 | tf_op jit(solution)/shard_map/ppermute | solution.py:14
  37.4 1.4 %collective-permute-start.11 = (bf16[64,1024]{1,0:T(8,128)(2,1)S(1)}, bf16[64,1024]{1,0:T(8,128)(2,1)S(1)}, u32[]{:S(2)}, u32[]{:S(2)}) collective-permute-start(bf16[64,1024]{1,0:T(8,128)(2,1)S(1)} %fusion), channel_id=1, source_target_pairs={{0,1},{1,0},{2,3},{3,2},{4,5},{5,4},{6,7},{7,6},{8,9},{9,8},{10,12... | collective-permute-start | bytes 393224 | tf_op jit(solution)/shard_map/ppermute | solution.py:28
  39.5 1.4 %collective-permute-start.12 = (bf16[64,1024]{1,0:T(8,128)(2,1)S(1)}, bf16[64,1024]{1,0:T(8,128)(2,1)S(1)}, u32[]{:S(2)}, u32[]{:S(2)}) collective-permute-start(bf16[64,1024]{1,0:T(8,128)(2,1)S(1)} %fusion.1), channel_id=1, source_target_pairs={{0,1},{1,0},{2,3},{3,2},{4,5},{5,4},{6,7},{7,6},{8,10},{9,11},{10,... | collective-permute-start | bytes 393224 | tf_op jit(solution)/shard_map/ppermute | solution.py:28
  41.7 1.4 %collective-permute-start.13 = (bf16[64,1024]{1,0:T(8,128)(2,1)S(1)}, bf16[64,1024]{1,0:T(8,128)(2,1)S(1)}, u32[]{:S(2)}, u32[]{:S(2)}) collective-permute-start(bf16[64,1024]{1,0:T(8,128)(2,1)S(1)} %fusion.2), channel_id=1, source_target_pairs={{0,1},{1,0},{2,3},{3,2},{4,5},{5,4},{6,8},{7,9},{8,6},{9,7},{10,11... | collective-permute-start | bytes 393224 | tf_op jit(solution)/shard_map/ppermute | solution.py:28
  43.9 1.4 %collective-permute-start.14 = (bf16[64,1024]{1,0:T(8,128)(2,1)S(1)}, bf16[64,1024]{1,0:T(8,128)(2,1)S(1)}, u32[]{:S(2)}, u32[]{:S(2)}) collective-permute-start(bf16[64,1024]{1,0:T(8,128)(2,1)S(1)} %fusion.3), channel_id=1, source_target_pairs={{0,1},{1,0},{2,3},{3,2},{4,6},{5,7},{6,4},{7,5},{8,9},{9,8},{10,11... | collective-permute-start | bytes 393224 | tf_op jit(solution)/shard_map/ppermute | solution.py:28
  46.0 1.4 %collective-permute-start.15 = (bf16[64,1024]{1,0:T(8,128)(2,1)S(1)}, bf16[64,1024]{1,0:T(8,128)(2,1)S(1)}, u32[]{:S(2)}, u32[]{:S(2)}) collective-permute-start(bf16[64,1024]{1,0:T(8,128)(2,1)S(1)} %fusion.4), channel_id=1, source_target_pairs={{0,1},{1,0},{2,4},{3,5},{4,2},{5,3},{6,7},{7,6},{8,9},{9,8},{10,11... | collective-permute-start | bytes 393224 | tf_op jit(solution)/shard_map/ppermute | solution.py:28
  46.5 34.1 %collective-permute-start.17 = (bf16[64,1024]{1,0:T(8,128)(2,1)S(1)}, bf16[64,1024]{1,0:T(8,128)(2,1)S(1)}, u32[]{:S(2)}, u32[]{:S(2)}) collective-permute-start(bf16[64,1024]{1,0:T(8,128)(2,1)S(1)} %pad_maximum_fusion), channel_id=1, source_target_pairs={{0,1},{1,0},{2,3},{3,2},{4,5},{5,4},{6,7},{7,6},{8,9},{9,8},{10,11... | collective-permute-start | bytes 393224 | tf_op jit(solution)/shard_map/ppermute | solution.py:28
  48.2 35.3 %collective-permute-start.16 = (bf16[64,1024]{1,0:T(8,128)(2,1)S(1)}, bf16[64,1024]{1,0:T(8,128)(2,1)S(1)}, u32[]{:S(2)}, u32[]{:S(2)}) collective-permute-start(bf16[64,1024]{1,0:T(8,128)(2,1)S(1)} %fusion.5), channel_id=1, source_target_pairs={{0,2},{1,3},{2,0},{3,1},{4,5},{5,4},{6,7},{7,6},{8,9},{9,8},{10,11... | collective-permute-start | bytes 393224 | tf_op jit(solution)/shard_map/ppermute | solution.py:28

commit v5 on v4

--- a/solution.py
+++ b/solution.py
@@ -211,7 +211,11 @@
     after, *fields = lax.optimization_barrier((rounded(matmul(fields[-1], merged_t)), *fields))
     for step, field in enumerate(fields):
         mine = jnp.where(section == step + 1, field, mine)
-    echo = echo_of(mine, trans, other_t, refl, other_r)
+    echo = lax.cond(
+        section == last - 1,
+        lambda: jnp.zeros(mine.shape, jnp.float32),
+        lambda: echo_of(mine, trans, other_t, refl, other_r),
+    )
     incoming = swap_sections(after, last - 2, last - 1)
     incoming, echo = lax.optimization_barrier((incoming, echo))
     mine = jnp.where(section == last - 1, incoming, mine)

time: 85.1 us -> 85.2 us (level)
  local copies, waits for them, and re-layouts: 0.83 us -> 1.81 us
    another operation x1, local copies, waits for them, and re-layouts: 0.07 us -> 1.06 us
  transfers between devices with their start and end apart: 18 -> 18, of which waited for: 14 -> 14; matrix products, arithmetic and copies ran while one was open for 13% -> 12% of each run, Pallas kernels for 4% -> 4%
where the time goes in v5:
time: 85.2 us; the launch traced here: 85 us
  starting transfers between devices  40.6 us (48%)
  waiting for transfers between devices  21.3 us (25%)
  matrix products  17.4 us (20%)
  Pallas kernels  3.27 us (4%)
  local copies, waits for them, and re-layouts  1.81 us (2%)
    ppermute x14, starting transfers between devices, swap_sections(): return lax.ppermute(value, 'sec', pairs)  38.8 us
    ppermute x14, waiting for transfers between devices, swap_sections(): return lax.ppermute(value, 'sec', pairs)  16.1 us
    dot_general x9, matrix products, matmul(): return jnp.dot(left, right, preferred_element_type=jnp.float32)  11.4 us
    dot_general x7, matrix products, matmul_nt(): lax.dot_general(left, right, (((1,), (1,)), ((), ())), preferred_element_...  5.99 us
    ppermute x4, waiting for transfers between devices, swap_cores(): lax.ppermute(array, 'sec', [(i, i ^ 1) for i in range(lax.axis_size('sec'...  5.23 us
    pallas_call x1, Pallas kernels, echo_of(): pl.pallas_call(echo_kernel, out_shape=jax.ShapeDtypeStruct(down.shape, jn...  3.27 us
    ppermute x4, starting transfers between devices, swap_cores(): lax.ppermute(array, 'sec', [(i, i ^ 1) for i in range(lax.axis_size('sec'...  1.76 us
  transfers between devices with their start and end apart: 18, of which 14 were waited for; matrix products, arithmetic and copies ran while one was open for 12% of the time, Pallas kernels for 4%

profile of v5, /device:TPU:0, one launch (start us, length us, event | category | flops | bytes accessed | tf_op | source)
XLA Modules:
  0.0 85.0 jit_solution(2846572619319535952)
XLA Ops:
  1.2 3.3 %collective-permute-done.3 = bf16[1024,1024]{1,0:T(8,128)(2,1)} collective-permute-done((bf16[1024,1024]{1,0:T(8,128)(2,1)}, bf16[1024,1024]{1,0:T(8,128)(2,1)}, u32[]{:S(2)}, u32[]{:S(2)}) %collective-permute-start.3) | collective-permute-done | bytes 2097184 | tf_op jit(solution)/shard_map/ppermute | solution.py:14
  4.6 4.6 %conditional.5 = (bf16[1024,1024]{1,0:T(8,128)(2,1)S(1)}) conditional(s32[]{:T(128)} %clamp.3, (bf16[1024,1024]{1,0:T(8,128)(2,1)}, bf16[1024,1024]{1,0:T(8,128)(2,1)}) %tuple.71, (bf16[1024,1024]{1,0:T(8,128)(2,1)}, bf16[1024,1024]{1,0:T(8,128)(2,1)}) %tuple.72, bf16[1024,1024]{1,0:T(8,128)(2,1)} %bitcast.38), branch_computations={%region_0.1_spmd, %region_1.2_spmd, %region_2.3_spmd} | conditional | flops 2148532224 | bytes 6291464 | solution.py:181
  4.6 4.5 %convolution_convert_fusion = bf16[1024,1024]{1,0:T(8,128)(2,1)S(1)} fusion(bf16[1024,1024]{1,0:T(8,128)(2,1)} %get-tuple-element.60, bf16[1024,1024]{1,0:T(8,128)(2,1)} %get-tuple-element.62), kind=kOutput, calls=%fused_computation | convolution fusion | flops 2148532224 | bytes 6291456 | tf_op jit(solution)/shard_map/cond/branch_0_fun/dot_general | solution.py:32
  9.2 1.1 %conditional.6 = (bf16[1024,512]{1,0:T(8,128)(2,1)}) conditional(s32[]{:T(128)} %convert_element_type.70, () %tuple.48, (bf16[1024,1024]{1,0:T(8,128)(2,1)}, bf16[1024,1024]{1,0:T(8,128)(2,1)}, bf16[1024,1024]{1,0:T(8,128)(2,1)}, bf16[1024,1024]{1,0:T(8,128)(2,1)}) %tuple.76), branch_computations={%region_3.4_spmd, %region_4.5_spmd} | conditional | flops 2147483648 | bytes 6291464 | solution.py:190
  9.2 1.1 %broadcast.7 = bf16[1024,512]{1,0:T(8,128)(2,1)} broadcast(bf16[]{:T(256)} %constant.22.clone), dimensions={} | broadcast | bytes 1048578 | tf_op jit(solution)/shard_map/broadcast.1
  10.8 3.0 %collective-permute-start.4 = (bf16[64,1024]{1,0:T(8,128)(2,1)S(1)}, bf16[64,1024]{1,0:T(8,128)(2,1)S(1)}, u32[]{:S(2)}, u32[]{:S(2)}) collective-permute-start(bf16[64,1024]{1,0:T(8,128)(2,1)S(1)} %convolution_convert_fusion.9), channel_id=1, source_target_pairs={{0,2},{1,3},{2,0},{3,1},{4,5},{5,4},{6,7},{7,6},{8,9},{9,8},{10,11... | collective-permute-start | bytes 393224 | tf_op jit(solution)/shard_map/ppermute | solution.py:28
  13.7 3.8 %collective-permute-done.4 = bf16[64,1024]{1,0:T(8,128)(2,1)S(1)} collective-permute-done((bf16[64,1024]{1,0:T(8,128)(2,1)S(1)}, bf16[64,1024]{1,0:T(8,128)(2,1)S(1)}, u32[]{:S(2)}, u32[]{:S(2)}) %collective-permute-start.4) | collective-permute-done | bytes 131104 | tf_op jit(solution)/shard_map/ppermute | solution.py:28
  18.1 1.3 %collective-permute-done.5 = bf16[64,1024]{1,0:T(8,128)(2,1)S(1)} collective-permute-done((bf16[64,1024]{1,0:T(8,128)(2,1)S(1)}, bf16[64,1024]{1,0:T(8,128)(2,1)S(1)}, u32[]{:S(2)}, u32[]{:S(2)}) %collective-permute-start.5) | collective-permute-done | bytes 131104 | tf_op jit(solution)/shard_map/ppermute | solution.py:28
  21.3 5.0 %conditional.7 = (bf16[64,1024]{1,0:T(8,128)(2,1)}, bf16[64,1024]{1,0:T(8,128)(2,1)}) conditional(s32[]{:T(128)} %bitcast, bf16[64,1024]{1,0:T(8,128)(2,1)S(1)} %collective-permute-done.6, (bf16[64,1024]{1,0:T(8,128)(2,1)S(1)}, bf16[1024,1024]{1,0:T(8,128)(2,1)S(1)}) %tuple.51), branch_computations={%region_5.6_spmd, %region_6.7_spmd} | conditional | flops 268566528 | bytes 5767264 | solution.py:206
  22.0 1.3 %collective-permute-done = bf16[64,1024]{1,0:T(8,128)(2,1)} collective-permute-done((bf16[64,1024]{1,0:T(8,128)(2,1)S(1)}, bf16[64,1024]{1,0:T(8,128)(2,1)}, u32[]{:S(2)}, u32[]{:S(2)}) %collective-permute-start) | collective-permute-done | bytes 131104 | tf_op jit(solution)/shard_map/cond/branch_1_fun/ppermute | solution.py:28
  23.4 1.4 %convolution_convert_fusion.2 = bf16[64,1024]{1,0:T(8,128)(2,1)S(1)} fusion(bf16[64,1024]{1,0:T(8,128)(2,1)} %collective-permute-done, bf16[1024,1024]{1,0:T(8,128)(2,1)S(1)} %get-tuple-element.70), kind=kOutput, calls=%fused_computation.2 | convolution fusion | flops 134283264 | bytes 2359296 | tf_op jit(solution)/shard_map/cond/branch_1_fun/dot_general | solution.py:32
  25.0 1.3 %collective-permute-done.1 = bf16[64,1024]{1,0:T(8,128)(2,1)} collective-permute-done((bf16[64,1024]{1,0:T(8,128)(2,1)S(1)}, bf16[64,1024]{1,0:T(8,128)(2,1)}, u32[]{:S(2)}, u32[]{:S(2)}) %collective-permute-start.1) | collective-permute-done | bytes 131104 | tf_op jit(solution)/shard_map/cond/branch_1_fun/ppermute | solution.py:28
  26.3 1.5 %convolution_convert_fusion.6 = bf16[64,1024]{1,0:T(8,128)(2,1)S(1)} fusion(bf16[64,1024]{1,0:T(8,128)(2,1)} %get-tuple-element.103, bf16[1024,1024]{1,0:T(8,128)(2,1)S(1)} %get-tuple-element.119), kind=kOutput, calls=%fused_computation.20 | convolution fusion | flops 134283264 | bytes 2359296 | tf_op jit(solution)/shard_map/dot_general | solution.py:32
  28.4 3.3 %conditional.8 = (f32[64,1024]{1,0:T(8,128)S(1)}) conditional(s32[]{:T(128)} %convert_element_type.67, (bf16[64,1024]{1,0:T(8,128)(2,1)S(1)}, bf16[1024,1024]{1,0:T(8,128)(2,1)S(1)}, bf16[1024,1024]{1,0:T(8,128)(2,1)}, bf16[1024,1024]{1,0:T(8,128)(2,1)}, bf16[1024,1024]{1,0:T(8,128)(2,1)}) %tuple.77, () %tuple.54), branch_computations={%region_7.8_spmd, %region_8.9_spmd} | conditional | flops 524288 | bytes 262156 | solution.py:214
  28.4 3.3 %branch_0_fun.1 = f32[64,1024]{1,0:T(8,128)S(1)} custom-call(bf16[64,1024]{1,0:T(8,128)(2,1)S(1)} %get-tuple-element.71.down, bf16[1024,1024]{1,0:T(8,128)(2,1)S(1)} %get-tuple-element.72.trans, bf16[1024,1024]{1,0:T(8,128)(2,1)} %get-tuple-element.73.other_t, bf16[1024,1024]{1,0:T(8,128)(2,1)} %get-tuple-element.74.refl, ...), custom_call_target="tpu_custom_call" | custom-call | flops 524288 | bytes 6144 | tf_op jit(solution)/shard_map/cond/branch_0_fun/pallas_call | solution.py:94
  33.0 1.0 %collective-permute-done.9 = bf16[64,1024]{1,0:T(8,128)(2,1)S(1)} collective-permute-done((bf16[64,1024]{1,0:T(8,128)(2,1)S(1)}, bf16[64,1024]{1,0:T(8,128)(2,1)S(1)}, u32[]{:S(2)}, u32[]{:S(2)}) %collective-permute-start.9) | collective-permute-done | bytes 131104 | tf_op jit(solution)/shard_map/ppermute | solution.py:14
  34.0 1.5 %convolution_convert_fusion.4 = bf16[128,512]{1,0:T(8,128)(2,1)S(1)} fusion(bf16[1024,512]{1,0:T(8,128)(2,1)} %collective-permute-done.8, bf16[64,1024]{1,0:T(8,128)(2,1)S(1)} %collective-permute-done.9, bf16[64,1024]{1,0:T(8,128)(2,1)S(1)} %convolution_convert_fusion.5), kind=kOutput, calls=%fused_computation.18 | convolution fusion | flops 134807552 | bytes 1441792 | tf_op jit(solution)/shard_map/dot_general | solution.py:32
  38.1 1.0 %collective-permute-done.11 = bf16[64,1024]{1,0:T(8,128)(2,1)S(1)} collective-permute-done((bf16[64,1024]{1,0:T(8,128)(2,1)S(1)}, bf16[64,1024]{1,0:T(8,128)(2,1)S(1)}, u32[]{:S(2)}, u32[]{:S(2)}) %collective-permute-start.11) | collective-permute-done | bytes 131104 | tf_op jit(solution)/shard_map/ppermute | solution.py:28
  40.2 1.0 %collective-permute-done.12 = bf16[64,1024]{1,0:T(8,128)(2,1)S(1)} collective-permute-done((bf16[64,1024]{1,0:T(8,128)(2,1)S(1)}, bf16[64,1024]{1,0:T(8,128)(2,1)S(1)}, u32[]{:S(2)}, u32[]{:S(2)}) %collective-permute-start.12) | collective-permute-done | bytes 131104 | tf_op jit(solution)/shard_map/ppermute | solution.py:28
  42.4 1.0 %collective-permute-done.13 = bf16[64,1024]{1,0:T(8,128)(2,1)S(1)} collective-permute-done((bf16[64,1024]{1,0:T(8,128)(2,1)S(1)}, bf16[64,1024]{1,0:T(8,128)(2,1)S(1)}, u32[]{:S(2)}, u32[]{:S(2)}) %collective-permute-start.13) | collective-permute-done | bytes 131104 | tf_op jit(solution)/shard_map/ppermute | solution.py:28
  44.6 1.0 %collective-permute-done.14 = bf16[64,1024]{1,0:T(8,128)(2,1)S(1)} collective-permute-done((bf16[64,1024]{1,0:T(8,128)(2,1)S(1)}, bf16[64,1024]{1,0:T(8,128)(2,1)S(1)}, u32[]{:S(2)}, u32[]{:S(2)}) %collective-permute-start.14) | collective-permute-done | bytes 131104 | tf_op jit(solution)/shard_map/ppermute | solution.py:28
  48.5 32.1 %collective-permute-start.16 = (bf16[64,1024]{1,0:T(8,128)(2,1)S(1)}, bf16[64,1024]{1,0:T(8,128)(2,1)S(1)}, u32[]{:S(2)}, u32[]{:S(2)}) collective-permute-start(bf16[64,1024]{1,0:T(8,128)(2,1)S(1)} %fusion.5), channel_id=1, source_target_pairs={{0,2},{1,3},{2,0},{3,1},{4,5},{5,4},{6,7},{7,6},{8,9},{9,8},{10,11... | collective-permute-start | bytes 393224 | tf_op jit(solution)/shard_map/ppermute | solution.py:28
  80.6 2.9 %collective-permute-done.16 = bf16[64,1024]{1,0:T(8,128)(2,1)S(1)} collective-permute-done((bf16[64,1024]{1,0:T(8,128)(2,1)S(1)}, bf16[64,1024]{1,0:T(8,128)(2,1)S(1)}, u32[]{:S(2)}, u32[]{:S(2)}) %collective-permute-start.16) | collective-permute-done | bytes 131104 | tf_op jit(solution)/shard_map/ppermute | solution.py:28
  83.5 1.4 %fusion.8 = bf16[1,64,1024]{2,1,0:T(8,128)(2,1)} fusion(f32[64,1024]{1,0:T(8,128)S(1)} %get-tuple-element.122, bf16[64,1024]{1,0:T(8,128)(2,1)S(1)} %collective-permute-done.16, bf16[1024,1024]{1,0:T(8,128)(2,1)S(1)} %get-tuple-element.119, bf16[64,1024]{1,0:T(8,128)(2,1)S(1)} %fusion.5, bf16[64,1024]{1,0:T(8,128)(2,1)S(1)} %fusion.4, ...), kind=kOutput, calls=%fused_computation.25 | convolution fusion | flops 134807552 | bytes 3538951 | tf_op jit(solution)/shard_map/dot_general | solution.py:36
  (45 shorter events, 16.0 us)
Async XLA Ops:
  0.0 4.6 %collective-permute-start.3 = (bf16[1024,1024]{1,0:T(8,128)(2,1)}, bf16[1024,1024]{1,0:T(8,128)(2,1)}, u32[]{:S(2)}, u32[]{:S(2)}) collective-permute-start(bf16[1024,1024]{1,0:T(8,128)(2,1)} %bitcast.37), channel_id=1, source_target_pairs={{0,1},{1,0},{2,3},{3,2},{4,5},{5,4},{6,7},{7,6},{8,9},{9,8},{10,11... | collective-permute-start | bytes 6291464 | tf_op jit(solution)/shard_map/ppermute | solution.py:14
  0.5 8.7 %collective-permute-start.2 = (bf16[1024,1024]{1,0:T(8,128)(2,1)}, bf16[1024,1024]{1,0:T(8,128)(2,1)}, u32[]{:S(2)}, u32[]{:S(2)}) collective-permute-start(bf16[1024,1024]{1,0:T(8,128)(2,1)} %bitcast.44), channel_id=1, source_target_pairs={{0,1},{1,0},{2,3},{3,2},{4,5},{5,4},{6,7},{7,6},{8,9},{9,8},{10,11... | collective-permute-start | bytes 6291464 | tf_op jit(solution)/shard_map/ppermute | solution.py:14
  10.8 9.4 %copy-start.1 = (s32[128]{0:T(128)S(1)}, s32[128]{0:T(128)}, u32[]{:S(2)}) copy-start(s32[128]{0:T(128)} %param.16) | copy-start | bytes 1540
  10.8 6.8 %collective-permute-start.4 = (bf16[64,1024]{1,0:T(8,128)(2,1)S(1)}, bf16[64,1024]{1,0:T(8,128)(2,1)S(1)}, u32[]{:S(2)}, u32[]{:S(2)}) collective-permute-start(bf16[64,1024]{1,0:T(8,128)(2,1)S(1)} %convolution_convert_fusion.9), channel_id=1, source_target_pairs={{0,2},{1,3},{2,0},{3,1},{4,5},{5,4},{6,7},{7,6},{8,9},{9,8},{10,11... | collective-permute-start | bytes 393224 | tf_op jit(solution)/shard_map/ppermute | solution.py:28
  18.0 1.4 %collective-permute-start.5 = (bf16[64,1024]{1,0:T(8,128)(2,1)S(1)}, bf16[64,1024]{1,0:T(8,128)(2,1)S(1)}, u32[]{:S(2)}, u32[]{:S(2)}) collective-permute-start(bf16[64,1024]{1,0:T(8,128)(2,1)S(1)} %convolution_convert_fusion.8), channel_id=1, source_target_pairs={{0,1},{1,0},{2,4},{3,5},{4,2},{5,3},{6,7},{7,6},{8,9},{9,8},{10,11... | collective-permute-start | bytes 393224 | tf_op jit(solution)/shard_map/ppermute | solution.py:28
  19.9 1.4 %collective-permute-start.6 = (bf16[64,1024]{1,0:T(8,128)(2,1)S(1)}, bf16[64,1024]{1,0:T(8,128)(2,1)S(1)}, u32[]{:S(2)}, u32[]{:S(2)}) collective-permute-start(bf16[64,1024]{1,0:T(8,128)(2,1)S(1)} %convolution_convert_fusion.7), channel_id=1, source_target_pairs={{0,1},{1,0},{2,3},{3,2},{4,6},{5,7},{6,4},{7,5},{8,9},{9,8},{10,11... | collective-permute-start | bytes 393224 | tf_op jit(solution)/shard_map/ppermute | solution.py:28
  20.2 12.8 %collective-permute-start.8 = (bf16[1024,512]{1,0:T(8,128)(2,1)}, bf16[1024,512]{1,0:T(8,128)(2,1)}, u32[]{:S(2)}, u32[]{:S(2)}) collective-permute-start(bf16[1024,512]{1,0:T(8,128)(2,1)} %get-tuple-element.120), channel_id=1, source_target_pairs={{0,1},{1,0},{2,3},{3,2},{4,5},{5,4},{6,7},{7,6},{8,9},{9,8},{10,11... | collective-permute-start | bytes 3145736 | tf_op jit(solution)/shard_map/ppermute | solution.py:28
  21.8 1.5 %collective-permute-start = (bf16[64,1024]{1,0:T(8,128)(2,1)S(1)}, bf16[64,1024]{1,0:T(8,128)(2,1)}, u32[]{:S(2)}, u32[]{:S(2)}) collective-permute-start(bf16[64,1024]{1,0:T(8,128)(2,1)S(1)} %convolution_convert_fusion.3), channel_id=1, source_target_pairs={{0,1},{1,0},{2,3},{3,2},{4,5},{5,4},{6,8},{7,9},{8,6},{9,7},{10,11... | collective-permute-start | bytes 393224 | tf_op jit(solution)/shard_map/cond/branch_1_fun/ppermute | solution.py:28
  24.8 1.5 %collective-permute-start.1 = (bf16[64,1024]{1,0:T(8,128)(2,1)S(1)}, bf16[64,1024]{1,0:T(8,128)(2,1)}, u32[]{:S(2)}, u32[]{:S(2)}) collective-permute-start(bf16[64,1024]{1,0:T(8,128)(2,1)S(1)} %convolution_convert_fusion.2), channel_id=1, source_target_pairs={{0,1},{1,0},{2,3},{3,2},{4,5},{5,4},{6,7},{7,6},{8,10},{9,11},{10,... | collective-permute-start | bytes 393224 | tf_op jit(solution)/shard_map/cond/branch_1_fun/ppermute | solution.py:28
  26.3 2.1 %copy-start = (bf16[1,1024,1024]{2,1,0:T(8,128)(2,1)S(1)}, bf16[1,1024,1024]{2,1,0:T(8,128)(2,1)}, u32[]{:S(2)}) copy-start(bf16[1,1024,1024]{2,1,0:T(8,128)(2,1)} %param.14) | copy-start | bytes 6291460
  27.8 3.8 %collective-permute-start.7 = (bf16[64,1024]{1,0:T(8,128)(2,1)S(1)}, bf16[64,1024]{1,0:T(8,128)(2,1)S(1)}, u32[]{:S(2)}, u32[]{:S(2)}) collective-permute-start(bf16[64,1024]{1,0:T(8,128)(2,1)S(1)} %convolution_convert_fusion.6), channel_id=1, source_target_pairs={{0,1},{1,0},{2,3},{3,2},{4,5},{5,4},{6,7},{7,6},{8,9},{9,8},{10,12... | collective-permute-start | bytes 393224 | tf_op jit(solution)/shard_map/ppermute | solution.py:28
  32.2 1.8 %collective-permute-start.9 = (bf16[64,1024]{1,0:T(8,128)(2,1)S(1)}, bf16[64,1024]{1,0:T(8,128)(2,1)S(1)}, u32[]{:S(2)}, u32[]{:S(2)}) collective-permute-start(bf16[64,1024]{1,0:T(8,128)(2,1)S(1)} %convolution_convert_fusion.5), channel_id=1, source_target_pairs={{0,1},{1,0},{2,3},{3,2},{4,5},{5,4},{6,7},{7,6},{8,9},{9,8},{10,11... | collective-permute-start | bytes 393224 | tf_op jit(solution)/shard_map/ppermute | solution.py:14
  35.5 1.3 %collective-permute-start.10 = (bf16[64,512]{1,0:T(8,128)(2,1)S(1)}, bf16[64,512]{1,0:T(8,128)(2,1)S(1)}, u32[]{:S(2)}, u32[]{:S(2)}) collective-permute-start(bf16[64,512]{1,0:T(8,128)(2,1)S(1)} %slice.13), channel_id=1, source_target_pairs={{0,1},{1,0},{2,3},{3,2},{4,5},{5,4},{6,7},{7,6},{8,9},{9,8},{10,11... | collective-permute-start | bytes 196616 | tf_op jit(solution)/shard_map/ppermute | solution.py:14
  37.7 1.4 %collective-permute-start.11 = (bf16[64,1024]{1,0:T(8,128)(2,1)S(1)}, bf16[64,1024]{1,0:T(8,128)(2,1)S(1)}, u32[]{:S(2)}, u32[]{:S(2)}) collective-permute-start(bf16[64,1024]{1,0:T(8,128)(2,1)S(1)} %fusion), channel_id=1, source_target_pairs={{0,1},{1,0},{2,3},{3,2},{4,5},{5,4},{6,7},{7,6},{8,9},{9,8},{10,12... | collective-permute-start | bytes 393224 | tf_op jit(solution)/shard_map/ppermute | solution.py:28
  39.8 1.4 %collective-permute-start.12 = (bf16[64,1024]{1,0:T(8,128)(2,1)S(1)}, bf16[64,1024]{1,0:T(8,128)(2,1)S(1)}, u32[]{:S(2)}, u32[]{:S(2)}) collective-permute-start(bf16[64,1024]{1,0:T(8,128)(2,1)S(1)} %fusion.1), channel_id=1, source_target_pairs={{0,1},{1,0},{2,3},{3,2},{4,5},{5,4},{6,7},{7,6},{8,10},{9,11},{10,... | collective-permute-start | bytes 393224 | tf_op jit(solution)/shard_map/ppermute | solution.py:28
  42.0 1.4 %collective-permute-start.13 = (bf16[64,1024]{1,0:T(8,128)(2,1)S(1)}, bf16[64,1024]{1,0:T(8,128)(2,1)S(1)}, u32[]{:S(2)}, u32[]{:S(2)}) collective-permute-start(bf16[64,1024]{1,0:T(8,128)(2,1)S(1)} %fusion.2), channel_id=1, source_target_pairs={{0,1},{1,0},{2,3},{3,2},{4,5},{5,4},{6,8},{7,9},{8,6},{9,7},{10,11... | collective-permute-start | bytes 393224 | tf_op jit(solution)/shard_map/ppermute | solution.py:28
  44.2 1.4 %collective-permute-start.14 = (bf16[64,1024]{1,0:T(8,128)(2,1)S(1)}, bf16[64,1024]{1,0:T(8,128)(2,1)S(1)}, u32[]{:S(2)}, u32[]{:S(2)}) collective-permute-start(bf16[64,1024]{1,0:T(8,128)(2,1)S(1)} %fusion.3), channel_id=1, source_target_pairs={{0,1},{1,0},{2,3},{3,2},{4,6},{5,7},{6,4},{7,5},{8,9},{9,8},{10,11... | collective-permute-start | bytes 393224 | tf_op jit(solution)/shard_map/ppermute | solution.py:28
  46.3 1.4 %collective-permute-start.15 = (bf16[64,1024]{1,0:T(8,128)(2,1)S(1)}, bf16[64,1024]{1,0:T(8,128)(2,1)S(1)}, u32[]{:S(2)}, u32[]{:S(2)}) collective-permute-start(bf16[64,1024]{1,0:T(8,128)(2,1)S(1)} %fusion.4), channel_id=1, source_target_pairs={{0,1},{1,0},{2,4},{3,5},{4,2},{5,3},{6,7},{7,6},{8,9},{9,8},{10,11... | collective-permute-start | bytes 393224 | tf_op jit(solution)/shard_map/ppermute | solution.py:28
  46.8 33.8 %collective-permute-start.17 = (bf16[64,1024]{1,0:T(8,128)(2,1)S(1)}, bf16[64,1024]{1,0:T(8,128)(2,1)S(1)}, u32[]{:S(2)}, u32[]{:S(2)}) collective-permute-start(bf16[64,1024]{1,0:T(8,128)(2,1)S(1)} %pad_maximum_fusion), channel_id=1, source_target_pairs={{0,1},{1,0},{2,3},{3,2},{4,5},{5,4},{6,7},{7,6},{8,9},{9,8},{10,11... | collective-permute-start | bytes 393224 | tf_op jit(solution)/shard_map/ppermute | solution.py:28
  48.5 35.0 %collective-permute-start.16 = (bf16[64,1024]{1,0:T(8,128)(2,1)S(1)}, bf16[64,1024]{1,0:T(8,128)(2,1)S(1)}, u32[]{:S(2)}, u32[]{:S(2)}) collective-permute-start(bf16[64,1024]{1,0:T(8,128)(2,1)S(1)} %fusion.5), channel_id=1, source_target_pairs={{0,2},{1,3},{2,0},{3,1},{4,5},{5,4},{6,7},{7,6},{8,9},{9,8},{10,11... | collective-permute-start | bytes 393224 | tf_op jit(solution)/shard_map/ppermute | solution.py:28

commit v6 on v4

--- a/solution.py
+++ b/solution.py
@@ -7,7 +7,7 @@
 
 BLOCKS = 4
 KEEP = 3
-VMEM = 52 * 2**20
+VMEM = 46 * 2**20
 
 
 def swap_cores(array):

time: 85.1 us -> 85.1 us (level)
  no operation moved by 1% of the time
where the time goes in v6:
time: 85.1 us; the launch traced here: 84.9 us
  starting transfers between devices  40.8 us (48%)
  waiting for transfers between devices  21.7 us (25%)
  matrix products  17.8 us (21%)
  Pallas kernels  3.27 us (4%)
    ppermute x14, starting transfers between devices, swap_sections(): return lax.ppermute(value, 'sec', pairs)  39.1 us
    ppermute x14, waiting for transfers between devices, swap_sections(): return lax.ppermute(value, 'sec', pairs)  16.1 us
    dot_general x9, matrix products, matmul(): return jnp.dot(left, right, preferred_element_type=jnp.float32)  11.8 us
    dot_general x7, matrix products, matmul_nt(): lax.dot_general(left, right, (((1,), (1,)), ((), ())), preferred_element_...  5.99 us
    ppermute x4, waiting for transfers between devices, swap_cores(): lax.ppermute(array, 'sec', [(i, i ^ 1) for i in range(lax.axis_size('sec'...  5.57 us
    pallas_call x1, Pallas kernels, echo_of(): pl.pallas_call(echo_kernel, out_shape=jax.ShapeDtypeStruct(down.shape, jn...  3.27 us
  transfers between devices with their start and end apart: 18, of which 14 were waited for; matrix products, arithmetic and copies ran while one was open for 13% of the time, Pallas kernels for 4%

profile of v6, /device:TPU:0, one launch (start us, length us, event | category | flops | bytes accessed | tf_op | source)
XLA Modules:
  0.0 84.9 jit_solution(13405717461077919951)
XLA Ops:
  1.2 3.3 %collective-permute-done.3.other_t = bf16[1024,1024]{1,0:T(8,128)(2,1)} collective-permute-done((bf16[1024,1024]{1,0:T(8,128)(2,1)}, bf16[1024,1024]{1,0:T(8,128)(2,1)}, u32[]{:S(2)}, u32[]{:S(2)}) %collective-permute-start.3) | collective-permute-done | bytes 2097184 | tf_op jit(solution)/shard_map/ppermute | solution.py:14
  4.6 4.6 %conditional.4 = (bf16[1024,1024]{1,0:T(8,128)(2,1)S(1)}) conditional(s32[]{:T(128)} %clamp.3, (bf16[1024,1024]{1,0:T(8,128)(2,1)}, bf16[1024,1024]{1,0:T(8,128)(2,1)}) %tuple.61, (bf16[1024,1024]{1,0:T(8,128)(2,1)}, bf16[1024,1024]{1,0:T(8,128)(2,1)}) %tuple.62, bf16[1024,1024]{1,0:T(8,128)(2,1)} %bitcast.38), branch_computations={%region_0.1_spmd, %region_1.2_spmd, %region_2.3_spmd} | conditional | flops 2148532224 | bytes 6291464 | solution.py:181
  4.6 4.5 %convolution_convert_fusion = bf16[1024,1024]{1,0:T(8,128)(2,1)S(1)} fusion(bf16[1024,1024]{1,0:T(8,128)(2,1)} %get-tuple-element.48, bf16[1024,1024]{1,0:T(8,128)(2,1)} %get-tuple-element.49), kind=kOutput, calls=%fused_computation | convolution fusion | flops 2148532224 | bytes 6291456 | tf_op jit(solution)/shard_map/cond/branch_0_fun/dot_general | solution.py:32
  9.8 3.0 %collective-permute-start.4 = (bf16[64,1024]{1,0:T(8,128)(2,1)S(1)}, bf16[64,1024]{1,0:T(8,128)(2,1)S(1)}, u32[]{:S(2)}, u32[]{:S(2)}) collective-permute-start(bf16[64,1024]{1,0:T(8,128)(2,1)S(1)} %convolution_convert_fusion.9), channel_id=1, source_target_pairs={{0,2},{1,3},{2,0},{3,1},{4,5},{5,4},{6,7},{7,6},{8,9},{9,8},{10,11... | collective-permute-start | bytes 393224 | tf_op jit(solution)/shard_map/ppermute | solution.py:28
  12.8 3.8 %collective-permute-done.4 = bf16[64,1024]{1,0:T(8,128)(2,1)S(1)} collective-permute-done((bf16[64,1024]{1,0:T(8,128)(2,1)S(1)}, bf16[64,1024]{1,0:T(8,128)(2,1)S(1)}, u32[]{:S(2)}, u32[]{:S(2)}) %collective-permute-start.4) | collective-permute-done | bytes 131104 | tf_op jit(solution)/shard_map/ppermute | solution.py:28
  17.1 1.3 %collective-permute-done.5 = bf16[64,1024]{1,0:T(8,128)(2,1)S(1)} collective-permute-done((bf16[64,1024]{1,0:T(8,128)(2,1)S(1)}, bf16[64,1024]{1,0:T(8,128)(2,1)S(1)}, u32[]{:S(2)}, u32[]{:S(2)}) %collective-permute-start.5) | collective-permute-done | bytes 131104 | tf_op jit(solution)/shard_map/ppermute | solution.py:28
  20.4 5.0 %conditional.6 = (bf16[64,1024]{1,0:T(8,128)(2,1)}, bf16[64,1024]{1,0:T(8,128)(2,1)}) conditional(s32[]{:T(128)} %bitcast, bf16[64,1024]{1,0:T(8,128)(2,1)S(1)} %collective-permute-done.6, (bf16[64,1024]{1,0:T(8,128)(2,1)S(1)}, bf16[1024,1024]{1,0:T(8,128)(2,1)S(1)}) %tuple.45), branch_computations={%region_5.6_spmd, %region_6.7_spmd} | conditional | flops 268566528 | bytes 5767264 | solution.py:206
  21.1 1.3 %collective-permute-done = bf16[64,1024]{1,0:T(8,128)(2,1)} collective-permute-done((bf16[64,1024]{1,0:T(8,128)(2,1)S(1)}, bf16[64,1024]{1,0:T(8,128)(2,1)}, u32[]{:S(2)}, u32[]{:S(2)}) %collective-permute-start) | collective-permute-done | bytes 131104 | tf_op jit(solution)/shard_map/cond/branch_1_fun/ppermute | solution.py:28
  22.4 1.4 %convolution_convert_fusion.2 = bf16[64,1024]{1,0:T(8,128)(2,1)S(1)} fusion(bf16[64,1024]{1,0:T(8,128)(2,1)} %collective-permute-done, bf16[1024,1024]{1,0:T(8,128)(2,1)S(1)} %get-tuple-element.57), kind=kOutput, calls=%fused_computation.2 | convolution fusion | flops 134283264 | bytes 2359296 | tf_op jit(solution)/shard_map/cond/branch_1_fun/dot_general | solution.py:32
  24.1 1.2 %collective-permute-done.1 = bf16[64,1024]{1,0:T(8,128)(2,1)} collective-permute-done((bf16[64,1024]{1,0:T(8,128)(2,1)S(1)}, bf16[64,1024]{1,0:T(8,128)(2,1)}, u32[]{:S(2)}, u32[]{:S(2)}) %collective-permute-start.1) | collective-permute-done | bytes 131104 | tf_op jit(solution)/shard_map/cond/branch_1_fun/ppermute | solution.py:28
  25.4 1.5 %convolution_convert_fusion.6 = bf16[64,1024]{1,0:T(8,128)(2,1)S(1)} fusion(bf16[64,1024]{1,0:T(8,128)(2,1)} %get-tuple-element.85, bf16[1024,1024]{1,0:T(8,128)(2,1)S(1)} %get-tuple-element.101), kind=kOutput, calls=%fused_computation.20 | convolution fusion | flops 134283264 | bytes 2359296 | tf_op jit(solution)/shard_map/dot_general | solution.py:32
  27.4 3.3 %shard_map.37 = f32[64,1024]{1,0:T(8,128)S(1)} custom-call(bf16[64,1024]{1,0:T(8,128)(2,1)S(1)} %fusion.17.down, bf16[1024,1024]{1,0:T(8,128)(2,1)S(1)} %bitcast.43, bf16[1024,1024]{1,0:T(8,128)(2,1)} %collective-permute-done.3.other_t, bf16[1024,1024]{1,0:T(8,128)(2,1)} %bitcast.46, bf16[1024,1024]{1,0:T(8,128)(2,1)} %collective-permute-done.2.other_r), custom_call_target="tpu_custom_call" | custom-call | flops 524288 | bytes 6144 | tf_op jit(solution)/shard_map/pallas_call | solution.py:94
  30.7 1.1 %convolution_convert_fusion.5 = bf16[64,1024]{1,0:T(8,128)(2,1)} fusion(bf16[64,1024]{1,0:T(8,128)(2,1)S(1)} %broadcast_select_fusion, bf16[1024,1024]{1,0:T(8,128)(2,1)S(1)} %get-tuple-element.101), kind=kOutput, calls=%fused_computation.19 | convolution fusion | flops 134283264 | bytes 2359296 | tf_op jit(solution)/shard_map/dot_general | solution.py:32
  32.6 1.3 %collective-permute-done.9 = bf16[64,1024]{1,0:T(8,128)(2,1)} collective-permute-done((bf16[64,1024]{1,0:T(8,128)(2,1)}, bf16[64,1024]{1,0:T(8,128)(2,1)}, u32[]{:S(2)}, u32[]{:S(2)}) %collective-permute-start.9) | collective-permute-done | bytes 131104 | tf_op jit(solution)/shard_map/ppermute | solution.py:14
  34.0 1.3 %convolution_convert_fusion.4 = bf16[128,512]{1,0:T(8,128)(2,1)S(1)} fusion(bf16[1024,512]{1,0:T(8,128)(2,1)S(1)} %collective-permute-done.8, bf16[64,1024]{1,0:T(8,128)(2,1)} %collective-permute-done.9, bf16[64,1024]{1,0:T(8,128)(2,1)} %convolution_convert_fusion.5), kind=kOutput, calls=%fused_computation.18 | convolution fusion | flops 134807552 | bytes 1441792 | tf_op jit(solution)/shard_map/dot_general | solution.py:32
  35.7 0.9 %collective-permute-done.10 = bf16[64,512]{1,0:T(8,128)(2,1)S(1)} collective-permute-done((bf16[64,512]{1,0:T(8,128)(2,1)S(1)}, bf16[64,512]{1,0:T(8,128)(2,1)S(1)}, u32[]{:S(2)}, u32[]{:S(2)}) %collective-permute-start.10) | collective-permute-done | bytes 65568 | tf_op jit(solution)/shard_map/ppermute | solution.py:14
  36.6 0.8 fusion
  37.8 1.0 %collective-permute-done.11 = bf16[64,1024]{1,0:T(8,128)(2,1)S(1)} collective-permute-done((bf16[64,1024]{1,0:T(8,128)(2,1)S(1)}, bf16[64,1024]{1,0:T(8,128)(2,1)S(1)}, u32[]{:S(2)}, u32[]{:S(2)}) %collective-permute-start.11) | collective-permute-done | bytes 131104 | tf_op jit(solution)/shard_map/ppermute | solution.py:28
  40.0 1.0 %collective-permute-done.12 = bf16[64,1024]{1,0:T(8,128)(2,1)S(1)} collective-permute-done((bf16[64,1024]{1,0:T(8,128)(2,1)S(1)}, bf16[64,1024]{1,0:T(8,128)(2,1)S(1)}, u32[]{:S(2)}, u32[]{:S(2)}) %collective-permute-start.12) | collective-permute-done | bytes 131104 | tf_op jit(solution)/shard_map/ppermute | solution.py:28
  42.1 1.0 %collective-permute-done.13 = bf16[64,1024]{1,0:T(8,128)(2,1)S(1)} collective-permute-done((bf16[64,1024]{1,0:T(8,128)(2,1)S(1)}, bf16[64,1024]{1,0:T(8,128)(2,1)S(1)}, u32[]{:S(2)}, u32[]{:S(2)}) %collective-permute-start.13) | collective-permute-done | bytes 131104 | tf_op jit(solution)/shard_map/ppermute | solution.py:28
  44.3 1.0 %collective-permute-done.14 = bf16[64,1024]{1,0:T(8,128)(2,1)S(1)} collective-permute-done((bf16[64,1024]{1,0:T(8,128)(2,1)S(1)}, bf16[64,1024]{1,0:T(8,128)(2,1)S(1)}, u32[]{:S(2)}, u32[]{:S(2)}) %collective-permute-start.14) | collective-permute-done | bytes 131104 | tf_op jit(solution)/shard_map/ppermute | solution.py:28
  48.2 32.3 %collective-permute-start.16 = (bf16[64,1024]{1,0:T(8,128)(2,1)S(1)}, bf16[64,1024]{1,0:T(8,128)(2,1)S(1)}, u32[]{:S(2)}, u32[]{:S(2)}) collective-permute-start(bf16[64,1024]{1,0:T(8,128)(2,1)S(1)} %fusion.5), channel_id=1, source_target_pairs={{0,2},{1,3},{2,0},{3,1},{4,5},{5,4},{6,7},{7,6},{8,9},{9,8},{10,11... | collective-permute-start | bytes 393224 | tf_op jit(solution)/shard_map/ppermute | solution.py:28
  80.6 2.9 %collective-permute-done.16 = bf16[64,1024]{1,0:T(8,128)(2,1)S(1)} collective-permute-done((bf16[64,1024]{1,0:T(8,128)(2,1)S(1)}, bf16[64,1024]{1,0:T(8,128)(2,1)S(1)}, u32[]{:S(2)}, u32[]{:S(2)}) %collective-permute-start.16) | collective-permute-done | bytes 131104 | tf_op jit(solution)/shard_map/ppermute | solution.py:28
  83.5 1.4 %fusion.8 = bf16[1,64,1024]{2,1,0:T(8,128)(2,1)} fusion(f32[64,1024]{1,0:T(8,128)S(1)} %get-tuple-element.103, bf16[64,1024]{1,0:T(8,128)(2,1)S(1)} %collective-permute-done.16, bf16[1024,1024]{1,0:T(8,128)(2,1)S(1)} %get-tuple-element.101, bf16[64,1024]{1,0:T(8,128)(2,1)S(1)} %fusion.5, bf16[64,1024]{1,0:T(8,128)(2,1)S(1)} %fusion.4, ...), kind=kOutput, calls=%fused_computation.25 | convolution fusion | flops 134807552 | bytes 3538951 | tf_op jit(solution)/shard_map/dot_general | solution.py:36
  (50 shorter events, 13.9 us)
Async XLA Ops:
  0.0 4.6 %collective-permute-start.3 = (bf16[1024,1024]{1,0:T(8,128)(2,1)}, bf16[1024,1024]{1,0:T(8,128)(2,1)}, u32[]{:S(2)}, u32[]{:S(2)}) collective-permute-start(bf16[1024,1024]{1,0:T(8,128)(2,1)} %bitcast.37), channel_id=1, source_target_pairs={{0,1},{1,0},{2,3},{3,2},{4,5},{5,4},{6,7},{7,6},{8,9},{9,8},{10,11... | collective-permute-start | bytes 6291464 | tf_op jit(solution)/shard_map/ppermute | solution.py:14
  0.5 8.7 %collective-permute-start.2 = (bf16[1024,1024]{1,0:T(8,128)(2,1)}, bf16[1024,1024]{1,0:T(8,128)(2,1)}, u32[]{:S(2)}, u32[]{:S(2)}) collective-permute-start(bf16[1024,1024]{1,0:T(8,128)(2,1)} %bitcast.44), channel_id=1, source_target_pairs={{0,1},{1,0},{2,3},{3,2},{4,5},{5,4},{6,7},{7,6},{8,9},{9,8},{10,11... | collective-permute-start | bytes 6291464 | tf_op jit(solution)/shard_map/ppermute | solution.py:14
  9.3 7.8 %copy-start.1 = (bf16[1024,512]{1,0:T(8,128)(2,1)}, bf16[1024,512]{1,0:T(8,128)(2,1)S(1)}, u32[]{:S(2)}) copy-start(bf16[1024,512]{1,0:T(8,128)(2,1)S(1)} %get-tuple-element.102) | copy-start | bytes 3145732
  9.8 9.4 %copy-start.4 = (s32[128]{0:T(128)S(1)}, s32[128]{0:T(128)}, u32[]{:S(2)}) copy-start(s32[128]{0:T(128)} %param.14) | copy-start | bytes 1540
  9.8 6.8 %collective-permute-start.4 = (bf16[64,1024]{1,0:T(8,128)(2,1)S(1)}, bf16[64,1024]{1,0:T(8,128)(2,1)S(1)}, u32[]{:S(2)}, u32[]{:S(2)}) collective-permute-start(bf16[64,1024]{1,0:T(8,128)(2,1)S(1)} %convolution_convert_fusion.9), channel_id=1, source_target_pairs={{0,2},{1,3},{2,0},{3,1},{4,5},{5,4},{6,7},{7,6},{8,9},{9,8},{10,11... | collective-permute-start | bytes 393224 | tf_op jit(solution)/shard_map/ppermute | solution.py:28
  17.1 1.4 %collective-permute-start.5 = (bf16[64,1024]{1,0:T(8,128)(2,1)S(1)}, bf16[64,1024]{1,0:T(8,128)(2,1)S(1)}, u32[]{:S(2)}, u32[]{:S(2)}) collective-permute-start(bf16[64,1024]{1,0:T(8,128)(2,1)S(1)} %convolution_convert_fusion.8), channel_id=1, source_target_pairs={{0,1},{1,0},{2,4},{3,5},{4,2},{5,3},{6,7},{7,6},{8,9},{9,8},{10,11... | collective-permute-start | bytes 393224 | tf_op jit(solution)/shard_map/ppermute | solution.py:28
  18.5 0.8 copy-start.2
  19.0 1.4 %collective-permute-start.6 = (bf16[64,1024]{1,0:T(8,128)(2,1)S(1)}, bf16[64,1024]{1,0:T(8,128)(2,1)S(1)}, u32[]{:S(2)}, u32[]{:S(2)}) collective-permute-start(bf16[64,1024]{1,0:T(8,128)(2,1)S(1)} %convolution_convert_fusion.7), channel_id=1, source_target_pairs={{0,1},{1,0},{2,3},{3,2},{4,6},{5,7},{6,4},{7,5},{8,9},{9,8},{10,11... | collective-permute-start | bytes 393224 | tf_op jit(solution)/shard_map/ppermute | solution.py:28
  19.2 13.4 %collective-permute-start.8 = (bf16[1024,512]{1,0:T(8,128)(2,1)}, bf16[1024,512]{1,0:T(8,128)(2,1)S(1)}, u32[]{:S(2)}, u32[]{:S(2)}) collective-permute-start(bf16[1024,512]{1,0:T(8,128)(2,1)} %copy-done.1), channel_id=1, source_target_pairs={{0,1},{1,0},{2,3},{3,2},{4,5},{5,4},{6,7},{7,6},{8,9},{9,8},{10,11... | collective-permute-start | bytes 3145736 | tf_op jit(solution)/shard_map/ppermute | solution.py:28
  20.9 1.5 %collective-permute-start = (bf16[64,1024]{1,0:T(8,128)(2,1)S(1)}, bf16[64,1024]{1,0:T(8,128)(2,1)}, u32[]{:S(2)}, u32[]{:S(2)}) collective-permute-start(bf16[64,1024]{1,0:T(8,128)(2,1)S(1)} %convolution_convert_fusion.3), channel_id=1, source_target_pairs={{0,1},{1,0},{2,3},{3,2},{4,5},{5,4},{6,8},{7,9},{8,6},{9,7},{10,11... | collective-permute-start | bytes 393224 | tf_op jit(solution)/shard_map/cond/branch_1_fun/ppermute | solution.py:28
  23.8 1.5 %collective-permute-start.1 = (bf16[64,1024]{1,0:T(8,128)(2,1)S(1)}, bf16[64,1024]{1,0:T(8,128)(2,1)}, u32[]{:S(2)}, u32[]{:S(2)}) collective-permute-start(bf16[64,1024]{1,0:T(8,128)(2,1)S(1)} %convolution_convert_fusion.2), channel_id=1, source_target_pairs={{0,1},{1,0},{2,3},{3,2},{4,5},{5,4},{6,7},{7,6},{8,10},{9,11},{10,... | collective-permute-start | bytes 393224 | tf_op jit(solution)/shard_map/cond/branch_1_fun/ppermute | solution.py:28
  25.3 1.8 %copy-start.3 = (bf16[64,1024]{1,0:T(8,128)(2,1)S(1)}, bf16[64,1024]{1,0:T(8,128)(2,1)}, u32[]{:S(2)}) copy-start(bf16[64,1024]{1,0:T(8,128)(2,1)} %copy-done.2) | copy-start | bytes 393220
  25.4 2.1 %copy-start = (bf16[1,1024,1024]{2,1,0:T(8,128)(2,1)S(1)}, bf16[1,1024,1024]{2,1,0:T(8,128)(2,1)}, u32[]{:S(2)}) copy-start(bf16[1,1024,1024]{2,1,0:T(8,128)(2,1)} %param.12) | copy-start | bytes 6291460
  26.9 3.8 %collective-permute-start.7 = (bf16[64,1024]{1,0:T(8,128)(2,1)S(1)}, bf16[64,1024]{1,0:T(8,128)(2,1)S(1)}, u32[]{:S(2)}, u32[]{:S(2)}) collective-permute-start(bf16[64,1024]{1,0:T(8,128)(2,1)S(1)} %convolution_convert_fusion.6), channel_id=1, source_target_pairs={{0,1},{1,0},{2,3},{3,2},{4,5},{5,4},{6,7},{7,6},{8,9},{9,8},{10,12... | collective-permute-start | bytes 393224 | tf_op jit(solution)/shard_map/ppermute | solution.py:28
  31.9 2.1 %collective-permute-start.9 = (bf16[64,1024]{1,0:T(8,128)(2,1)}, bf16[64,1024]{1,0:T(8,128)(2,1)}, u32[]{:S(2)}, u32[]{:S(2)}) collective-permute-start(bf16[64,1024]{1,0:T(8,128)(2,1)} %convolution_convert_fusion.5), channel_id=1, source_target_pairs={{0,1},{1,0},{2,3},{3,2},{4,5},{5,4},{6,7},{7,6},{8,9},{9,8},{10,11... | collective-permute-start | bytes 393224 | tf_op jit(solution)/shard_map/ppermute | solution.py:14
  35.3 1.3 %collective-permute-start.10 = (bf16[64,512]{1,0:T(8,128)(2,1)S(1)}, bf16[64,512]{1,0:T(8,128)(2,1)S(1)}, u32[]{:S(2)}, u32[]{:S(2)}) collective-permute-start(bf16[64,512]{1,0:T(8,128)(2,1)S(1)} %slice.13), channel_id=1, source_target_pairs={{0,1},{1,0},{2,3},{3,2},{4,5},{5,4},{6,7},{7,6},{8,9},{9,8},{10,11... | collective-permute-start | bytes 196616 | tf_op jit(solution)/shard_map/ppermute | solution.py:14
  37.4 1.4 %collective-permute-start.11 = (bf16[64,1024]{1,0:T(8,128)(2,1)S(1)}, bf16[64,1024]{1,0:T(8,128)(2,1)S(1)}, u32[]{:S(2)}, u32[]{:S(2)}) collective-permute-start(bf16[64,1024]{1,0:T(8,128)(2,1)S(1)} %fusion), channel_id=1, source_target_pairs={{0,1},{1,0},{2,3},{3,2},{4,5},{5,4},{6,7},{7,6},{8,9},{9,8},{10,12... | collective-permute-start | bytes 393224 | tf_op jit(solution)/shard_map/ppermute | solution.py:28
  39.5 1.4 %collective-permute-start.12 = (bf16[64,1024]{1,0:T(8,128)(2,1)S(1)}, bf16[64,1024]{1,0:T(8,128)(2,1)S(1)}, u32[]{:S(2)}, u32[]{:S(2)}) collective-permute-start(bf16[64,1024]{1,0:T(8,128)(2,1)S(1)} %fusion.1), channel_id=1, source_target_pairs={{0,1},{1,0},{2,3},{3,2},{4,5},{5,4},{6,7},{7,6},{8,10},{9,11},{10,... | collective-permute-start | bytes 393224 | tf_op jit(solution)/shard_map/ppermute | solution.py:28
  41.7 1.4 %collective-permute-start.13 = (bf16[64,1024]{1,0:T(8,128)(2,1)S(1)}, bf16[64,1024]{1,0:T(8,128)(2,1)S(1)}, u32[]{:S(2)}, u32[]{:S(2)}) collective-permute-start(bf16[64,1024]{1,0:T(8,128)(2,1)S(1)} %fusion.2), channel_id=1, source_target_pairs={{0,1},{1,0},{2,3},{3,2},{4,5},{5,4},{6,8},{7,9},{8,6},{9,7},{10,11... | collective-permute-start | bytes 393224 | tf_op jit(solution)/shard_map/ppermute | solution.py:28
  43.9 1.4 %collective-permute-start.14 = (bf16[64,1024]{1,0:T(8,128)(2,1)S(1)}, bf16[64,1024]{1,0:T(8,128)(2,1)S(1)}, u32[]{:S(2)}, u32[]{:S(2)}) collective-permute-start(bf16[64,1024]{1,0:T(8,128)(2,1)S(1)} %fusion.3), channel_id=1, source_target_pairs={{0,1},{1,0},{2,3},{3,2},{4,6},{5,7},{6,4},{7,5},{8,9},{9,8},{10,11... | collective-permute-start | bytes 393224 | tf_op jit(solution)/shard_map/ppermute | solution.py:28
  46.0 1.4 %collective-permute-start.15 = (bf16[64,1024]{1,0:T(8,128)(2,1)S(1)}, bf16[64,1024]{1,0:T(8,128)(2,1)S(1)}, u32[]{:S(2)}, u32[]{:S(2)}) collective-permute-start(bf16[64,1024]{1,0:T(8,128)(2,1)S(1)} %fusion.4), channel_id=1, source_target_pairs={{0,1},{1,0},{2,4},{3,5},{4,2},{5,3},{6,7},{7,6},{8,9},{9,8},{10,11... | collective-permute-start | bytes 393224 | tf_op jit(solution)/shard_map/ppermute | solution.py:28
  46.5 34.1 %collective-permute-start.17 = (bf16[64,1024]{1,0:T(8,128)(2,1)S(1)}, bf16[64,1024]{1,0:T(8,128)(2,1)S(1)}, u32[]{:S(2)}, u32[]{:S(2)}) collective-permute-start(bf16[64,1024]{1,0:T(8,128)(2,1)S(1)} %pad_maximum_fusion), channel_id=1, source_target_pairs={{0,1},{1,0},{2,3},{3,2},{4,5},{5,4},{6,7},{7,6},{8,9},{9,8},{10,11... | collective-permute-start | bytes 393224 | tf_op jit(solution)/shard_map/ppermute | solution.py:28
  48.2 35.3 %collective-permute-start.16 = (bf16[64,1024]{1,0:T(8,128)(2,1)S(1)}, bf16[64,1024]{1,0:T(8,128)(2,1)S(1)}, u32[]{:S(2)}, u32[]{:S(2)}) collective-permute-start(bf16[64,1024]{1,0:T(8,128)(2,1)S(1)} %fusion.5), channel_id=1, source_target_pairs={{0,2},{1,3},{2,0},{3,1},{4,5},{5,4},{6,7},{7,6},{8,9},{9,8},{10,11... | collective-permute-start | bytes 393224 | tf_op jit(solution)/shard_map/ppermute | solution.py:28
